TPU v7x, 32 devices: a whole 2x2x4 slice. The times are simulated.
32 devices in a mesh: dom: 8 (over z, y), sub: 4 (over x, core).
Axes of the slice: x: 2, y: 2, z: 4, core: 2. Of those that a mesh axis runs over, the one named last changes fastest.
Arguments:
- velocity: float32 [5, 262144], P(None, ('dom', 'sub')), may hold values from -6 to 6
- position: float32 [3, 262144], P(None, ('dom', 'sub')), may hold values from 0 to 1
- inv_mass: float32 [262144], P(('dom', 'sub')), may hold values from 0.05 to 0.3
- connectivity: int32 [4, 262144], P(None, ('dom', 'sub')), may hold values from 0 to 8447, as said below
- shape_grad: float32 [2, 4, 262144], P(None, None, ('dom', 'sub')), may hold values from -3 to 3
- area: float32 [262144], P(('dom', 'sub')), may hold values from 0.5 to 2
- thickness: float32 [262144], P(('dom', 'sub')), may hold values from 0.5 to 1.5
- yield_stress: float32 [262144], P(('dom', 'sub')), may hold values from 0.5 to 3
- stress: float32 [5, 5, 262144], P(None, None, ('dom', 'sub')), may hold values from -6 to 6
- contact_owner: int32 [262144, 1], P(('dom', 'sub')), may hold values from 0 to 31; in each aligned block of 8192 rows (0 to 8191, 8192 to 16383, ...) at most 512 rows name the same one
- face_center: float32 [3, 65536], P(None, ('dom', 'sub')), may hold values from 0 to 1
- face_angle: float32 [2, 65536], P(None, ('dom', 'sub')), may hold values from -3.140625 to 3.140625
- face_stiffness: float32 [65536], P(('dom', 'sub')), may hold values from 1 to 10
- ghost_list: int32 [16384], P(('dom', 'sub')), may hold values from 0 to 2047
- pair_node: int32 [4096], P(('dom', 'sub')), may hold values from 0 to 127
- pair_face: int32 [4096], P(('dom', 'sub')), may hold values from 0 to 19
- pair_count: int32 [32], P(('dom', 'sub')), may hold values from 16 to 128, as said below
Outputs:
- new_velocity: float32 [5, 262144], P(None, ('dom', 'sub'))
- new_stress: float32 [5, 5, 262144], P(None, None, ('dom', 'sub'))
Inputs may be any that keep to these rules, and one draw needn't show every extreme that they name: `connectivity`: the corners of the element at local index e of a device lie in e .. e + 256; on the first device at least 128, on the last below 8320. `contact_owner`: the 8192 nodes of one device name any one contact device at most 512 times; some device reaches 512. `pair_count`: some device's count is 128 in every draw.
All inputs are finite; a program needn't handle non-finite values.
Results may differ from a plain program's by a relative error of at most 0.0003.
Values sent between devices are 32-bit elements; how exact they have to be, the bound alone decides.
No kernel may reach another device: no remote copies, remote signals or barrier semaphores. Data moves between devices by JAX's collectives and lax.ppermute only.
A program may use at most 128 MiB of HBM per device.

v0:
```python
import math

import jax
import jax.numpy as jnp
from jax import lax
from jax.sharding import PartitionSpec as P

TILE = 128
HALO = 128
GHOST = 256


LOBATTO_POINTS = (-1.0, -0.6546536707079771, 0.0, 0.6546536707079771, 1.0)
LOBATTO_WEIGHTS = (0.1, 49.0 / 90.0, 32.0 / 45.0, 49.0 / 90.0, 0.1)
PLANE_MODULUS = 1.0 / 0.91
POISSON = 0.3
SHEAR_MODULUS = 5.0 / 6.0 / 2.6
DAMPING = 0.3
REACH_SQ = 0.5


def padded_2(x, sides, width):
    for axis, dim in sides:
        count, length = (lax.axis_size(axis), x.shape[dim])
        up = [(i, (i + 1) % count) for i in range(count - 1)]
        down = [(j, i) for i, j in up]
        last = lax.slice_in_dim(x, length - width, length, axis=dim)
        first = lax.slice_in_dim(x, 0, width, axis=dim)
        before = lax.ppermute(last, axis, up)
        after = lax.ppermute(first, axis, down)
        x = jnp.concatenate([before, x, after], axis=dim)
    return x


def element_forces(corner, grads, area, thickness, yield_stress, old_stress):
    vel_x, vel_y, vel_z, rot_x, rot_y = (corner[0], corner[1], corner[2], corner[3], corner[4])
    grad_x, grad_y = (grads[0], grads[1])
    memb_xx = jnp.sum(grad_x * vel_x, axis=0)
    bend_xx = jnp.sum(grad_x * rot_y, axis=0)
    memb_yy = jnp.sum(grad_y * vel_y, axis=0)
    bend_yy = -jnp.sum(grad_y * rot_x, axis=0)
    memb_xy = jnp.sum(grad_y * vel_x + grad_x * vel_y, axis=0)
    bend_xy = jnp.sum(grad_y * rot_y - grad_x * rot_x, axis=0)
    shear_xz = jnp.sum(grad_x * vel_z, axis=0) + 0.25 * jnp.sum(rot_y, axis=0)
    shear_yz = jnp.sum(grad_y * vel_z, axis=0) - 0.25 * jnp.sum(rot_x, axis=0)
    layers = []
    membrane = []
    moments = []
    for layer in range(5):
        height = 0.5 * thickness * LOBATTO_POINTS[layer]
        strain_xx = memb_xx + height * bend_xx
        strain_yy = memb_yy + height * bend_yy
        strain_xy = memb_xy + height * bend_xy
        trial_xx = old_stress[layer, 0] + PLANE_MODULUS * (strain_xx + POISSON * strain_yy)
        trial_yy = old_stress[layer, 1] + PLANE_MODULUS * (strain_yy + POISSON * strain_xx)
        trial_xy = old_stress[layer, 2] + PLANE_MODULUS * 0.5 * (1.0 - POISSON) * strain_xy
        trial_xz = old_stress[layer, 3] + SHEAR_MODULUS * shear_xz
        trial_yz = old_stress[layer, 4] + SHEAR_MODULUS * shear_yz
        mises = jnp.sqrt(
            0.25 * (trial_xx + trial_yy) ** 2
            + 0.75 * (trial_xx - trial_yy) ** 2
            + 3.0 * (trial_xy**2 + trial_xz**2 + trial_yz**2)
        )
        factor = yield_stress / jnp.maximum(mises, yield_stress)
        updated = jnp.stack([trial_xx, trial_yy, trial_xy, trial_xz, trial_yz]) * factor
        layers.append(updated)
        weight = LOBATTO_WEIGHTS[layer] * 0.5 * thickness * area
        membrane.append(weight * updated)
        moments.append(weight * height * updated[0:3])
    new_stress = jnp.stack(layers)
    force_sum = sum(membrane)
    moment_sum = sum(moments)
    force_x = grad_x * force_sum[0] + grad_y * force_sum[2]
    force_y = grad_y * force_sum[1] + grad_x * force_sum[2]
    force_z = grad_x * force_sum[3] + grad_y * force_sum[4]
    moment_x = -(grad_y * moment_sum[1] + grad_x * moment_sum[2]) - 0.25 * force_sum[4]
    moment_y = grad_x * moment_sum[0] + grad_y * moment_sum[2] + 0.25 * force_sum[3]
    return (jnp.stack([force_x, force_y, force_z, moment_x, moment_y]), new_stress)


def ranks_and_counts(target, number):
    total_rows = target.shape[0]
    rows = min(512, total_rows)
    blocks = total_rows // rows
    owners = jnp.arange(number, dtype=jnp.int32)
    onehot = (target.reshape(blocks, rows)[:, :, None] == owners[None, None, :]).astype(
        jnp.bfloat16
    )
    earlier = (jnp.arange(rows)[:, None] > jnp.arange(rows)[None, :]).astype(jnp.bfloat16)
    within = jnp.einsum("ij,bjd->bid", earlier, onehot, preferred_element_type=jnp.float32)
    totals = jnp.sum(onehot.astype(jnp.float32), axis=1)
    offsets = jnp.cumsum(totals, axis=0) - totals
    rank = jnp.sum((within + offsets[:, None, :]) * onehot.astype(jnp.float32), axis=2)
    counts = jnp.sum(totals, axis=0)
    return (rank.reshape(total_rows).astype(jnp.int32), counts.astype(jnp.int32))


def face_normals(face_angle):
    azimuth, elevation = (face_angle[0], face_angle[1])
    return jnp.stack(
        [
            jnp.cos(azimuth) * jnp.cos(elevation),
            jnp.sin(azimuth) * jnp.cos(elevation),
            jnp.sin(elevation),
        ]
    )


def pair_forces(node_block, face_block, live):
    offset = node_block[0:3, :, :, None] - face_block[0:3, :, None, :]
    normal = face_block[3:6, :, None, :]
    depth = jnp.maximum(-jnp.sum(normal * offset, axis=0), 0.0)
    reach = jnp.exp(-jnp.sum(offset * offset, axis=0) / REACH_SQ)
    along = jnp.sum(normal * node_block[3:6, :, :, None], axis=0)
    magnitude = face_block[6][:, None, :] * reach * depth * (1.0 - DAMPING * along)
    magnitude = magnitude * node_block[6][:, :, None] * live[:, None, None]
    return jnp.einsum("bij,cbj->cbi", magnitude, face_block[3:6], precision=lax.Precision.HIGHEST)


def body(
    velocity,
    position,
    inv_mass,
    connectivity,
    shape_grad,
    area,
    thickness,
    yield_stress,
    stress,
    contact_owner,
    face_center,
    face_angle,
    face_stiffness,
    ghost_list,
    pair_node,
    pair_face,
    pair_count,
):
    dom_count = lax.axis_size("dom")
    sub_count = lax.axis_size("sub")
    devices = dom_count * sub_count
    node_dev = velocity.shape[1]
    capacity = 2 * node_dev // devices
    padded = padded_2(velocity, ((("dom", "sub"), 1),), HALO)
    extent = padded.shape[1]
    rows = min(256, node_dev)
    blocks = node_dev // rows
    span = rows + 2 * HALO
    reach = 1 + (2 * HALO + rows - 1) // rows
    limit = max(1, 2**20 // (rows * span))
    group = math.gcd(blocks, 1 << limit.bit_length() - 1)
    turns = blocks // group
    extended = jnp.pad(padded, ((0, 0), (0, (blocks + reach) * rows - extent)))
    pieces = extended.reshape(5, blocks + reach, rows)
    windows = jnp.concatenate([pieces[:, shift : shift + blocks] for shift in range(reach)], axis=2)
    starts = (jnp.arange(blocks, dtype=jnp.int32) * rows)[None, :, None]
    local = connectivity.reshape(4, blocks, rows) - starts
    local_grouped = local.transpose(1, 0, 2).reshape(turns, group, 4, rows)
    window_grouped = windows.transpose(1, 0, 2).reshape(turns, group, 5, span)
    positions = jnp.arange(span, dtype=jnp.int32)

    def pick_corners(inputs):
        where, window = inputs
        selector = (where[..., None] == positions).astype(jnp.float32)
        return jnp.einsum("gaew,gcw->gcae", selector, window, precision=lax.Precision.HIGHEST)

    corners = lax.map(pick_corners, (local_grouped, window_grouped))
    corners = corners.transpose(2, 3, 0, 1, 4).reshape(5, 4, node_dev)
    forces, new_stress = element_forces(corners, shape_grad, area, thickness, yield_stress, stress)
    forces_grouped = forces.reshape(5, 4, turns, group, rows).transpose(2, 3, 0, 1, 4)

    def spread_forces(inputs):
        where, part = inputs
        selector = (where[..., None] == positions).astype(jnp.float32)
        return jnp.einsum("gaew,gcae->gcw", selector, part, precision=lax.Precision.HIGHEST)

    shares = lax.map(spread_forces, (local_grouped, forces_grouped))
    shares = shares.reshape(blocks, 5, span).transpose(1, 0, 2)
    shares = shares.reshape(5, blocks, reach, rows)
    gathered = jnp.zeros((5, blocks + reach, rows), jnp.float32)
    for shift in range(reach):
        gathered = gathered + jnp.pad(shares[:, :, shift], ((0, 0), (shift, reach - shift), (0, 0)))
    summed = gathered.reshape(5, (blocks + reach) * rows)[:, :extent]
    rims = jnp.concatenate([summed[:, :HALO], summed[:, HALO + node_dev :]], axis=1)
    arrived = padded_2(rims, ((("dom", "sub"), 1),), HALO)
    internal = summed[:, HALO : HALO + node_dev]
    internal = internal.at[:, :HALO].add(arrived[:, :HALO])
    internal = internal.at[:, node_dev - HALO :].add(arrived[:, 3 * HALO :])
    target = contact_owner[:, 0]
    ranks, sent_counts = ranks_and_counts(target, devices)
    slots = target * capacity + ranks
    payload = jnp.concatenate(
        [position, velocity[0:3], jnp.ones((1, node_dev), jnp.float32)], axis=0
    )
    outgoing = jnp.zeros((7, devices * capacity), jnp.float32).at[:, slots].set(payload)
    incoming = lax.all_to_all(outgoing, ("dom", "sub"), split_axis=1, concat_axis=1, tiled=True)
    face_data = jnp.concatenate(
        [face_center, face_normals(face_angle), face_stiffness[None, :]], axis=0
    )
    leaving = face_data[:, ghost_list]
    borrowed = padded_2(leaving, ((("dom", "sub"), 1),), GHOST)
    all_faces = jnp.concatenate([borrowed[:, :GHOST], face_data, borrowed[:, 3 * GHOST :]], axis=1)
    node_tiles = incoming.reshape(7, -1, TILE)
    face_tiles = all_faces.reshape(7, -1, TILE)
    tile_count = node_tiles.shape[1]
    pair_total = pair_node.shape[0]
    block = math.gcd(32, pair_total)
    tile_ids = jnp.arange(tile_count, dtype=jnp.int32)

    def one_block(step, accum):
        start = step * block
        node_ids = lax.dynamic_slice_in_dim(pair_node, start, block)
        face_ids = lax.dynamic_slice_in_dim(pair_face, start, block)
        live = (start + jnp.arange(block, dtype=jnp.int32) < pair_count[0]).astype(jnp.float32)
        result = pair_forces(
            jnp.take(node_tiles, node_ids, axis=1), jnp.take(face_tiles, face_ids, axis=1), live
        )
        onehot = (node_ids[:, None] == tile_ids[None, :]).astype(jnp.float32)
        return accum + jnp.einsum("cbi,bt->cti", result, onehot, precision=lax.Precision.HIGHEST)

    accum = lax.fori_loop(
        0, pair_total // block, one_block, jnp.zeros((3, tile_count, TILE), jnp.float32)
    )
    returned = accum.reshape(3, devices * capacity)
    back = lax.all_to_all(returned, ("dom", "sub"), split_axis=1, concat_axis=1, tiled=True)
    contact = back[:, slots]
    total = (-internal).at[0:3].add(contact)
    new_velocity = velocity + inv_mass[None, :] * total
    return (new_velocity, new_stress)


def solution(mesh):
    in_specs = (
        P(None, ("dom", "sub")),
        P(None, ("dom", "sub")),
        P(("dom", "sub")),
        P(None, ("dom", "sub")),
        P(None, None, ("dom", "sub")),
        P(("dom", "sub")),
        P(("dom", "sub")),
        P(("dom", "sub")),
        P(None, None, ("dom", "sub")),
        P(("dom", "sub"), None),
        P(None, ("dom", "sub")),
        P(None, ("dom", "sub")),
        P(("dom", "sub")),
        P(("dom", "sub")),
        P(("dom", "sub")),
        P(("dom", "sub")),
        P(("dom", "sub")),
    )
    out_specs = (P(None, ("dom", "sub")), P(None, None, ("dom", "sub")))
    return jax.shard_map(body, mesh=mesh, in_specs=in_specs, out_specs=out_specs, check_vma=False)
```

profile of v0, /device:TPU:0, one launch (start us, length us, event | category | flops | bytes accessed | tf_op | source)
XLA Modules:
  0.0 310.1 jit_solution(9605289136040208521)
XLA Ops:
  10.0 5.8 %collective-permute-start.4 = (f32[7,256]{0,1:T(8,128)}, f32[7,256]{0,1:T(8,128)}, u32[]{:S(2)}, u32[]{:S(2)}) collective-permute-start(f32[7,256]{0,1:T(8,128)} %get-tuple-element.530), channel_id=1, source_target_pairs={{0,1},{1,2},{2,3},{3,4},{4,5},{5,6},{6,7},{7,8},{8,9},{9,10},{10,1... | collective-permute-start | bytes 21512 | tf_op jit(solution)/shard_map/ppermute | solution.py:29
  22.9 24.6 %scatter_custom_fusion = f32[7,16384]{0,1:T(8,128)} fusion(s32[8192]{0:T(1024)S(1)} %bitcast.375, f32[8192,7]{1,0:T(8,128)} %copy.189, f32[]{:T(128)} %constant.237.clone.1), kind=kCustom, calls=%fused_computation.73 | custom fusion | bytes 459264 | tf_op jit(solution)/shard_map/scatter | solution.py:195
  47.5 6.1 %copy.190 = f32[7,32,512]{2,0,1:T(8,128)} copy(f32[7,32,512]{0,2,1:T(8,128)} %bitcast.288) | data formatting | bytes 917504 | tf_op jit(solution)/shard_map/all_to_all | solution.py:196
  53.6 9.6 %all-to-all-start = ((f32[7,32,512]{2,0,1:T(8,128)}), f32[7,32,512]{2,0,1:T(8,128)S(1)}, u32[]{:S(2)}, u32[]{:S(2)}) async-start(f32[7,32,512]{2,0,1:T(8,128)} %copy.190), calls=%async_computation | async-start | bytes 1048576 | tf_op jit(solution)/shard_map/all_to_all | solution.py:196
  68.2 37.3 %while.39 = (s32[]{:T(128)}, f32[4,8,5,4,256]{4,2,3,1,0:T(8,128)}, f32[4,8,5,512]{3,2,1,0:T(8,128)S(1)}, s32[4,8,4,256]{3,2,1,0:T(4,128)S(1)}, s32[]{:T(128)}) while((s32[]{:T(128)}, f32[4,8,5,4,256]{4,2,3,1,0:T(8,128)}, f32[4,8,5,512]{3,2,1,0:T(8,128)S(1)}, s32[4,8,4,256]{3,2,1,0:T(4,128)S(1)}, s32[]{:T(128)}) %tuple.250), condition=%wide.region_1.2_spmd.clone, body=%wide.region_0.1_spmd.clone.sunk | while | flops 255852544 | bytes 492609 | solution.py:167
  68.3 9.3 %fusion.102 = f32[4,8,5,4,256]{4,2,3,1,0:T(8,128)} fusion(f32[4,8,5,4,256]{4,2,3,1,0:T(8,128)} %get-tuple-element.688, s32[]{:T(128)} %get-tuple-element.687, s32[8,4,256]{2,1,0:T(4,128)S(1)} %dynamic-slice_bitcast_fusion.4, f32[4,8,5,512]{3,2,1,0:T(8,128)S(1)} %get-tuple-element.694), kind=kOutput, calls=%fused_computation.12.clone.1 | convolution fusion | flops 255852544 | bytes 427008 | tf_op jit(solution)/shard_map/while/body/eval_jaxpr/gaew,gcw->gcae/dot_general | solution.py:165
  77.6 9.3 %fusion.102 = f32[4,8,5,4,256]{4,2,3,1,0:T(8,128)} fusion(f32[4,8,5,4,256]{4,2,3,1,0:T(8,128)} %get-tuple-element.688, s32[]{:T(128)} %get-tuple-element.687, s32[8,4,256]{2,1,0:T(4,128)S(1)} %dynamic-slice_bitcast_fusion.4, f32[4,8,5,512]{3,2,1,0:T(8,128)S(1)} %get-tuple-element.694), kind=kOutput, calls=%fused_computation.12.clone.1 | convolution fusion | flops 255852544 | bytes 427008 | tf_op jit(solution)/shard_map/while/body/eval_jaxpr/gaew,gcw->gcae/dot_general | solution.py:165
  86.9 9.3 %fusion.102 = f32[4,8,5,4,256]{4,2,3,1,0:T(8,128)} fusion(f32[4,8,5,4,256]{4,2,3,1,0:T(8,128)} %get-tuple-element.688, s32[]{:T(128)} %get-tuple-element.687, s32[8,4,256]{2,1,0:T(4,128)S(1)} %dynamic-slice_bitcast_fusion.4, f32[4,8,5,512]{3,2,1,0:T(8,128)S(1)} %get-tuple-element.694), kind=kOutput, calls=%fused_computation.12.clone.1 | convolution fusion | flops 255852544 | bytes 427008 | tf_op jit(solution)/shard_map/while/body/eval_jaxpr/gaew,gcw->gcae/dot_general | solution.py:165
  96.3 9.3 %fusion.102 = f32[4,8,5,4,256]{4,2,3,1,0:T(8,128)} fusion(f32[4,8,5,4,256]{4,2,3,1,0:T(8,128)} %get-tuple-element.688, s32[]{:T(128)} %get-tuple-element.687, s32[8,4,256]{2,1,0:T(4,128)S(1)} %dynamic-slice_bitcast_fusion.4, f32[4,8,5,512]{3,2,1,0:T(8,128)S(1)} %get-tuple-element.694), kind=kOutput, calls=%fused_computation.12.clone.1 | convolution fusion | flops 255852544 | bytes 427008 | tf_op jit(solution)/shard_map/while/body/eval_jaxpr/gaew,gcw->gcae/dot_general | solution.py:165
  105.6 4.1 %slice_reduce_fusion = (f32[4,8,256]{2,1,0:T(8,128)S(1)}, f32[4,8,256]{2,1,0:T(8,128)S(1)}, f32[1,4,4,8,256]{4,0,1,3,2:T(1,128)S(1)}, f32[1,4,4,8,256]{4,0,1,3,2...) fusion(f32[5,4,4,8,256]{4,0,1,3,2:T(8,128)} %bitcast.310), kind=kLoop, calls=%fused_computation.232 | loop fusion | flops 49152 | bytes 1376256 | tf_op jit(solution)/shard_map/reduce_sum | solution.py:45
  130.6 26.4 %while.40 = (s32[]{:T(128)}, f32[4,8,5,512]{3,2,1,0:T(8,128)S(1)}, f32[4,8,5,4,256]{4,1,0,3,2:T(8,128)S(1)}, s32[4,8,4,256]{3,2,1,0:T(4,128)S(1)}, s32[]{:T(128)}) while((s32[]{:T(128)}, f32[4,8,5,512]{3,2,1,0:T(8,128)S(1)}, f32[4,8,5,4,256]{4,1,0,3,2:T(8,128)S(1)}, s32[4,8,4,256]{3,2,1,0:T(4,128)S(1)}, s32[]{:T(128)}) %tuple.251), condition=%wide.region_13.14_spmd.clone, body=%wide.region_12.13_spmd.clone.sunk | while | flops 255852544 | bytes 720969 | solution.py:177
  130.7 6.6 %fusion.103 = f32[4,8,5,512]{3,2,1,0:T(8,128)S(1)} fusion(f32[4,8,5,512]{3,2,1,0:T(8,128)S(1)} %get-tuple-element.703, s32[]{:T(128)} %get-tuple-element.702, s32[8,4,256]{2,1,0:T(4,128)S(1)} %dynamic-slice_bitcast_fusion.5, f32[1,8,5,4,256]{4,1,0,3,2:T(8,128)S(1)} %constant_dynamic-slice_fusion.2), kind=kOutput, calls=%fused_computation.21.clone.1 | convolution fusion | flops 255852544 | bytes 327684 | tf_op jit(solution)/shard_map/while/body/eval_jaxpr/gaew,gcae->gcw/dot_general | solution.py:175
  137.3 6.6 %fusion.103 = f32[4,8,5,512]{3,2,1,0:T(8,128)S(1)} fusion(f32[4,8,5,512]{3,2,1,0:T(8,128)S(1)} %get-tuple-element.703, s32[]{:T(128)} %get-tuple-element.702, s32[8,4,256]{2,1,0:T(4,128)S(1)} %dynamic-slice_bitcast_fusion.5, f32[1,8,5,4,256]{4,1,0,3,2:T(8,128)S(1)} %constant_dynamic-slice_fusion.2), kind=kOutput, calls=%fused_computation.21.clone.1 | convolution fusion | flops 255852544 | bytes 327684 | tf_op jit(solution)/shard_map/while/body/eval_jaxpr/gaew,gcae->gcw/dot_general | solution.py:175
  143.9 6.6 %fusion.103 = f32[4,8,5,512]{3,2,1,0:T(8,128)S(1)} fusion(f32[4,8,5,512]{3,2,1,0:T(8,128)S(1)} %get-tuple-element.703, s32[]{:T(128)} %get-tuple-element.702, s32[8,4,256]{2,1,0:T(4,128)S(1)} %dynamic-slice_bitcast_fusion.5, f32[1,8,5,4,256]{4,1,0,3,2:T(8,128)S(1)} %constant_dynamic-slice_fusion.2), kind=kOutput, calls=%fused_computation.21.clone.1 | convolution fusion | flops 255852544 | bytes 327684 | tf_op jit(solution)/shard_map/while/body/eval_jaxpr/gaew,gcae->gcw/dot_general | solution.py:175
  150.5 6.6 %fusion.103 = f32[4,8,5,512]{3,2,1,0:T(8,128)S(1)} fusion(f32[4,8,5,512]{3,2,1,0:T(8,128)S(1)} %get-tuple-element.703, s32[]{:T(128)} %get-tuple-element.702, s32[8,4,256]{2,1,0:T(4,128)S(1)} %dynamic-slice_bitcast_fusion.5, f32[1,8,5,4,256]{4,1,0,3,2:T(8,128)S(1)} %constant_dynamic-slice_fusion.2), kind=kOutput, calls=%fused_computation.21.clone.1 | convolution fusion | flops 255852544 | bytes 327684 | tf_op jit(solution)/shard_map/while/body/eval_jaxpr/gaew,gcae->gcw/dot_general | solution.py:175
  169.2 4.4 %slice.395 = f32[5,8192]{0,1:T(8,128)} slice(f32[5,8704]{0,1:T(8,128)} %bitcast.290), slice={[0:5], [128:8320]} | slice | bytes 327680 | tf_op jit(solution)/shard_map/slice | solution.py:186
  175.7 43.9 %while.41 = (s32[]{:T(128)}, f32[3,128,128]{2,1,0:T(8,128)S(1)}, s32[128]{0:T(128)S(1)}, s32[128]{0:T(128)S(1)}, f32[7,20,128]{2,0,1:T(8,128)S(1)}, /*index=5*/f...) while((s32[]{:T(128)}, f32[3,128,128]{2,1,0:T(8,128)S(1)}, ...), condition=%wide.region_23.24_spmd.clone, body=%wide.region_19.23_spmd.clone.sunk | while | flops 53115464 | bytes 15149361 | solution.py:221
  177.3 4.3 %fusion.110 = (f32[32,128,128]{2,1,0:T(8,128)S(1)}, f32[32,128,128]{2,1,0:T(8,128)S(1)}, f32[32,128,128]{2,1,0:T(8,128)S(1)}) fusion(f32[3,32,128]{2,1,0:T(8,128)S(1)} %copy.235, f32[3,32,128]{2,1,0:T(8,128)S(1)} %copy.236, f32[3,32,128]{2,1,0:T(8,128)S(1)} %copy.237, f32[3,32,128]{2,1,0:T(8,128)S(1)} %copy.238), kind=kLoop, calls=%fused_computation.27.clone.1 | loop fusion | flops 9437184 | bytes 6488064 | tf_op jit(solution)/shard_map/while/body/eval_jaxpr/reduce_sum | solution.py:113
  182.4 3.9 %fusion.111 = f32[3,32,128]{2,0,1:T(4,128)S(1)} fusion(f32[32,128,128]{2,1,0:T(8,128)S(1)} %get-tuple-element.679, f32[32,128,128]{2,1,0:T(8,128)S(1)} %get-tuple-element.680, f32[32,128,128]{2,1,0:T(8,128)S(1)} %get-tuple-element.681, f32[32]{0:T(128)S(1)} %compare_convert_fusion.2, f32[32,128]{1,0:T(8,128)S(1)} %bitcast.311, ...), kind=kOutput, calls=%fused_computation.45.clone.1 | convolution fusion | flops 24641536 | bytes 6439424 | tf_op jit(solution)/shard_map/while/body/eval_jaxpr/bij,cbj->cbi/dot_general | solution.py:117
  188.3 4.3 %fusion.110 = (f32[32,128,128]{2,1,0:T(8,128)S(1)}, f32[32,128,128]{2,1,0:T(8,128)S(1)}, f32[32,128,128]{2,1,0:T(8,128)S(1)}) fusion(f32[3,32,128]{2,1,0:T(8,128)S(1)} %copy.235, f32[3,32,128]{2,1,0:T(8,128)S(1)} %copy.236, f32[3,32,128]{2,1,0:T(8,128)S(1)} %copy.237, f32[3,32,128]{2,1,0:T(8,128)S(1)} %copy.238), kind=kLoop, calls=%fused_computation.27.clone.1 | loop fusion | flops 9437184 | bytes 6488064 | tf_op jit(solution)/shard_map/while/body/eval_jaxpr/reduce_sum | solution.py:113
  193.3 3.9 %fusion.111 = f32[3,32,128]{2,0,1:T(4,128)S(1)} fusion(f32[32,128,128]{2,1,0:T(8,128)S(1)} %get-tuple-element.679, f32[32,128,128]{2,1,0:T(8,128)S(1)} %get-tuple-element.680, f32[32,128,128]{2,1,0:T(8,128)S(1)} %get-tuple-element.681, f32[32]{0:T(128)S(1)} %compare_convert_fusion.2, f32[32,128]{1,0:T(8,128)S(1)} %bitcast.311, ...), kind=kOutput, calls=%fused_computation.45.clone.1 | convolution fusion | flops 24641536 | bytes 6439424 | tf_op jit(solution)/shard_map/while/body/eval_jaxpr/bij,cbj->cbi/dot_general | solution.py:117
  199.3 4.3 %fusion.110 = (f32[32,128,128]{2,1,0:T(8,128)S(1)}, f32[32,128,128]{2,1,0:T(8,128)S(1)}, f32[32,128,128]{2,1,0:T(8,128)S(1)}) fusion(f32[3,32,128]{2,1,0:T(8,128)S(1)} %copy.235, f32[3,32,128]{2,1,0:T(8,128)S(1)} %copy.236, f32[3,32,128]{2,1,0:T(8,128)S(1)} %copy.237, f32[3,32,128]{2,1,0:T(8,128)S(1)} %copy.238), kind=kLoop, calls=%fused_computation.27.clone.1 | loop fusion | flops 9437184 | bytes 6488064 | tf_op jit(solution)/shard_map/while/body/eval_jaxpr/reduce_sum | solution.py:113
  204.3 3.9 %fusion.111 = f32[3,32,128]{2,0,1:T(4,128)S(1)} fusion(f32[32,128,128]{2,1,0:T(8,128)S(1)} %get-tuple-element.679, f32[32,128,128]{2,1,0:T(8,128)S(1)} %get-tuple-element.680, f32[32,128,128]{2,1,0:T(8,128)S(1)} %get-tuple-element.681, f32[32]{0:T(128)S(1)} %compare_convert_fusion.2, f32[32,128]{1,0:T(8,128)S(1)} %bitcast.311, ...), kind=kOutput, calls=%fused_computation.45.clone.1 | convolution fusion | flops 24641536 | bytes 6439424 | tf_op jit(solution)/shard_map/while/body/eval_jaxpr/bij,cbj->cbi/dot_general | solution.py:117
  210.3 4.3 %fusion.110 = (f32[32,128,128]{2,1,0:T(8,128)S(1)}, f32[32,128,128]{2,1,0:T(8,128)S(1)}, f32[32,128,128]{2,1,0:T(8,128)S(1)}) fusion(f32[3,32,128]{2,1,0:T(8,128)S(1)} %copy.235, f32[3,32,128]{2,1,0:T(8,128)S(1)} %copy.236, f32[3,32,128]{2,1,0:T(8,128)S(1)} %copy.237, f32[3,32,128]{2,1,0:T(8,128)S(1)} %copy.238), kind=kLoop, calls=%fused_computation.27.clone.1 | loop fusion | flops 9437184 | bytes 6488064 | tf_op jit(solution)/shard_map/while/body/eval_jaxpr/reduce_sum | solution.py:113
  215.3 3.9 %fusion.111 = f32[3,32,128]{2,0,1:T(4,128)S(1)} fusion(f32[32,128,128]{2,1,0:T(8,128)S(1)} %get-tuple-element.679, f32[32,128,128]{2,1,0:T(8,128)S(1)} %get-tuple-element.680, f32[32,128,128]{2,1,0:T(8,128)S(1)} %get-tuple-element.681, f32[32]{0:T(128)S(1)} %compare_convert_fusion.2, f32[32,128]{1,0:T(8,128)S(1)} %bitcast.311, ...), kind=kOutput, calls=%fused_computation.45.clone.1 | convolution fusion | flops 24641536 | bytes 6439424 | tf_op jit(solution)/shard_map/while/body/eval_jaxpr/bij,cbj->cbi/dot_general | solution.py:117
  220.5 7.9 %all-to-all-start.1 = ((f32[3,32,512]{2,0,1:T(4,128)}), f32[3,32,512]{2,0,1:T(4,128)S(1)}, u32[]{:S(2)}, u32[]{:S(2)}) async-start(f32[3,32,512]{2,0,1:T(4,128)} %copy.193), calls=%async_computation.1 | async-start | bytes 524288 | tf_op jit(solution)/shard_map/all_to_all | solution.py:225
  232.0 4.4 %neg.26 = f32[5,8192]{0,1:T(8,128)} negate(f32[5,8192]{0,1:T(8,128)} %fusion.77) | non-fusion elementwise | flops 40960 | bytes 327680 | tf_op jit(solution)/shard_map/neg | solution.py:227
  239.0 4.9 %copy.194 = f32[3,32,512]{0,2,1:T(8,128)} copy(f32[3,32,512]{2,0,1:T(4,128)S(1)} %all-to-all-done.1) | data formatting | bytes 393216 | tf_op jit(solution)/shard_map/all_to_all | solution.py:225
  243.9 31.3 %gather_fusion.3 = f32[8192,3]{1,0:T(8,128)} fusion(f32[3,16384]{0,1:T(8,128)} %bitcast.292, s32[8192]{0:T(1024)S(1)} %copy-done.29), kind=kCustom, calls=%fused_computation.3 | custom fusion | bytes 229376 | tf_op jit(solution)/shard_map/gather | solution.py:226
  275.2 5.8 %slice_add_fusion = f32[3,8192]{0,1:T(8,128)} fusion(f32[5,8192]{0,1:T(8,128)} %neg.26, f32[8192,3]{1,0:T(8,128)} %gather_fusion.3), kind=kLoop, calls=%fused_computation.71 | loop fusion | flops 24576 | bytes 294912 | tf_op jit(solution)/shard_map/add | solution.py:227
  281.0 20.1 %scatter-add.14 = f32[5,8192]{0,1:T(8,128)} dynamic-update-slice(f32[5,8192]{0,1:T(8,128)} %neg.26, f32[3,8192]{0,1:T(8,128)} %slice_add_fusion, s32[]{:T(128)} %constant.236.clone.1, s32[]{:T(128)} %constant.236.clone.1) | dynamic-update-slice | bytes 196612 | tf_op jit(solution)/shard_map/scatter-add | solution.py:227
  301.1 5.4 %multiply_add_fusion = f32[5,8192]{0,1:T(8,128)} fusion(f32[5,8192]{0,1:T(8,128)} %copy.195, f32[5,8192]{0,1:T(8,128)} %scatter-add.14, f32[8192]{0:T(1024)S(1)} %copy-done.46), kind=kLoop, calls=%fused_computation.72 | loop fusion | flops 81920 | bytes 524288 | tf_op jit(solution)/shard_map/add | solution.py:228
  (301 shorter events, 76.8 us)
Async XLA Ops:
  0.6 19.5 %slice-start = ((f32[5,8192]{1,0:T(8,128)}), f32[3,8192]{1,0:T(4,128)S(1)}, s32[]{:S(2)}) async-start(f32[5,8192]{1,0:T(8,128)} %param.29), calls=%async_computation.2 | async-start | bytes 262144 | tf_op jit(solution)/shard_map/slice | solution.py:193
  0.6 19.3 %copy-start.28 = (s32[8192,1]{0,1:T(1,128)S(1)}, s32[8192,1]{0,1:T(1,128)}, u32[]{:S(2)}) copy-start(s32[8192,1]{0,1:T(1,128)} %param.38) | copy-start | bytes 98308
  0.7 19.5 %copy-start.27 = (f32[3,8192]{1,0:T(4,128)S(1)}, f32[3,8192]{1,0:T(4,128)}, u32[]{:S(2)}) copy-start(f32[3,8192]{1,0:T(4,128)} %param.30) | copy-start | bytes 294916
  1.4 66.7 %collective-permute-start = (f32[5,128]{1,0:T(8,128)S(1)}, f32[5,128]{1,0:T(8,128)S(1)}, u32[]{:S(2)}, u32[]{:S(2)}) collective-permute-start(f32[5,128]{1,0:T(8,128)S(1)} %get-tuple-element.541), channel_id=1, source_target_pairs={{0,1},{1,2},{2,3},{3,4},{4,5},{5,6},{6,7},{7,8},{8,9},{9,10},{10,1... | collective-permute-start | bytes 7688 | tf_op jit(solution)/shard_map/ppermute | solution.py:29
  3.8 64.3 %collective-permute-start.1 = (f32[5,128]{1,0:T(8,128)S(1)}, f32[5,128]{1,0:T(8,128)S(1)}, u32[]{:S(2)}, u32[]{:S(2)}) collective-permute-start(f32[5,128]{1,0:T(8,128)S(1)} %get-tuple-element.542), channel_id=1, source_target_pairs={{1,0},{2,1},{3,2},{4,3},{5,4},{6,5},{7,6},{8,7},{9,8},{10,9},{11,1... | collective-permute-start | bytes 7688 | tf_op jit(solution)/shard_map/ppermute | solution.py:30
  10.0 163.6 %collective-permute-start.4 = (f32[7,256]{0,1:T(8,128)}, f32[7,256]{0,1:T(8,128)}, u32[]{:S(2)}, u32[]{:S(2)}) collective-permute-start(f32[7,256]{0,1:T(8,128)} %get-tuple-element.530), channel_id=1, source_target_pairs={{0,1},{1,2},{2,3},{3,4},{4,5},{5,6},{6,7},{7,8},{8,9},{9,10},{10,1... | collective-permute-start | bytes 21512 | tf_op jit(solution)/shard_map/ppermute | solution.py:29
  15.8 158.8 %collective-permute-start.5 = (f32[7,256]{0,1:T(8,128)}, f32[7,256]{0,1:T(8,128)}, u32[]{:S(2)}, u32[]{:S(2)}) collective-permute-start(f32[7,256]{0,1:T(8,128)} %get-tuple-element.531), channel_id=1, source_target_pairs={{1,0},{2,1},{3,2},{4,3},{5,4},{6,5},{7,6},{8,7},{9,8},{10,9},{11,1... | collective-permute-start | bytes 21512 | tf_op jit(solution)/shard_map/ppermute | solution.py:30
  47.5 15.7 %copy-start.2 = (f32[5,5,8192]{2,1,0:T(8,128)S(1)}, f32[5,5,8192]{2,1,0:T(8,128)}, u32[]{:S(2)}) copy-start(f32[5,5,8192]{2,1,0:T(8,128)} %param.37) | copy-start | bytes 2457604
  47.5 16.4 %copy-start.30 = (s32[4,8192]{1,0:T(4,128)S(1)}, s32[4,8192]{1,0:T(4,128)}, u32[]{:S(2)}) copy-start(s32[4,8192]{1,0:T(4,128)} %param.32) | copy-start | bytes 393220
  47.5 17.1 %copy-start.1 = (f32[5,8192]{1,0:T(8,128)S(1)}, f32[5,8192]{1,0:T(8,128)}, u32[]{:S(2)}) copy-start(f32[5,8192]{1,0:T(8,128)} %param.29) | copy-start | bytes 491524
  53.6 122.0 %all-to-all-start = ((f32[7,32,512]{2,0,1:T(8,128)}), f32[7,32,512]{2,0,1:T(8,128)S(1)}, u32[]{:S(2)}, u32[]{:S(2)}) async-start(f32[7,32,512]{2,0,1:T(8,128)} %copy.190), calls=%async_computation | async-start | bytes 1048576 | tf_op jit(solution)/shard_map/all_to_all | solution.py:196
  105.6 12.3 %copy-start.3 = (f32[8192]{0:T(1024)S(1)}, f32[8192]{0:T(1024)}, u32[]{:S(2)}) copy-start(f32[8192]{0:T(1024)} %param.35) | copy-start | bytes 98308
  105.6 12.3 %copy-start.4 = (f32[8192]{0:T(1024)S(1)}, f32[8192]{0:T(1024)}, u32[]{:S(2)}) copy-start(f32[8192]{0:T(1024)} %param.36) | copy-start | bytes 98308
  117.9 8.4 %copy-start.39 = (f32[1,8192]{1,0:T(1,128)S(1)}, f32[1,8192]{1,0:T(1,128)}, u32[]{:S(2)}) copy-start(f32[1,8192]{1,0:T(1,128)} %get-tuple-element.482) | copy-start | bytes 98308
  157.0 8.1 %copy-start.11 = (f32[8192]{0:T(1024)S(1)}, f32[8192]{0:T(1024)}, u32[]{:S(2)}) copy-start(f32[8192]{0:T(1024)} %copy-done.10) | copy-start | bytes 98308
  157.0 8.1 %copy-start.37 = (f32[1,1,8192]{2,1,0:T(1,128)S(1)}, f32[1,1,8192]{2,1,0:T(1,128)}, u32[]{:S(2)}) copy-start(f32[1,1,8192]{2,1,0:T(1,128)} %get-tuple-element.470) | copy-start | bytes 98308
  157.3 8.9 %copy-start.13 = (f32[8192]{0:T(1024)S(1)}, f32[8192]{0:T(1024)}, u32[]{:S(2)}) copy-start(f32[8192]{0:T(1024)} %copy-done.12) | copy-start | bytes 98308
  157.3 8.9 %copy-start.15 = (f32[8192]{0:T(1024)S(1)}, f32[8192]{0:T(1024)}, u32[]{:S(2)}) copy-start(f32[8192]{0:T(1024)} %copy-done.14) | copy-start | bytes 98308
  157.3 8.9 %copy-start.17 = (f32[8192]{0:T(1024)S(1)}, f32[8192]{0:T(1024)}, u32[]{:S(2)}) copy-start(f32[8192]{0:T(1024)} %copy-done.16) | copy-start | bytes 98308
  157.3 8.9 %copy-start.35 = (f32[1,1,8192]{2,1,0:T(1,128)S(1)}, f32[1,1,8192]{2,1,0:T(1,128)}, u32[]{:S(2)}) copy-start(f32[1,1,8192]{2,1,0:T(1,128)} %get-tuple-element.469) | copy-start | bytes 98308
  157.3 8.9 %copy-start.36 = (f32[1,1,8192]{2,1,0:T(1,128)S(1)}, f32[1,1,8192]{2,1,0:T(1,128)}, u32[]{:S(2)}) copy-start(f32[1,1,8192]{2,1,0:T(1,128)} %get-tuple-element.486) | copy-start | bytes 98308
  157.8 9.4 %copy-start.19 = (f32[8192]{0:T(1024)S(1)}, f32[8192]{0:T(1024)}, u32[]{:S(2)}) copy-start(f32[8192]{0:T(1024)} %copy-done.18) | copy-start | bytes 98308
  157.8 9.4 %copy-start.21 = (f32[8192]{0:T(1024)S(1)}, f32[8192]{0:T(1024)}, u32[]{:S(2)}) copy-start(f32[8192]{0:T(1024)} %copy-done.20) | copy-start | bytes 98308
  157.8 9.4 %copy-start.23 = (f32[8192]{0:T(1024)S(1)}, f32[8192]{0:T(1024)}, u32[]{:S(2)}) copy-start(f32[8192]{0:T(1024)} %copy-done.22) | copy-start | bytes 98308
  157.8 9.4 %copy-start.33 = (f32[1,1,8192]{2,1,0:T(1,128)S(1)}, f32[1,1,8192]{2,1,0:T(1,128)}, u32[]{:S(2)}) copy-start(f32[1,1,8192]{2,1,0:T(1,128)} %get-tuple-element.468) | copy-start | bytes 98308
  157.8 9.4 %copy-start.34 = (f32[1,1,8192]{2,1,0:T(1,128)S(1)}, f32[1,1,8192]{2,1,0:T(1,128)}, u32[]{:S(2)}) copy-start(f32[1,1,8192]{2,1,0:T(1,128)} %get-tuple-element.487) | copy-start | bytes 98308
  157.9 10.3 %copy-start.31 = (f32[1,1,8192]{2,1,0:T(1,128)S(1)}, f32[1,1,8192]{2,1,0:T(1,128)}, u32[]{:S(2)}) copy-start(f32[1,1,8192]{2,1,0:T(1,128)} %get-tuple-element.424) | copy-start | bytes 98308
  157.9 10.3 %copy-start.32 = (f32[1,1,8192]{2,1,0:T(1,128)S(1)}, f32[1,1,8192]{2,1,0:T(1,128)}, u32[]{:S(2)}) copy-start(f32[1,1,8192]{2,1,0:T(1,128)} %get-tuple-element.497) | copy-start | bytes 98308
  161.6 66.8 %collective-permute-start.2 = (f32[5,128]{0,1:T(8,128)S(1)}, f32[5,128]{0,1:T(8,128)S(1)}, u32[]{:S(2)}, u32[]{:S(2)}) collective-permute-start(f32[5,128]{0,1:T(8,128)S(1)} %get-tuple-element.467), channel_id=1, source_target_pairs={{0,1},{1,2},{2,3},{3,4},{4,5},{5,6},{6,7},{7,8},{8,9},{9,10},{10,1... | collective-permute-start | bytes 7688 | tf_op jit(solution)/shard_map/ppermute | solution.py:29
  163.6 66.9 %collective-permute-start.3 = (f32[5,128]{0,1:T(8,128)S(1)}, f32[5,128]{0,1:T(8,128)S(1)}, u32[]{:S(2)}, u32[]{:S(2)}) collective-permute-start(f32[5,128]{0,1:T(8,128)S(1)} %get-tuple-element.466), channel_id=1, source_target_pairs={{1,0},{2,1},{3,2},{4,3},{5,4},{6,5},{7,6},{8,7},{9,8},{10,9},{11,1... | collective-permute-start | bytes 7688 | tf_op jit(solution)/shard_map/ppermute | solution.py:30
  220.5 18.5 %all-to-all-start.1 = ((f32[3,32,512]{2,0,1:T(4,128)}), f32[3,32,512]{2,0,1:T(4,128)S(1)}, u32[]{:S(2)}, u32[]{:S(2)}) async-start(f32[3,32,512]{2,0,1:T(4,128)} %copy.193), calls=%async_computation.1 | async-start | bytes 524288 | tf_op jit(solution)/shard_map/all_to_all | solution.py:225
  281.0 20.1 %copy-start.46 = (f32[8192]{0:T(1024)S(1)}, f32[8192]{0:T(1024)}, u32[]{:S(2)}) copy-start(f32[8192]{0:T(1024)} %param.31) | copy-start | bytes 98308
  (26 other events, 146.9 us)
where the time goes:
time: 312 us; the launch traced here: 310 us
  local copies, waits for them, and re-layouts  126 us (40%)
  matrix products  81.2 us (26%)
  other arithmetic  66 us (21%)
  starting transfers between devices  31.8 us (10%)
    dot_general x4, matrix products, pick_corners(): jnp.einsum('gaew,gcw->gcae', selector, window, precision=lax.Precision.HI...  37.3 us
    gather x1, local copies, waits for them, and re-layouts, body(): contact = back[:, slots]  31.3 us
    dot_general x4, matrix products, spread_forces(): jnp.einsum('gaew,gcae->gcw', selector, part, precision=lax.Precision.HIGH...  26.2 us
    scatter x1, local copies, waits for them, and re-layouts, body(): jnp.zeros((7, devices * capacity), jnp.float32).at[:, slots].set(payload)  24.6 us
    scatter-add x1, local copies, waits for them, and re-layouts, body(): total = (-internal).at[0:3].add(contact)  20.1 us
    reduce_sum x4, other arithmetic, pair_forces(): reach = jnp.exp(-jnp.sum(offset * offset, axis=0) / REACH_SQ)  17.3 us
    dot_general x4, matrix products, pair_forces(): jnp.einsum('bij,cbj->cbi', magnitude, face_block[3:6], precision=lax.Prec...  15.5 us
    ppermute x3, starting transfers between devices, padded_2(): before = lax.ppermute(last, axis, up)  10.1 us
  transfers between devices with their start and end apart: 8, of which 1 were waited for; matrix products, arithmetic and copies ran while one was open for 65% of the time, Pallas kernels for 0%

commit v1 on v0

v1 whole, which is shorter than its diff:
```python
import functools

import jax
import jax.numpy as jnp
from jax import lax
from jax.experimental import pallas as pl
from jax.experimental.pallas import tpu as pltpu
from jax.sharding import PartitionSpec as P

LANES = 128
HALO = 128
GHOST = 256
LOW = 64

LOBATTO_POINTS = (-1.0, -0.6546536707079771, 0.0, 0.6546536707079771, 1.0)
LOBATTO_WEIGHTS = (0.1, 49.0 / 90.0, 32.0 / 45.0, 49.0 / 90.0, 0.1)
PLANE_MODULUS = 1.0 / 0.91
POISSON = 0.3
SHEAR_MODULUS = 5.0 / 6.0 / 2.6
DAMPING = 0.3
REACH_SQ = 0.5
LOG2E = 1.4426950408889634

F32 = jnp.float32
BF16 = jnp.bfloat16
NT = (((1,), (1,)), ((), ()))
NN = (((1,), (0,)), ((), ()))


def iota(shape, dim):
    return lax.broadcasted_iota(jnp.int32, shape, dim)


def split2(x):
    high = x.astype(BF16).astype(F32)
    return high, x - high


def tiled_rows(row, count):
    packed = jnp.broadcast_to(row, (16, row.shape[1])).astype(BF16)
    return packed if count == 16 else jnp.concatenate([packed] * (count // 16), axis=0)


def arrange_kernel(owner, position, velocity, out, slot_out, lhs, rhs, acc, *, devices, capacity):
    rows = owner.shape[0]
    tiles = capacity // LANES
    upper = jnp.where(iota((LANES, 2 * LANES), 1) > iota((LANES, 2 * LANES), 0), 1.0, 0.0).astype(BF16)
    device_ids = iota((devices, LANES), 0)
    low_ids = iota((LOW, LANES), 0).astype(F32).astype(BF16)
    group_ids = iota((2 * LANES, LANES), 0).astype(F32).astype(BF16)
    acc[...] = jnp.zeros_like(acc)
    one, zero = jnp.ones((), BF16), jnp.zeros((), BF16)

    def step(k, base):
        owners = owner[pl.ds(pl.multiple_of(k * 8, 8), 8), :]
        masks = [jnp.broadcast_to(owners[s : s + 1], (devices, LANES)) == device_ids for s in range(8)]
        hot = jnp.concatenate([jnp.where(m, 1.0, 0.0).astype(BF16) for m in masks], axis=0)
        counted = lax.dot_general(hot, upper, NN, preferred_element_type=F32)
        ranks = []
        for s in range(8):
            part = counted[s * devices : (s + 1) * devices]
            ranks.append(jnp.sum(jnp.where(masks[s], part[:, :LANES] + base, 0.0), axis=0, keepdims=True))
            base = base + part[:, LANES:]
        rank = jnp.concatenate(ranks, axis=0).astype(jnp.int32)
        slot = owners * capacity + rank
        slot_out[pl.ds(pl.multiple_of(k * 8, 8), 8), :] = slot
        low = (slot & (LOW - 1)).astype(F32)
        group = (((slot >> 6) & 1) * LANES + (slot >> 7)).astype(F32)
        for s in range(8):
            lanes = pl.ds(pl.multiple_of(k * 8 * LANES + s * LANES, LANES), LANES)
            here = pl.ds(s * LANES, LANES)
            hot_low = jnp.where(tiled_rows(low[s : s + 1], LOW) == low_ids, one, zero)
            rhs[:, here] = jnp.where(tiled_rows(group[s : s + 1], 2 * LANES) == group_ids, one, zero)
            place = position[:, lanes]
            place = place + jnp.where(iota(place.shape, 0) == 0, 1.0, 0.0)
            for base_row, data in ((0, place), (3, velocity[0:3, lanes])):
                parts = split2(data)
                for c in range(3):
                    for half in range(2):
                        row = (base_row + c) * 2 + half
                        lhs[row * LOW : (row + 1) * LOW, here] = hot_low * tiled_rows(parts[half][c : c + 1], LOW)
        acc[...] += lax.dot_general(lhs[...], rhs[...], NT, preferred_element_type=F32)
        return base

    lax.fori_loop(0, rows // 8, step, jnp.zeros((devices, LANES), F32))
    for c in range(6):
        both = acc[2 * c * LOW : (2 * c + 1) * LOW, :] + acc[(2 * c + 1) * LOW : (2 * c + 2) * LOW, :]
        square = jnp.concatenate([both[:, :LANES], both[:, LANES:]], axis=0).T
        out[:, c * tiles : (c + 1) * tiles, :] = square.reshape(devices, tiles, LANES)


def face_kernel(center, angle, stiffness, ghost, velocity, slot, own, up, down):
    del slot
    count = stiffness.shape[0]
    faces = count * LANES
    azimuth = angle[0, :].reshape(count, LANES)
    elevation = angle[1, :].reshape(count, LANES)
    flat = jnp.cos(elevation)
    data = [center[c, :].reshape(count, LANES) for c in range(3)]
    data += [jnp.cos(azimuth) * flat, jnp.sin(azimuth) * flat, jnp.sin(elevation), stiffness[...]]
    wanted = ghost[...]
    wanted = jnp.concatenate([wanted, wanted], axis=0)
    row_of, lane_of = wanted >> 7, wanted & (LANES - 1)
    nodes = velocity.shape[1]
    up[...] = jnp.zeros_like(up)
    down[...] = jnp.zeros_like(down)
    up[0:5, :] = velocity[:, nodes - HALO :]
    down[0:5, :] = velocity[:, :HALO]
    for c in range(8):
        if c == 7:
            own[pl.ds(c, count, stride=8), :] = jnp.zeros((count, LANES), F32)
            continue
        own[pl.ds(c, count, stride=8), :] = data[c]
        found = jnp.zeros((8, LANES), F32)
        for r in range(count):
            source = jnp.broadcast_to(data[c][r : r + 1], (8, LANES))
            found = jnp.where(row_of == r, jnp.take_along_axis(source, lane_of, axis=1), found)
        for t in range(2):
            down[8 + 8 * t + c : 9 + 8 * t + c, :] = found[t : t + 1]
            up[8 + 8 * t + c : 9 + 8 * t + c, :] = found[2 + t : 3 + t]


def element_kernel(
    velocity, before, after, connectivity, grads, area, thickness, yields, stress,
    new_stress, own, rim_down, rim_up, ext, spread, where_row, where_lane, acc,
):
    nodes = velocity.shape[1]
    rows = nodes // LANES
    pitch = ext.shape[0] // 5
    chunk = 8 * LANES
    for c in range(5):
        ext[c * pitch : c * pitch + 1, :] = before[c : c + 1, :]
        for k in range(rows // 8):
            ext[c * pitch + 1 + 8 * k : c * pitch + 9 + 8 * k, :] = velocity[c, pl.ds(k * chunk, chunk)].reshape(8, LANES)
        ext[c * pitch + rows + 1 : c * pitch + rows + 2, :] = after[c : c + 1, :]
    for a in range(4):
        spread[(a * 8 + 5) * rows : (a * 8 + 8) * rows, :] = jnp.zeros((3 * rows, LANES), F32)
    acc[...] = jnp.zeros_like(acc)

    def elements(k, carry):
        here = pl.ds(pl.multiple_of(k * chunk, chunk), chunk)
        first = pl.multiple_of(k * 8, 8)
        packed = pl.ds(first, 8)
        sources = [[ext[pl.ds(c * pitch + k * 8 + j, 8), :] for j in range(3)] for c in range(5)]
        row_ids = iota((8, LANES), 0) + k * 8
        corner = []
        for a in range(4):
            index = connectivity[a, here].reshape(8, LANES)
            lane = index & (LANES - 1)
            rel = (index >> 7) - row_ids
            where_lane[pl.ds(a * rows + first, 8), :] = lane.astype(F32)
            where_row[pl.ds(a * rows + first, 8), :] = rel.astype(F32)
            second, third = rel == 1, rel == 2
            values = []
            for c in range(5):
                g = [jnp.take_along_axis(sources[c][j], lane, axis=1) for j in range(3)]
                values.append(jnp.where(third, g[2], jnp.where(second, g[1], g[0])))
            corner.append(values)
        gx = [grads[0, a, here].reshape(8, LANES) for a in range(4)]
        gy = [grads[1, a, here].reshape(8, LANES) for a in range(4)]

        def total(f):
            t = [f(a) for a in range(4)]
            return (t[0] + t[1]) + (t[2] + t[3])

        memb_xx = total(lambda a: gx[a] * corner[a][0])
        bend_xx = total(lambda a: gx[a] * corner[a][4])
        memb_yy = total(lambda a: gy[a] * corner[a][1])
        bend_yy = -total(lambda a: gy[a] * corner[a][3])
        memb_xy = total(lambda a: gy[a] * corner[a][0] + gx[a] * corner[a][1])
        bend_xy = total(lambda a: gy[a] * corner[a][4] - gx[a] * corner[a][3])
        shear_xz = total(lambda a: gx[a] * corner[a][2]) + 0.25 * total(lambda a: corner[a][4])
        shear_yz = total(lambda a: gy[a] * corner[a][2]) - 0.25 * total(lambda a: corner[a][3])
        thick = thickness[packed, :]
        limit = yields[packed, :]
        half_area = 0.5 * thick * area[packed, :]
        force = [None] * 5
        moment = [None] * 3
        for layer in range(5):
            height = (0.5 * LOBATTO_POINTS[layer]) * thick
            xx = memb_xx + height * bend_xx
            yy = memb_yy + height * bend_yy
            xy = memb_xy + height * bend_xy
            old = [stress[layer, c, here].reshape(8, LANES) for c in range(5)]
            t = [
                old[0] + PLANE_MODULUS * (xx + POISSON * yy),
                old[1] + PLANE_MODULUS * (yy + POISSON * xx),
                old[2] + (PLANE_MODULUS * 0.5 * (1.0 - POISSON)) * xy,
                old[3] + SHEAR_MODULUS * shear_xz,
                old[4] + SHEAR_MODULUS * shear_yz,
            ]
            plus, minus = t[0] + t[1], t[0] - t[1]
            mises = jnp.sqrt(
                0.25 * (plus * plus) + 0.75 * (minus * minus) + 3.0 * (t[2] * t[2] + t[3] * t[3] + t[4] * t[4])
            )
            factor = limit / jnp.maximum(mises, limit)
            weight = LOBATTO_WEIGHTS[layer] * half_area
            lever = weight * height
            for c in range(5):
                value = t[c] * factor
                new_stress[layer, c, here] = value.reshape(chunk)
                term = weight * value
                force[c] = term if layer == 0 else force[c] + term
                if c < 3 and layer != 2:
                    term = lever * value
                    moment[c] = term if layer == 0 else moment[c] + term
        for a in range(4):
            out = (
                gx[a] * force[0] + gy[a] * force[2],
                gy[a] * force[1] + gx[a] * force[2],
                gx[a] * force[3] + gy[a] * force[4],
                -(gy[a] * moment[1] + gx[a] * moment[2]) - 0.25 * force[4],
                gx[a] * moment[0] + gy[a] * moment[2] + 0.25 * force[3],
            )
            for c in range(5):
                spread[pl.ds((a * 8 + c) * rows + first, 8), :] = out[c]
        return carry

    lax.fori_loop(0, rows // 8, elements, 0)
    lane_ids = iota((LANES, LANES), 0).astype(F32).astype(BF16)
    one, zero = jnp.ones((), BF16), jnp.zeros((), BF16)

    def scatter_row(b):
        left, right = [], []
        for a in range(4):
            data = spread[pl.ds(a * 8 * rows + b, 8, stride=rows), :]
            high, low = split2(data)
            both = jnp.concatenate([high, low], axis=0).astype(BF16)
            rel = tiled_rows(where_row[pl.ds(a * rows + b, 1), :], 16)
            left.append(jnp.concatenate([jnp.where(rel == jnp.asarray(j, BF16), both, zero) for j in range(3)], axis=0))
            lane = tiled_rows(where_lane[pl.ds(a * rows + b, 1), :], LANES)
            right.append(jnp.where(lane == lane_ids, one, zero))
        out = lax.dot_general(
            jnp.concatenate(left, axis=1), jnp.concatenate(right, axis=1), NT, preferred_element_type=F32
        )
        return [out[16 * j : 16 * j + 8] + out[16 * j + 8 : 16 * j + 16] for j in range(3)]

    def scatter(step, carry):
        b = step * 4
        parts = [scatter_row(b + i) for i in range(4)]
        for i in range(4):
            for j in range(3):
                at = pl.ds(pl.multiple_of((b + i + j) * 8, 8), 8)
                acc[at, :] += parts[i][j]
        return carry

    lax.fori_loop(0, rows // 4, scatter, 0)
    rim_down[...] = acc[0:8, :]
    own[...] = acc[8 : 8 + 8 * rows, :]
    rim_up[...] = acc[8 + 8 * rows : 16 + 8 * rows, :]


def contact_kernel(pair_node, pair_face, pair_count, nodes, own, before, after, out, raw, face, normal, acc, *, devices, tiles):
    own_rows = own.shape[0]
    face_tiles = (own_rows + 32) // 8
    raw[0:16, :] = before[8:24, :]
    raw[16 : 16 + own_rows, :] = own[...]
    raw[16 + own_rows :, :] = after[8:24, :]
    sub = iota((8, LANES), 0)

    def prepare(f, carry):
        at = pl.multiple_of(f * 8, 8)
        data = raw[pl.ds(at, 8), :]
        centre = data - 0.5
        mean = [jnp.broadcast_to(data[3 + c : 4 + c], (8, LANES)) for c in range(3)]
        place = [jnp.broadcast_to(centre[c : c + 1], (8, LANES)) for c in range(3)]
        stiff = jnp.broadcast_to(data[6:7], (8, LANES))
        m_low = jnp.where(sub == 0, mean[0], jnp.where(sub == 1, mean[1], jnp.where(sub == 2, mean[2], 0.0)))
        coef_e = jnp.where(sub < 3, (2.0 / REACH_SQ * LOG2E) * centre, jnp.where(sub == 6, 1.0, 0.0))
        coef_d = -m_low
        coef_a = jnp.where((sub >= 3) & (sub < 6), (-DAMPING) * stiff * data, jnp.where(sub == 7, stiff, 0.0))
        square = place[0] * place[0] + place[1] * place[1] + place[2] * place[2]
        along = mean[0] * place[0] + mean[1] * place[1] + mean[2] * place[2]
        pieces = []
        for coef, const in ((coef_e, (-LOG2E / REACH_SQ) * square), (coef_d, along), (coef_a, None)):
            high, low = split2(coef)
            if const is None:
                last = jnp.zeros((8, LANES), F32)
            else:
                c_high, c_low = split2(const)
                last = jnp.where(sub == 0, c_high, jnp.where(sub == 1, c_low, 0.0))
            pieces.append(jnp.concatenate([high, high, low, last], axis=0).astype(BF16))
        face[pl.ds(pl.multiple_of(f * 32, 32), 32), :] = jnp.concatenate(pieces, axis=1)
        high, low = split2(m_low)
        top = jnp.concatenate([high, low], axis=0).astype(BF16)
        bottom = jnp.concatenate([high, jnp.zeros_like(high)], axis=0).astype(BF16)
        normal[pl.ds(pl.multiple_of(f * 16, 16), 16), :] = jnp.concatenate([top, bottom], axis=1)
        return carry

    lax.fori_loop(0, face_tiles, prepare, 0)
    acc[...] = jnp.zeros_like(acc)
    shift = jnp.where(iota((6, LANES), 0) == 0, 1.5, jnp.where(iota((6, LANES), 0) < 3, 0.5, 0.0))
    ones = jnp.ones((8, LANES), F32)

    def pair_force(node, which):
        source = node // tiles
        data = nodes[pl.ds(source * (6 * tiles) + (node - source * tiles), 6, stride=tiles), :]
        live = jnp.where(data[0:1] > 0.5, 1.0, 0.0)
        data = data - shift
        square = data * data
        square = square[0:1] + square[1:2] + square[2:3]
        full = jnp.concatenate([data, (-LOG2E / REACH_SQ) * square, live], axis=0)
        high, low = split2(full)
        matrix = jnp.concatenate([high, low, high, ones], axis=0).T.astype(BF16)
        at = pl.ds(pl.multiple_of(which * 32, 32), 32)
        terms = lax.dot_general(matrix, face[at, :], NN, preferred_element_type=F32)
        power, depth, scale = terms[:, :LANES], terms[:, LANES : 2 * LANES], terms[:, 2 * LANES :]
        magnitude = jnp.exp2(power) * jnp.maximum(depth, 0.0) * scale
        high = magnitude.astype(BF16)
        low = (magnitude - high.astype(F32)).astype(BF16)
        both = jnp.concatenate([high, low], axis=1)
        at = pl.ds(pl.multiple_of(which * 16, 16), 16)
        result = lax.dot_general(normal[at, :], both, NT, preferred_element_type=F32)
        return result[0:8] + result[8:16]

    count = pair_count[0]
    group = 4

    def step(i, carry):
        ids = [i * group + n for n in range(group)]
        at = [pair_node[q] for q in ids]
        found = [pair_force(at[n], pair_face[ids[n]]) for n in range(group)]
        for n in range(group):
            keep = jnp.where(ids[n] < count, 1.0, 0.0)
            rows = pl.ds(pl.multiple_of(at[n] * 8, 8), 8)
            acc[rows, :] += found[n] * keep
        return carry

    lax.fori_loop(0, (count + group - 1) // group, step, 0)
    total = devices * tiles
    for c in range(3):
        out[:, c * tiles : (c + 1) * tiles, :] = acc[pl.ds(c, total, stride=8), :].reshape(devices, tiles, LANES)


def final_kernel(back, slot, own, below, above, velocity, inv_mass, out, table, *, tiles):
    devices = back.shape[0]
    rows = slot.shape[0]
    for c in range(3):
        square = back[:, c * tiles : (c + 1) * tiles, :].reshape(devices * tiles, LANES).T
        wide = jnp.concatenate([square[:LOW], square[LOW:]], axis=1)
        high, low = split2(wide)
        table[2 * c * LOW : (2 * c + 1) * LOW, :] = high.astype(BF16)
        table[(2 * c + 1) * LOW : (2 * c + 2) * LOW, :] = low.astype(BF16)
    group_ids = iota((2 * LANES, LANES), 0).astype(F32).astype(BF16)
    low_ids = iota((LOW, LANES), 0)
    one, zero = jnp.ones((), BF16), jnp.zeros((), BF16)
    sub = iota((8, LANES), 0)

    def step(k, carry):
        slots = slot[pl.ds(pl.multiple_of(k * 8, 8), 8), :]
        low = slots & (LOW - 1)
        group = (((slots >> 6) & 1) * LANES + (slots >> 7)).astype(F32)
        for s in range(0, 8, 2):
            hot = [jnp.where(tiled_rows(group[i : i + 1], 2 * LANES) == group_ids, one, zero) for i in (s, s + 1)]
            picked = lax.dot_general(table[...], jnp.concatenate(hot, axis=1), NN, preferred_element_type=F32)
            for i in range(2):
                r = k * 8 + s + i
                mask = jnp.broadcast_to(low[s + i : s + i + 1], (LOW, LANES)) == low_ids
                contact = jnp.zeros((8, LANES), F32)
                for c in range(3):
                    part = picked[2 * c * LOW : (2 * c + 2) * LOW, i * LANES : (i + 1) * LANES]
                    value = jnp.sum(jnp.where(mask, part[:LOW] + part[LOW:], 0.0), axis=0, keepdims=True)
                    contact = jnp.where(sub == c, value, contact)
                lanes = pl.ds(pl.multiple_of(r * LANES, LANES), LANES)
                total = contact - own[pl.ds(pl.multiple_of(r * 8, 8), 8), :]
                out[:, lanes] = velocity[:, lanes] + inv_mass[pl.ds(r, 1), :] * total[0:5]
        return carry

    lax.fori_loop(0, rows // 8, step, 0)
    last = (rows - 1) * LANES
    out[:, 0:LANES] = out[:, 0:LANES] - inv_mass[0:1, :] * below[0:5, :]
    out[:, last:] = out[:, last:] - inv_mass[rows - 1 : rows, :] * above[0:5, :]


def call(kernel, outs, ins, scratch, cost, smem=0):
    vmem = pl.BlockSpec(memory_space=pltpu.VMEM)
    scalar = pl.BlockSpec(memory_space=pltpu.SMEM)
    return pl.pallas_call(
        kernel,
        out_shape=outs,
        in_specs=[scalar] * smem + [vmem] * (len(ins) - smem),
        out_specs=jax.tree.map(lambda _: vmem, outs),
        scratch_shapes=scratch,
        cost_estimate=pl.CostEstimate(flops=cost, bytes_accessed=cost // 100, transcendentals=0),
    )(*ins)


def body(
    velocity, position, inv_mass, connectivity, shape_grad, area, thickness, yield_stress, stress,
    contact_owner, face_center, face_angle, face_stiffness, ghost_list, pair_node, pair_face, pair_count,
):
    axes = ("dom", "sub")
    devices = lax.axis_size("dom") * lax.axis_size("sub")
    nodes = velocity.shape[1]
    faces = face_center.shape[1]
    rows = nodes // LANES
    capacity = 2 * nodes // devices
    tiles = capacity // LANES
    shape = lambda *s: jax.ShapeDtypeStruct(s, F32)
    view = lambda x: x.reshape(-1, LANES)

    outgoing, slot = call(
        functools.partial(arrange_kernel, devices=devices, capacity=capacity),
        (shape(devices, 6 * tiles, LANES), jax.ShapeDtypeStruct((rows, LANES), jnp.int32)),
        (view(contact_owner), position, velocity),
        [
            pltpu.VMEM((12 * LOW, 8 * LANES), BF16),
            pltpu.VMEM((2 * LANES, 8 * LANES), BF16),
            pltpu.VMEM((12 * LOW, 2 * LANES), F32),
        ],
        10**9,
    )
    incoming = lax.all_to_all(outgoing, axes, split_axis=0, concat_axis=0, tiled=True)
    own_faces, send_up, send_down = call(
        face_kernel,
        (shape(faces // LANES * 8, LANES), shape(24, LANES), shape(24, LANES)),
        (face_center, face_angle, view(face_stiffness), view(ghost_list), velocity, slot),
        [],
        10**8,
    )
    up = [(i, i + 1) for i in range(devices - 1)]
    down = [(j, i) for i, j in up]
    before = lax.ppermute(send_up, axes, up)
    after = lax.ppermute(send_down, axes, down)
    pitch = rows + 8
    new_stress, own, rim_down, rim_up = call(
        element_kernel,
        (shape(*stress.shape), shape(8 * rows, LANES), shape(8, LANES), shape(8, LANES)),
        (velocity, before, after, connectivity, shape_grad, view(area), view(thickness), view(yield_stress), stress),
        [
            pltpu.VMEM((5 * pitch, LANES), F32),
            pltpu.VMEM((4 * 8 * rows, LANES), F32),
            pltpu.VMEM((4 * rows, LANES), F32),
            pltpu.VMEM((4 * rows, LANES), F32),
            pltpu.VMEM((8 * (rows + 2), LANES), F32),
        ],
        2 * 10**9,
    )
    face_rows = own_faces.shape[0] + 32
    returned = call(
        functools.partial(contact_kernel, devices=devices, tiles=tiles),
        shape(devices, 3 * tiles, LANES),
        (pair_node, pair_face, pair_count, view(incoming), own_faces, before, after),
        [
            pltpu.VMEM((face_rows, LANES), F32),
            pltpu.VMEM((face_rows * 4, 3 * LANES), BF16),
            pltpu.VMEM((face_rows * 2, 2 * LANES), BF16),
            pltpu.VMEM((devices * tiles * 8, LANES), F32),
        ],
        10**9,
        smem=3,
    )
    back = lax.all_to_all(returned, axes, split_axis=0, concat_axis=0, tiled=True)
    above = lax.ppermute(rim_down, axes, down)
    below = lax.ppermute(rim_up, axes, up)
    new_velocity = call(
        functools.partial(final_kernel, tiles=tiles),
        shape(*velocity.shape),
        (back, slot, own, below, above, velocity, view(inv_mass)),
        [pltpu.VMEM((6 * LOW, 2 * LANES), BF16)],
        10**9,
    )
    return (new_velocity, new_stress)


def solution(mesh):
    split = ("dom", "sub")
    in_specs = (
        P(None, split), P(None, split), P(split), P(None, split), P(None, None, split),
        P(split), P(split), P(split), P(None, None, split), P(split, None),
        P(None, split), P(None, split), P(split), P(split), P(split), P(split), P(split),
    )
    out_specs = (P(None, split), P(None, None, split))
    return jax.shard_map(body, mesh=mesh, in_specs=in_specs, out_specs=out_specs, check_vma=False)
```

time: 312 us -> 88.1 us (0.28)
  the two profiles are of different devices: /device:TPU:0 before, /device:TPU:7 now
where the time goes in v1:
time: 88.1 us; the launch traced here: 87.5 us
  Pallas kernels  41.3 us (47%)
  starting transfers between devices  34 us (39%)
  waiting for transfers between devices  9.42 us (11%)
  local copies, waits for them, and re-layouts  1.44 us (2%)
  between operations  1.37 us (2%)
    pallas_call x5, Pallas kernels, call(): pl.pallas_call(kernel, out_shape=outs, in_specs=[scalar] * smem + [vmem]...  41.3 us
    all_to_all x1, starting transfers between devices, body(): lax.all_to_all(returned, axes, split_axis=0, concat_axis=0, tiled=True)  17.1 us
    all_to_all x1, starting transfers between devices, body(): lax.all_to_all(outgoing, axes, split_axis=0, concat_axis=0, tiled=True)  6.37 us
    ppermute x1, waiting for transfers between devices, body(): above = lax.ppermute(rim_down, axes, down)  4.99 us
    ppermute x1, waiting for transfers between devices, body(): after = lax.ppermute(send_down, axes, down)  4.43 us
    ppermute x1, starting transfers between devices, body(): below = lax.ppermute(rim_up, axes, up)  3.37 us
    ppermute x1, starting transfers between devices, body(): before = lax.ppermute(send_up, axes, up)  3.36 us
    ppermute x1, starting transfers between devices, body(): after = lax.ppermute(send_down, axes, down)  1.92 us
  transfers between devices with their start and end apart: 6, of which 2 were waited for; matrix products, arithmetic and copies ran while one was open for 0% of the time, Pallas kernels for 13%

profile of v1, /device:TPU:7, one launch (start us, length us, event | category | flops | bytes accessed | tf_op | source)
XLA Modules:
  0.0 87.5 jit_solution(18431528428856921829)
XLA Ops:
  0.6 9.3 %shard_map.176 = (f32[32,24,128]{2,1,0:T(8,128)}, s32[64,128]{1,0:T(8,128)}) custom-call(s32[64,128]{1,0:T(8,128)} %bitcast.9, f32[3,8192]{1,0:T(4,128)} %position.1, f32[5,8192]{1,0:T(8,128)} %velocity.7), custom_call_target="tpu_custom_call" | custom-call | flops 1000000000 | bytes 10000000 | tf_op jit(solution)/shard_map/pallas_call | solution.py:378
  9.9 6.4 %all-to-all-start = ((f32[32,24,128]{2,1,0:T(8,128)}), f32[32,24,128]{2,1,0:T(8,128)S(1)}, u32[]{:S(2)}, u32[]{:S(2)}) async-start(f32[32,24,128]{2,1,0:T(8,128)} %get-tuple-element.11), calls=%async_computation | async-start | bytes 786432 | tf_op jit(solution)/shard_map/all_to_all | solution.py:413
  16.3 1.8 %shard_map.177 = (f32[128,128]{1,0:T(8,128)}, f32[24,128]{1,0:T(8,128)}, f32[24,128]{1,0:T(8,128)}) custom-call(f32[3,2048]{1,0:T(4,128)} %center.1, f32[2,2048]{1,0:T(2,128)} %angle.1, f32[16,128]{1,0:T(8,128)} %bitcast.14, s32[4,128]{1,0:T(4,128)} %bitcast.15, f32[5,8192]{1,0:T(8,128)} %velocity.7, s32[64,128]{1,0:T(8,128)} %get-tuple-element.12.slot), custom_call_target="tpu_custom_call" | custom-call | flops 100000000 | bytes 1000000 | tf_op jit(solution)/shard_map/pallas_call | solution.py:378
  18.1 3.4 %collective-permute-start = (f32[24,128]{1,0:T(8,128)}, f32[24,128]{1,0:T(8,128)S(1)}, u32[]{:S(2)}, u32[]{:S(2)}) collective-permute-start(f32[24,128]{1,0:T(8,128)} %get-tuple-element.14), channel_id=1, source_target_pairs={{0,1},{1,2},{2,3},{3,4},{4,5},{5,6},{6,7},{7,8},{8,9},{9,10},{10,1... | collective-permute-start | bytes 36872 | tf_op jit(solution)/shard_map/ppermute | solution.py:423
  21.5 1.9 %collective-permute-start.1 = (f32[24,128]{1,0:T(8,128)}, f32[24,128]{1,0:T(8,128)S(1)}, u32[]{:S(2)}, u32[]{:S(2)}) collective-permute-start(f32[24,128]{1,0:T(8,128)} %get-tuple-element.15), channel_id=1, source_target_pairs={{1,0},{2,1},{3,2},{4,3},{5,4},{6,5},{7,6},{8,7},{9,8},{10,9},{11,1... | collective-permute-start | bytes 36872 | tf_op jit(solution)/shard_map/ppermute | solution.py:424
  24.0 0.0 collective-permute-done.before
  24.1 0.0 copy-start.2
  24.1 4.4 %collective-permute-done.1.after = f32[24,128]{1,0:T(8,128)S(1)} collective-permute-done((f32[24,128]{1,0:T(8,128)}, f32[24,128]{1,0:T(8,128)S(1)}, u32[]{:S(2)}, u32[]{:S(2)}) %collective-permute-start.1) | collective-permute-done | bytes 12320 | tf_op jit(solution)/shard_map/ppermute | solution.py:424
  28.5 0.0 copy-start.3
  28.5 0.0 all-to-all-done
  28.5 0.0 copy-start
  28.5 0.0 copy-done.2
  28.5 0.6 copy-done.3
  29.1 0.2 copy-done
  29.2 15.8 %shard_map.178 = f32[32,12,128]{2,1,0:T(8,128)} custom-call(s32[128]{0:T(128)} %pair_node.1, s32[128]{0:T(128)} %pair_face.1, s32[1]{0:T(128)S(6)} %copy.19.pair_count, f32[768,128]{1,0:T(8,128)} %bitcast.8, f32[128,128]{1,0:T(8,128)} %get-tuple-element.13.own, f32[24,128]{1,0:T(8,128)} %copy-done.2, f32[24,128]{1,0:T(8,128)} %copy-done.3), custom_call_target="tpu_custom_call" | custom-call | flops 1000000000 | bytes 10000000 | tf_op jit(solution)/shard_map/pallas_call | solution.py:378
  45.0 17.1 %all-to-all-start.1 = ((f32[32,12,128]{2,1,0:T(8,128)}), f32[32,12,128]{2,1,0:T(8,128)S(1)}, u32[]{:S(2)}, u32[]{:S(2)}) async-start(f32[32,12,128]{2,1,0:T(8,128)} %shard_map.178), calls=%async_computation.1 | async-start | bytes 524288 | tf_op jit(solution)/shard_map/all_to_all | solution.py:453
  62.1 9.3 %shard_map.179 = (f32[5,5,8192]{2,1,0:T(8,128)}, f32[512,128]{1,0:T(8,128)}, f32[8,128]{1,0:T(8,128)}, f32[8,128]{1,0:T(8,128)}) custom-call(f32[5,8192]{1,0:T(8,128)} %velocity.7, f32[24,128]{1,0:T(8,128)} %copy-done.2, f32[24,128]{1,0:T(8,128)} %copy-done.3, s32[4,8192]{1,0:T(4,128)} %connectivity.1, f32[2,4,8192]{2,1,0:T(4,128)} %grads.1, ...), custom_call_target="tpu_custom_call" | custom-call | flops 2000000000 | bytes 20000000 | tf_op jit(solution)/shard_map/pallas_call | solution.py:378
  71.4 3.4 %collective-permute-start.2 = (f32[8,128]{1,0:T(8,128)}, f32[8,128]{1,0:T(8,128)S(1)}, u32[]{:S(2)}, u32[]{:S(2)}) collective-permute-start(f32[8,128]{1,0:T(8,128)} %get-tuple-element.17), channel_id=1, source_target_pairs={{0,1},{1,2},{2,3},{3,4},{4,5},{5,6},{6,7},{7,8},{8,9},{9,10},{10,1... | collective-permute-start | bytes 12296 | tf_op jit(solution)/shard_map/ppermute | solution.py:455
  74.8 1.9 %collective-permute-start.3 = (f32[8,128]{1,0:T(8,128)}, f32[8,128]{1,0:T(8,128)S(1)}, u32[]{:S(2)}, u32[]{:S(2)}) collective-permute-start(f32[8,128]{1,0:T(8,128)} %get-tuple-element.18), channel_id=1, source_target_pairs={{1,0},{2,1},{3,2},{4,3},{5,4},{6,5},{7,6},{8,7},{9,8},{10,9},{11,1... | collective-permute-start | bytes 12296 | tf_op jit(solution)/shard_map/ppermute | solution.py:454
  76.7 0.0 collective-permute-done.2.below
  76.7 0.0 copy-start.4
  76.7 5.0 %collective-permute-done.3.above = f32[8,128]{1,0:T(8,128)S(1)} collective-permute-done((f32[8,128]{1,0:T(8,128)}, f32[8,128]{1,0:T(8,128)S(1)}, u32[]{:S(2)}, u32[]{:S(2)}) %collective-permute-start.3) | collective-permute-done | bytes 4128 | tf_op jit(solution)/shard_map/ppermute | solution.py:454
  81.7 0.0 copy-start.5
  81.7 0.0 all-to-all-done.1.back
  81.7 0.0 copy-start.1
  81.7 0.0 copy-done.4
  81.7 0.6 copy-done.5
  82.3 0.1 copy-done.1
  82.4 5.1 %shard_map.180 = f32[5,8192]{1,0:T(8,128)} custom-call(f32[32,12,128]{2,1,0:T(8,128)} %copy-done.1, s32[64,128]{1,0:T(8,128)} %get-tuple-element.12.slot, f32[512,128]{1,0:T(8,128)} %get-tuple-element.16.own, f32[8,128]{1,0:T(8,128)} %copy-done.4, f32[8,128]{1,0:T(8,128)} %copy-done.5, f32[5,8192]{1,0:T(8,128)} %velocity.7, f32[64,128]{1,0:T(8,128)} %bitcast.13), custom_call_target="tpu_custom_call" | custom-call | flops 1000000000 | bytes 10000000 | tf_op jit(solution)/shard_map/pallas_call | solution.py:378
Async XLA Ops:
  9.9 18.6 %all-to-all-start = ((f32[32,24,128]{2,1,0:T(8,128)}), f32[32,24,128]{2,1,0:T(8,128)S(1)}, u32[]{:S(2)}, u32[]{:S(2)}) async-start(f32[32,24,128]{2,1,0:T(8,128)} %get-tuple-element.11), calls=%async_computation | async-start | bytes 786432 | tf_op jit(solution)/shard_map/all_to_all | solution.py:413
  18.1 5.9 %collective-permute-start = (f32[24,128]{1,0:T(8,128)}, f32[24,128]{1,0:T(8,128)S(1)}, u32[]{:S(2)}, u32[]{:S(2)}) collective-permute-start(f32[24,128]{1,0:T(8,128)} %get-tuple-element.14), channel_id=1, source_target_pairs={{0,1},{1,2},{2,3},{3,4},{4,5},{5,6},{6,7},{7,8},{8,9},{9,10},{10,1... | collective-permute-start | bytes 36872 | tf_op jit(solution)/shard_map/ppermute | solution.py:423
  21.5 7.0 %collective-permute-start.1 = (f32[24,128]{1,0:T(8,128)}, f32[24,128]{1,0:T(8,128)S(1)}, u32[]{:S(2)}, u32[]{:S(2)}) collective-permute-start(f32[24,128]{1,0:T(8,128)} %get-tuple-element.15), channel_id=1, source_target_pairs={{1,0},{2,1},{3,2},{4,3},{5,4},{6,5},{7,6},{8,7},{9,8},{10,9},{11,1... | collective-permute-start | bytes 36872 | tf_op jit(solution)/shard_map/ppermute | solution.py:424
  24.1 4.4 %copy-start.2 = (f32[24,128]{1,0:T(8,128)}, f32[24,128]{1,0:T(8,128)S(1)}, u32[]{:S(2)}) copy-start(f32[24,128]{1,0:T(8,128)S(1)} %collective-permute-done.before) | copy-start | bytes 36868
  28.5 0.6 copy-start.3
  28.5 0.7 copy-start
  45.0 36.7 %all-to-all-start.1 = ((f32[32,12,128]{2,1,0:T(8,128)}), f32[32,12,128]{2,1,0:T(8,128)S(1)}, u32[]{:S(2)}, u32[]{:S(2)}) async-start(f32[32,12,128]{2,1,0:T(8,128)} %shard_map.178), calls=%async_computation.1 | async-start | bytes 524288 | tf_op jit(solution)/shard_map/all_to_all | solution.py:453
  71.4 5.3 %collective-permute-start.2 = (f32[8,128]{1,0:T(8,128)}, f32[8,128]{1,0:T(8,128)S(1)}, u32[]{:S(2)}, u32[]{:S(2)}) collective-permute-start(f32[8,128]{1,0:T(8,128)} %get-tuple-element.17), channel_id=1, source_target_pairs={{0,1},{1,2},{2,3},{3,4},{4,5},{5,6},{6,7},{7,8},{8,9},{9,10},{10,1... | collective-permute-start | bytes 12296 | tf_op jit(solution)/shard_map/ppermute | solution.py:455
  74.8 6.9 %collective-permute-start.3 = (f32[8,128]{1,0:T(8,128)}, f32[8,128]{1,0:T(8,128)S(1)}, u32[]{:S(2)}, u32[]{:S(2)}) collective-permute-start(f32[8,128]{1,0:T(8,128)} %get-tuple-element.18), channel_id=1, source_target_pairs={{1,0},{2,1},{3,2},{4,3},{5,4},{6,5},{7,6},{8,7},{9,8},{10,9},{11,1... | collective-permute-start | bytes 12296 | tf_op jit(solution)/shard_map/ppermute | solution.py:454
  76.7 5.0 %copy-start.4 = (f32[8,128]{1,0:T(8,128)}, f32[8,128]{1,0:T(8,128)S(1)}, u32[]{:S(2)}) copy-start(f32[8,128]{1,0:T(8,128)S(1)} %collective-permute-done.2.below) | copy-start | bytes 12292
  81.7 0.6 copy-start.5
  81.7 0.7 copy-start.1

commit v2 on v1

--- a/solution.py
+++ b/solution.py
@@ -68,9 +68,8 @@
         group = (((slot >> 6) & 1) * LANES + (slot >> 7)).astype(F32)
         for s in range(8):
             lanes = pl.ds(pl.multiple_of(k * 8 * LANES + s * LANES, LANES), LANES)
-            here = pl.ds(s * LANES, LANES)
             hot_low = jnp.where(tiled_rows(low[s : s + 1], LOW) == low_ids, one, zero)
-            rhs[:, here] = jnp.where(tiled_rows(group[s : s + 1], 2 * LANES) == group_ids, one, zero)
+            rhs[s, :, :] = jnp.where(tiled_rows(group[s : s + 1], 2 * LANES) == group_ids, one, zero)
             place = position[:, lanes]
             place = place + jnp.where(iota(place.shape, 0) == 0, 1.0, 0.0)
             for base_row, data in ((0, place), (3, velocity[0:3, lanes])):
@@ -78,8 +77,10 @@
                 for c in range(3):
                     for half in range(2):
                         row = (base_row + c) * 2 + half
-                        lhs[row * LOW : (row + 1) * LOW, here] = hot_low * tiled_rows(parts[half][c : c + 1], LOW)
-        acc[...] += lax.dot_general(lhs[...], rhs[...], NT, preferred_element_type=F32)
+                        lhs[s, row * LOW : (row + 1) * LOW, :] = hot_low * tiled_rows(parts[half][c : c + 1], LOW)
+        left = jnp.concatenate([lhs[s] for s in range(8)], axis=1)
+        right = jnp.concatenate([rhs[s] for s in range(8)], axis=1)
+        acc[...] += lax.dot_general(left, right, NT, preferred_element_type=F32)
         return base
 
     lax.fori_loop(0, rows // 8, step, jnp.zeros((devices, LANES), F32))
@@ -122,7 +123,7 @@
 
 def element_kernel(
     velocity, before, after, connectivity, grads, area, thickness, yields, stress,
-    new_stress, own, rim_down, rim_up, ext, spread, where_row, where_lane, acc,
+    new_stress, spread, token, ext,
 ):
     nodes = velocity.shape[1]
     rows = nodes // LANES
@@ -133,9 +134,8 @@
         for k in range(rows // 8):
             ext[c * pitch + 1 + 8 * k : c * pitch + 9 + 8 * k, :] = velocity[c, pl.ds(k * chunk, chunk)].reshape(8, LANES)
         ext[c * pitch + rows + 1 : c * pitch + rows + 2, :] = after[c : c + 1, :]
-    for a in range(4):
-        spread[(a * 8 + 5) * rows : (a * 8 + 8) * rows, :] = jnp.zeros((3 * rows, LANES), F32)
-    acc[...] = jnp.zeros_like(acc)
+    spread[20 * rows :, :] = jnp.zeros((3 * rows, LANES), F32)
+    token[...] = jnp.zeros_like(token)
 
     def elements(k, carry):
         here = pl.ds(pl.multiple_of(k * chunk, chunk), chunk)
@@ -148,8 +148,6 @@
             index = connectivity[a, here].reshape(8, LANES)
             lane = index & (LANES - 1)
             rel = (index >> 7) - row_ids
-            where_lane[pl.ds(a * rows + first, 8), :] = lane.astype(F32)
-            where_row[pl.ds(a * rows + first, 8), :] = rel.astype(F32)
             second, third = rel == 1, rel == 2
             values = []
             for c in range(5):
@@ -213,22 +211,31 @@
                 gx[a] * moment[0] + gy[a] * moment[2] + 0.25 * force[3],
             )
             for c in range(5):
-                spread[pl.ds((a * 8 + c) * rows + first, 8), :] = out[c]
+                spread[pl.ds((a * 5 + c) * rows + first, 8), :] = out[c]
         return carry
 
     lax.fori_loop(0, rows // 8, elements, 0)
+
+
+def spread_kernel(spread, connectivity, after, own, rim_down, rim_up, acc):
+    del after
+    rows = connectivity.shape[1] // LANES
+    acc[...] = jnp.zeros_like(acc)
     lane_ids = iota((LANES, LANES), 0).astype(F32).astype(BF16)
     one, zero = jnp.ones((), BF16), jnp.zeros((), BF16)
 
     def scatter_row(b):
         left, right = [], []
+        index = connectivity[:, pl.ds(pl.multiple_of(b * LANES, LANES), LANES)]
+        lanes = (index & (LANES - 1)).astype(F32)
+        rels = ((index >> 7) - b).astype(F32)
         for a in range(4):
-            data = spread[pl.ds(a * 8 * rows + b, 8, stride=rows), :]
+            data = spread[pl.ds(a * 5 * rows + b, 8, stride=rows), :]
             high, low = split2(data)
             both = jnp.concatenate([high, low], axis=0).astype(BF16)
-            rel = tiled_rows(where_row[pl.ds(a * rows + b, 1), :], 16)
+            rel = tiled_rows(rels[a : a + 1], 16)
             left.append(jnp.concatenate([jnp.where(rel == jnp.asarray(j, BF16), both, zero) for j in range(3)], axis=0))
-            lane = tiled_rows(where_lane[pl.ds(a * rows + b, 1), :], LANES)
+            lane = tiled_rows(lanes[a : a + 1], LANES)
             right.append(jnp.where(lane == lane_ids, one, zero))
         out = lax.dot_general(
             jnp.concatenate(left, axis=1), jnp.concatenate(right, axis=1), NT, preferred_element_type=F32
@@ -250,7 +257,10 @@
     rim_up[...] = acc[8 + 8 * rows : 16 + 8 * rows, :]
 
 
-def contact_kernel(pair_node, pair_face, pair_count, nodes, own, before, after, out, raw, face, normal, acc, *, devices, tiles):
+def contact_kernel(
+    pair_node, pair_face, pair_count, nodes, own, before, after, token, out, raw, face, mean, table, acc, *, devices, tiles
+):
+    del token
     own_rows = own.shape[0]
     face_tiles = (own_rows + 32) // 8
     raw[0:16, :] = before[8:24, :]
@@ -258,63 +268,72 @@
     raw[16 + own_rows :, :] = after[8:24, :]
     sub = iota((8, LANES), 0)
 
-    def prepare(f, carry):
-        at = pl.multiple_of(f * 8, 8)
-        data = raw[pl.ds(at, 8), :]
+    def prepare(f):
+        data = raw[pl.ds(pl.multiple_of(f * 8, 8), 8), :]
         centre = data - 0.5
-        mean = [jnp.broadcast_to(data[3 + c : 4 + c], (8, LANES)) for c in range(3)]
+        normal = [jnp.broadcast_to(data[3 + c : 4 + c], (8, LANES)) for c in range(3)]
         place = [jnp.broadcast_to(centre[c : c + 1], (8, LANES)) for c in range(3)]
         stiff = jnp.broadcast_to(data[6:7], (8, LANES))
-        m_low = jnp.where(sub == 0, mean[0], jnp.where(sub == 1, mean[1], jnp.where(sub == 2, mean[2], 0.0)))
+        m_low = jnp.where(sub == 0, normal[0], jnp.where(sub == 1, normal[1], jnp.where(sub == 2, normal[2], 0.0)))
         coef_e = jnp.where(sub < 3, (2.0 / REACH_SQ * LOG2E) * centre, jnp.where(sub == 6, 1.0, 0.0))
         coef_d = -m_low
-        coef_a = jnp.where((sub >= 3) & (sub < 6), (-DAMPING) * stiff * data, jnp.where(sub == 7, stiff, 0.0))
+        inside = (sub >= 3) & (sub < 6)
+        coef_a = jnp.where(inside, (-DAMPING) * stiff * data, jnp.where(sub == 7, stiff, 0.0))
         square = place[0] * place[0] + place[1] * place[1] + place[2] * place[2]
-        along = mean[0] * place[0] + mean[1] * place[1] + mean[2] * place[2]
-        pieces = []
-        for coef, const in ((coef_e, (-LOG2E / REACH_SQ) * square), (coef_d, along), (coef_a, None)):
+        along = normal[0] * place[0] + normal[1] * place[1] + normal[2] * place[2]
+        for q, (coef, const) in enumerate(((coef_e, (-LOG2E / REACH_SQ) * square), (coef_d, along), (coef_a, None))):
             high, low = split2(coef)
             if const is None:
-                last = jnp.zeros((8, LANES), F32)
+                last = jnp.where(inside, data, 0.0)
             else:
                 c_high, c_low = split2(const)
                 last = jnp.where(sub == 0, c_high, jnp.where(sub == 1, c_low, 0.0))
-            pieces.append(jnp.concatenate([high, high, low, last], axis=0).astype(BF16))
-        face[pl.ds(pl.multiple_of(f * 32, 32), 32), :] = jnp.concatenate(pieces, axis=1)
-        high, low = split2(m_low)
-        top = jnp.concatenate([high, low], axis=0).astype(BF16)
-        bottom = jnp.concatenate([high, jnp.zeros_like(high)], axis=0).astype(BF16)
-        normal[pl.ds(pl.multiple_of(f * 16, 16), 16), :] = jnp.concatenate([top, bottom], axis=1)
+            turned = jnp.concatenate([high, high, low, last], axis=0).T
+            packed = turned.astype(BF16)
+            for j in range(8):
+                at = f * 384 + j * 48
+                face[pl.ds(pl.multiple_of(at + q * 16, 16), 16), :] = packed[j * 16 : j * 16 + 16]
+                if const is None:
+                    for c in range(3):
+                        column = turned[j * 16 : j * 16 + 16, 27 + c : 28 + c]
+                        mean[pl.ds(pl.multiple_of(at + c * 16, 16), 16), :] = jnp.broadcast_to(column, (16, LANES))
+
+    def prepare_group(i, carry):
+        for n in range(4):
+            prepare(i * 4 + n)
         return carry
 
-    lax.fori_loop(0, face_tiles, prepare, 0)
+    lax.fori_loop(0, face_tiles // 4, prepare_group, 0)
+    total = devices * tiles
     acc[...] = jnp.zeros_like(acc)
-    shift = jnp.where(iota((6, LANES), 0) == 0, 1.5, jnp.where(iota((6, LANES), 0) < 3, 0.5, 0.0))
-    ones = jnp.ones((8, LANES), F32)
+    for c in range(6):
+        flat = nodes[:, c * tiles : (c + 1) * tiles, :].reshape(total, LANES)
+        if c == 0:
+            table[pl.ds(7, total, stride=8), :] = jnp.where(flat > 0.5, 1.0, 0.0)
+        flat = flat - (1.5, 0.5, 0.5)[c] if c < 3 else flat
+        if c < 3:
+            square = flat * flat if c == 0 else square + flat * flat
+        table[pl.ds(c, total, stride=8), :] = flat
+    table[pl.ds(6, total, stride=8), :] = (-LOG2E / REACH_SQ) * square
+    ones = jnp.where(sub < 2, 1.0, 0.0)
 
     def pair_force(node, which):
-        source = node // tiles
-        data = nodes[pl.ds(source * (6 * tiles) + (node - source * tiles), 6, stride=tiles), :]
-        live = jnp.where(data[0:1] > 0.5, 1.0, 0.0)
-        data = data - shift
-        square = data * data
-        square = square[0:1] + square[1:2] + square[2:3]
-        full = jnp.concatenate([data, (-LOG2E / REACH_SQ) * square, live], axis=0)
-        high, low = split2(full)
-        matrix = jnp.concatenate([high, low, high, ones], axis=0).T.astype(BF16)
-        at = pl.ds(pl.multiple_of(which * 32, 32), 32)
-        terms = lax.dot_general(matrix, face[at, :], NN, preferred_element_type=F32)
-        power, depth, scale = terms[:, :LANES], terms[:, LANES : 2 * LANES], terms[:, 2 * LANES :]
-        magnitude = jnp.exp2(power) * jnp.maximum(depth, 0.0) * scale
-        high = magnitude.astype(BF16)
-        low = (magnitude - high.astype(F32)).astype(BF16)
-        both = jnp.concatenate([high, low], axis=1)
-        at = pl.ds(pl.multiple_of(which * 16, 16), 16)
-        result = lax.dot_general(normal[at, :], both, NT, preferred_element_type=F32)
-        return result[0:8] + result[8:16]
+        high, low = split2(table[pl.ds(pl.multiple_of(node * 8, 8), 8), :])
+        matrix = jnp.concatenate([high, low, high, ones], axis=0).astype(BF16)
+        at = pl.ds(pl.multiple_of(which * 384, 384), 384)
+        terms = lax.dot_general(face[at, :], matrix, NN, preferred_element_type=F32)
+        sums = [None] * 3
+        for j in range(8):
+            power, depth, scale = [terms[j * 48 + q * 16 : j * 48 + q * 16 + 16] for q in range(3)]
+            magnitude = jnp.exp2(power) * jnp.maximum(depth, 0.0) * scale
+            for c in range(3):
+                term = magnitude * mean[pl.ds(pl.multiple_of(which * 384 + j * 48 + c * 16, 16), 16), :]
+                term = term[:8] + term[8:]
+                sums[c] = term if j == 0 else sums[c] + term
+        return sums
 
     count = pair_count[0]
-    group = 4
+    group = 8
 
     def step(i, carry):
         ids = [i * group + n for n in range(group)]
@@ -322,14 +341,17 @@
         found = [pair_force(at[n], pair_face[ids[n]]) for n in range(group)]
         for n in range(group):
             keep = jnp.where(ids[n] < count, 1.0, 0.0)
-            rows = pl.ds(pl.multiple_of(at[n] * 8, 8), 8)
-            acc[rows, :] += found[n] * keep
+            for c in range(3):
+                rows = pl.ds(pl.multiple_of(at[n] * 24 + c * 8, 8), 8)
+                acc[rows, :] += found[n][c] * keep
         return carry
 
     lax.fori_loop(0, (count + group - 1) // group, step, 0)
-    total = devices * tiles
     for c in range(3):
-        out[:, c * tiles : (c + 1) * tiles, :] = acc[pl.ds(c, total, stride=8), :].reshape(devices, tiles, LANES)
+        value = acc[pl.ds(c * 8, total, stride=24), :]
+        for r in range(1, 8):
+            value = value + acc[pl.ds(c * 8 + r, total, stride=24), :]
+        out[:, c * tiles : (c + 1) * tiles, :] = value.reshape(devices, tiles, LANES)
 
 
 def final_kernel(back, slot, own, below, above, velocity, inv_mass, out, table, *, tiles):
@@ -337,10 +359,10 @@
     rows = slot.shape[0]
     for c in range(3):
         square = back[:, c * tiles : (c + 1) * tiles, :].reshape(devices * tiles, LANES).T
-        wide = jnp.concatenate([square[:LOW], square[LOW:]], axis=1)
-        high, low = split2(wide)
-        table[2 * c * LOW : (2 * c + 1) * LOW, :] = high.astype(BF16)
-        table[(2 * c + 1) * LOW : (2 * c + 2) * LOW, :] = low.astype(BF16)
+        for half, data in enumerate((square[:LOW], square[LOW:])):
+            high, low = split2(data)
+            table[half, 2 * c * LOW : (2 * c + 1) * LOW, :] = high.astype(BF16)
+            table[half, (2 * c + 1) * LOW : (2 * c + 2) * LOW, :] = low.astype(BF16)
     group_ids = iota((2 * LANES, LANES), 0).astype(F32).astype(BF16)
     low_ids = iota((LOW, LANES), 0)
     one, zero = jnp.ones((), BF16), jnp.zeros((), BF16)
@@ -352,7 +374,8 @@
         group = (((slots >> 6) & 1) * LANES + (slots >> 7)).astype(F32)
         for s in range(0, 8, 2):
             hot = [jnp.where(tiled_rows(group[i : i + 1], 2 * LANES) == group_ids, one, zero) for i in (s, s + 1)]
-            picked = lax.dot_general(table[...], jnp.concatenate(hot, axis=1), NN, preferred_element_type=F32)
+            left = jnp.concatenate([table[0], table[1]], axis=1)
+            picked = lax.dot_general(left, jnp.concatenate(hot, axis=1), NN, preferred_element_type=F32)
             for i in range(2):
                 r = k * 8 + s + i
                 mask = jnp.broadcast_to(low[s + i : s + i + 1], (LOW, LANES)) == low_ids
@@ -372,7 +395,7 @@
     out[:, last:] = out[:, last:] - inv_mass[rows - 1 : rows, :] * above[0:5, :]
 
 
-def call(kernel, outs, ins, scratch, cost, smem=0):
+def call(kernel, outs, ins, scratch, cost, smem=0, limit=12):
     vmem = pl.BlockSpec(memory_space=pltpu.VMEM)
     scalar = pl.BlockSpec(memory_space=pltpu.SMEM)
     return pl.pallas_call(
@@ -381,6 +404,7 @@
         in_specs=[scalar] * smem + [vmem] * (len(ins) - smem),
         out_specs=jax.tree.map(lambda _: vmem, outs),
         scratch_shapes=scratch,
+        compiler_params=pltpu.CompilerParams(vmem_limit_bytes=limit << 20),
         cost_estimate=pl.CostEstimate(flops=cost, bytes_accessed=cost // 100, transcendentals=0),
     )(*ins)
 
@@ -404,11 +428,12 @@
         (shape(devices, 6 * tiles, LANES), jax.ShapeDtypeStruct((rows, LANES), jnp.int32)),
         (view(contact_owner), position, velocity),
         [
-            pltpu.VMEM((12 * LOW, 8 * LANES), BF16),
-            pltpu.VMEM((2 * LANES, 8 * LANES), BF16),
+            pltpu.VMEM((8, 12 * LOW, LANES), BF16),
+            pltpu.VMEM((8, 2 * LANES, LANES), BF16),
             pltpu.VMEM((12 * LOW, 2 * LANES), F32),
         ],
         10**9,
+        limit=56,
     )
     incoming = lax.all_to_all(outgoing, axes, split_axis=0, concat_axis=0, tiled=True)
     own_faces, send_up, send_down = call(
@@ -422,33 +447,34 @@
     down = [(j, i) for i, j in up]
     before = lax.ppermute(send_up, axes, up)
     after = lax.ppermute(send_down, axes, down)
-    pitch = rows + 8
-    new_stress, own, rim_down, rim_up = call(
+    new_stress, shares, token = call(
         element_kernel,
-        (shape(*stress.shape), shape(8 * rows, LANES), shape(8, LANES), shape(8, LANES)),
+        (shape(*stress.shape), shape(23 * rows, LANES), shape(8, LANES)),
         (velocity, before, after, connectivity, shape_grad, view(area), view(thickness), view(yield_stress), stress),
-        [
-            pltpu.VMEM((5 * pitch, LANES), F32),
-            pltpu.VMEM((4 * 8 * rows, LANES), F32),
-            pltpu.VMEM((4 * rows, LANES), F32),
-            pltpu.VMEM((4 * rows, LANES), F32),
-            pltpu.VMEM((8 * (rows + 2), LANES), F32),
-        ],
-        2 * 10**9,
+        [pltpu.VMEM((5 * (rows + 8), LANES), F32)],
+        10**9,
     )
     face_rows = own_faces.shape[0] + 32
     returned = call(
         functools.partial(contact_kernel, devices=devices, tiles=tiles),
         shape(devices, 3 * tiles, LANES),
-        (pair_node, pair_face, pair_count, view(incoming), own_faces, before, after),
+        (pair_node, pair_face, pair_count, incoming, own_faces, before, after, token),
         [
             pltpu.VMEM((face_rows, LANES), F32),
-            pltpu.VMEM((face_rows * 4, 3 * LANES), BF16),
-            pltpu.VMEM((face_rows * 2, 2 * LANES), BF16),
+            pltpu.VMEM((face_rows * 48, 32), BF16),
+            pltpu.VMEM((face_rows * 48, LANES), F32),
             pltpu.VMEM((devices * tiles * 8, LANES), F32),
+            pltpu.VMEM((devices * tiles * 24, LANES), F32),
         ],
         10**9,
         smem=3,
+    )
+    own, rim_down, rim_up = call(
+        spread_kernel,
+        (shape(8 * rows, LANES), shape(8, LANES), shape(8, LANES)),
+        (shares, connectivity, returned),
+        [pltpu.VMEM((8 * (rows + 2), LANES), F32)],
+        10**9,
     )
     back = lax.all_to_all(returned, axes, split_axis=0, concat_axis=0, tiled=True)
     above = lax.ppermute(rim_down, axes, down)
@@ -457,7 +483,7 @@
         functools.partial(final_kernel, tiles=tiles),
         shape(*velocity.shape),
         (back, slot, own, below, above, velocity, view(inv_mass)),
-        [pltpu.VMEM((6 * LOW, 2 * LANES), BF16)],
+        [pltpu.VMEM((2, 6 * LOW, LANES), BF16)],
         10**9,
     )
     return (new_velocity, new_stress)

time: 88.1 us -> 65.7 us (0.75)
  Pallas kernels: 41.3 us -> 28.5 us
  starting transfers between devices: 34 us -> 24.9 us
    pallas_call x5 -> x6, Pallas kernels: 41.3 us -> 28.5 us  [call(): pl.pallas_call(kernel, out_shape=outs, in_specs=[scalar] * smem + [vmem]...]
    all_to_all x1, starting transfers between devices: 17.1 us -> 7.94 us  [body(): lax.all_to_all(returned, axes, split_axis=0, concat_axis=0, tiled=True)]
  transfers between devices with their start and end apart: 6 -> 6, of which waited for: 2 -> 2; matrix products, arithmetic and copies ran while one was open for 0% -> 0% of each run, Pallas kernels for 13% -> 14%
where the time goes in v2:
time: 65.7 us; the launch traced here: 64.9 us
  Pallas kernels  28.5 us (43%)
  starting transfers between devices  24.9 us (38%)
  waiting for transfers between devices  9.16 us (14%)
  between operations  1.56 us (2%)
  local copies, waits for them, and re-layouts  0.82 us (1%)
    pallas_call x6, Pallas kernels, call(): pl.pallas_call(kernel, out_shape=outs, in_specs=[scalar] * smem + [vmem]...  28.5 us
    all_to_all x1, starting transfers between devices, body(): lax.all_to_all(returned, axes, split_axis=0, concat_axis=0, tiled=True)  7.94 us
    all_to_all x1, starting transfers between devices, body(): lax.all_to_all(outgoing, axes, split_axis=0, concat_axis=0, tiled=True)  6.35 us
    ppermute x1, waiting for transfers between devices, body(): above = lax.ppermute(rim_down, axes, down)  4.79 us
    ppermute x1, waiting for transfers between devices, body(): after = lax.ppermute(send_down, axes, down)  4.36 us
    ppermute x1, starting transfers between devices, body(): before = lax.ppermute(send_up, axes, up)  3.37 us
    ppermute x1, starting transfers between devices, body(): below = lax.ppermute(rim_up, axes, up)  3.37 us
    ppermute x1, starting transfers between devices, body(): after = lax.ppermute(send_down, axes, down)  1.92 us
  transfers between devices with their start and end apart: 6, of which 2 were waited for; matrix products, arithmetic and copies ran while one was open for 0% of the time, Pallas kernels for 14%

profile of v2, /device:TPU:7, one launch (start us, length us, event | category | flops | bytes accessed | tf_op | source)
XLA Modules:
  0.0 64.9 jit_solution(5935024197629111450)
XLA Ops:
  0.6 0.0 copy-start.2
  0.6 0.0 copy-start.4
  0.7 0.0 copy-start.9
  0.7 0.0 copy-start.10
  0.7 0.0 copy-start.11
  0.7 0.0 copy-start
  0.7 0.0 copy-start.1
  0.7 0.0 copy-start.3
  0.7 0.0 copy-start.5
  0.7 9.5 %shard_map.176 = (f32[32,24,128]{2,1,0:T(8,128)}, s32[64,128]{1,0:T(8,128)}) custom-call(s32[64,128]{1,0:T(8,128)} %bitcast.13, f32[3,8192]{1,0:T(4,128)} %position.1, f32[5,8192]{1,0:T(8,128)} %velocity.7), custom_call_target="tpu_custom_call" | custom-call | flops 1000000000 | bytes 10000000 | tf_op jit(solution)/shard_map/pallas_call | solution.py:401
  10.2 6.3 %all-to-all-start = ((f32[32,24,128]{2,1,0:T(8,128)}), f32[32,24,128]{2,1,0:T(8,128)S(1)}, u32[]{:S(2)}, u32[]{:S(2)}) async-start(f32[32,24,128]{2,1,0:T(8,128)} %get-tuple-element.13), calls=%async_computation | async-start | bytes 786432 | tf_op jit(solution)/shard_map/all_to_all | solution.py:438
  16.7 0.7 %copy-done.14 = s32[64,128]{1,0:T(8,128)S(1)} copy-done((s32[64,128]{1,0:T(8,128)S(1)}, s32[64,128]{1,0:T(8,128)}, u32[]{:S(2)}) %copy-start.14) | copy-done | bytes 32792
  17.4 0.2 shard_map.177
  17.6 3.4 %collective-permute-start = (f32[24,128]{1,0:T(8,128)S(1)}, f32[24,128]{1,0:T(8,128)S(1)}, u32[]{:S(2)}, u32[]{:S(2)}) collective-permute-start(f32[24,128]{1,0:T(8,128)S(1)} %get-tuple-element.16), channel_id=1, source_target_pairs={{0,1},{1,2},{2,3},{3,4},{4,5},{5,6},{6,7},{7,8},{8,9},{9,10},{10,1... | collective-permute-start | bytes 36872 | tf_op jit(solution)/shard_map/ppermute | solution.py:448
  21.0 1.9 %collective-permute-start.1 = (f32[24,128]{1,0:T(8,128)S(1)}, f32[24,128]{1,0:T(8,128)S(1)}, u32[]{:S(2)}, u32[]{:S(2)}) collective-permute-start(f32[24,128]{1,0:T(8,128)S(1)} %get-tuple-element.17), channel_id=1, source_target_pairs={{1,0},{2,1},{3,2},{4,3},{5,4},{6,5},{7,6},{8,7},{9,8},{10,9},{11,1... | collective-permute-start | bytes 36872 | tf_op jit(solution)/shard_map/ppermute | solution.py:449
  23.6 0.0 collective-permute-done.before
  23.6 4.4 %collective-permute-done.1.after = f32[24,128]{1,0:T(8,128)S(1)} collective-permute-done((f32[24,128]{1,0:T(8,128)S(1)}, f32[24,128]{1,0:T(8,128)S(1)}, u32[]{:S(2)}, u32[]{:S(2)}) %collective-permute-start.1) | collective-permute-done | bytes 12320 | tf_op jit(solution)/shard_map/ppermute | solution.py:449
  28.0 0.0 copy-start.12
  28.0 0.0 copy-start.13
  28.0 3.0 %shard_map.178 = (f32[5,5,8192]{2,1,0:T(8,128)}, f32[1472,128]{1,0:T(8,128)S(1)}, f32[8,128]{1,0:T(8,128)S(1)}) custom-call(f32[5,8192]{1,0:T(8,128)S(1)} %copy-done.2, f32[24,128]{1,0:T(8,128)S(1)} %collective-permute-done.before, f32[24,128]{1,0:T(8,128)S(1)} %collective-permute-done.1.after, s32[4,8192]{1,0:T(4,128)S(1)} %copy-done.3, ...), custom_call_target="tpu_custom_call" | custom-call | flops 1000000000 | bytes 10000000 | tf_op jit(solution)/shard_map/pallas_call | solution.py:401
  31.0 0.0 all-to-all-done.nodes
  31.0 0.0 copy-done.13
  31.1 5.9 %shard_map.179.after = f32[32,12,128]{2,1,0:T(8,128)} custom-call(s32[128]{0:T(128)S(1)} %copy-done.12, s32[128]{0:T(128)S(1)} %copy-done.13, s32[1]{0:T(128)S(6)} %copy.19.pair_count, f32[32,24,128]{2,1,0:T(8,128)S(1)} %all-to-all-done.nodes, f32[128,128]{1,0:T(8,128)S(1)} %get-tuple-element.15.own, f32[24,128]{1,0:T(8,128)S(1)} %collective-permute-done.before, ...), custom_call_target="tpu_custom_call" | custom-call | flops 1000000000 | bytes 10000000 | tf_op jit(solution)/shard_map/pallas_call | solution.py:401
  36.9 7.9 %all-to-all-start.1 = ((f32[32,12,128]{2,1,0:T(8,128)}), f32[32,12,128]{2,1,0:T(8,128)S(1)}, u32[]{:S(2)}, u32[]{:S(2)}) async-start(f32[32,12,128]{2,1,0:T(8,128)} %shard_map.179.after), calls=%async_computation.1 | async-start | bytes 524288 | tf_op jit(solution)/shard_map/all_to_all | solution.py:479
  44.9 0.0 copy-start.8
  44.9 5.9 %shard_map.180 = (f32[512,128]{1,0:T(8,128)S(1)}, f32[8,128]{1,0:T(8,128)S(1)}, f32[8,128]{1,0:T(8,128)S(1)}) custom-call(f32[1472,128]{1,0:T(8,128)S(1)} %get-tuple-element.19.spread, s32[4,8192]{1,0:T(4,128)S(1)} %copy-done.3, f32[32,12,128]{2,1,0:T(8,128)} %shard_map.179.after), custom_call_target="tpu_custom_call" | custom-call | flops 1000000000 | bytes 10000000 | tf_op jit(solution)/shard_map/pallas_call | solution.py:401
  50.8 3.4 %collective-permute-start.2 = (f32[8,128]{1,0:T(8,128)S(1)}, f32[8,128]{1,0:T(8,128)S(1)}, u32[]{:S(2)}, u32[]{:S(2)}) collective-permute-start(f32[8,128]{1,0:T(8,128)S(1)} %get-tuple-element.21), channel_id=1, source_target_pairs={{0,1},{1,2},{2,3},{3,4},{4,5},{5,6},{6,7},{7,8},{8,9},{9,10},{10,1... | collective-permute-start | bytes 12296 | tf_op jit(solution)/shard_map/ppermute | solution.py:481
  54.2 1.9 %collective-permute-start.3 = (f32[8,128]{1,0:T(8,128)S(1)}, f32[8,128]{1,0:T(8,128)S(1)}, u32[]{:S(2)}, u32[]{:S(2)}) collective-permute-start(f32[8,128]{1,0:T(8,128)S(1)} %get-tuple-element.22), channel_id=1, source_target_pairs={{1,0},{2,1},{3,2},{4,3},{5,4},{6,5},{7,6},{8,7},{9,8},{10,9},{11,1... | collective-permute-start | bytes 12296 | tf_op jit(solution)/shard_map/ppermute | solution.py:480
  56.1 0.0 collective-permute-done.2.below
  56.1 4.8 %collective-permute-done.3.above = f32[8,128]{1,0:T(8,128)S(1)} collective-permute-done((f32[8,128]{1,0:T(8,128)S(1)}, f32[8,128]{1,0:T(8,128)S(1)}, u32[]{:S(2)}, u32[]{:S(2)}) %collective-permute-start.3) | collective-permute-done | bytes 4128 | tf_op jit(solution)/shard_map/ppermute | solution.py:480
  60.9 0.0 all-to-all-done.1.back
  60.9 4.0 %shard_map.181 = f32[5,8192]{1,0:T(8,128)} custom-call(f32[32,12,128]{2,1,0:T(8,128)S(1)} %all-to-all-done.1.back, s32[64,128]{1,0:T(8,128)S(1)} %copy-done.15, f32[512,128]{1,0:T(8,128)S(1)} %get-tuple-element.20.own, f32[8,128]{1,0:T(8,128)S(1)} %collective-permute-done.2.below, f32[8,128]{1,0:T(8,128)S(1)} %collective-permute-done.3.above, ...), custom_call_target="tpu_custom_call" | custom-call | flops 1000000000 | bytes 10000000 | tf_op jit(solution)/shard_map/pallas_call | solution.py:401
  (18 shorter events, 0.0 us)
Async XLA Ops:
  0.6 16.0 %copy-start.2 = (f32[5,8192]{1,0:T(8,128)S(1)}, f32[5,8192]{1,0:T(8,128)}, u32[]{:S(2)}) copy-start(f32[5,8192]{1,0:T(8,128)} %velocity.7) | copy-start | bytes 491524
  0.6 16.0 %copy-start.4 = (f32[3,2048]{1,0:T(4,128)S(1)}, f32[3,2048]{1,0:T(4,128)}, u32[]{:S(2)}) copy-start(f32[3,2048]{1,0:T(4,128)} %center.1) | copy-start | bytes 73732
  0.7 16.0 %copy-start.9 = (f32[2,2048]{1,0:T(2,128)S(1)}, f32[2,2048]{1,0:T(2,128)}, u32[]{:S(2)}) copy-start(f32[2,2048]{1,0:T(2,128)} %angle.1) | copy-start | bytes 49156
  0.7 16.0 %copy-start.10 = (f32[2048]{0:T(1024)S(1)}, f32[2048]{0:T(1024)}, u32[]{:S(2)}) copy-start(f32[2048]{0:T(1024)} %param.29) | copy-start | bytes 24580
  0.7 16.0 %copy-start.11 = (s32[512]{0:T(512)S(1)}, s32[512]{0:T(512)}, u32[]{:S(2)}) copy-start(s32[512]{0:T(512)} %param.30) | copy-start | bytes 6148
  0.7 27.3 %copy-start = (f32[5,5,8192]{2,1,0:T(8,128)S(1)}, f32[5,5,8192]{2,1,0:T(8,128)}, u32[]{:S(2)}) copy-start(f32[5,5,8192]{2,1,0:T(8,128)} %stress.1) | copy-start | bytes 2457604
  0.7 27.3 %copy-start.1 = (f32[2,4,8192]{2,1,0:T(4,128)S(1)}, f32[2,4,8192]{2,1,0:T(4,128)}, u32[]{:S(2)}) copy-start(f32[2,4,8192]{2,1,0:T(4,128)} %grads.1) | copy-start | bytes 786436
  0.7 27.3 %copy-start.3 = (s32[4,8192]{1,0:T(4,128)S(1)}, s32[4,8192]{1,0:T(4,128)}, u32[]{:S(2)}) copy-start(s32[4,8192]{1,0:T(4,128)} %connectivity.3) | copy-start | bytes 393220
  0.7 27.2 %copy-start.5 = (f32[8192]{0:T(1024)S(1)}, f32[8192]{0:T(1024)}, u32[]{:S(2)}) copy-start(f32[8192]{0:T(1024)} %param.22) | copy-start | bytes 98308
  0.7 27.2 %copy-start.6 = (f32[8192]{0:T(1024)S(1)}, f32[8192]{0:T(1024)}, u32[]{:S(2)}) copy-start(f32[8192]{0:T(1024)} %param.23) | copy-start | bytes 98308
  0.7 27.2 %copy-start.7 = (f32[8192]{0:T(1024)S(1)}, f32[8192]{0:T(1024)}, u32[]{:S(2)}) copy-start(f32[8192]{0:T(1024)} %param.24) | copy-start | bytes 98308
  10.2 20.8 %all-to-all-start = ((f32[32,24,128]{2,1,0:T(8,128)}), f32[32,24,128]{2,1,0:T(8,128)S(1)}, u32[]{:S(2)}, u32[]{:S(2)}) async-start(f32[32,24,128]{2,1,0:T(8,128)} %get-tuple-element.13), calls=%async_computation | async-start | bytes 786432 | tf_op jit(solution)/shard_map/all_to_all | solution.py:438
  16.7 0.8 %copy-start.14 = (s32[64,128]{1,0:T(8,128)S(1)}, s32[64,128]{1,0:T(8,128)}, u32[]{:S(2)}) copy-start(s32[64,128]{1,0:T(8,128)} %get-tuple-element.14.slot) | copy-start | bytes 98308
  17.6 6.0 %collective-permute-start = (f32[24,128]{1,0:T(8,128)S(1)}, f32[24,128]{1,0:T(8,128)S(1)}, u32[]{:S(2)}, u32[]{:S(2)}) collective-permute-start(f32[24,128]{1,0:T(8,128)S(1)} %get-tuple-element.16), channel_id=1, source_target_pairs={{0,1},{1,2},{2,3},{3,4},{4,5},{5,6},{6,7},{7,8},{8,9},{9,10},{10,1... | collective-permute-start | bytes 36872 | tf_op jit(solution)/shard_map/ppermute | solution.py:448
  21.0 6.9 %collective-permute-start.1 = (f32[24,128]{1,0:T(8,128)S(1)}, f32[24,128]{1,0:T(8,128)S(1)}, u32[]{:S(2)}, u32[]{:S(2)}) collective-permute-start(f32[24,128]{1,0:T(8,128)S(1)} %get-tuple-element.17), channel_id=1, source_target_pairs={{1,0},{2,1},{3,2},{4,3},{5,4},{6,5},{7,6},{8,7},{9,8},{10,9},{11,1... | collective-permute-start | bytes 36872 | tf_op jit(solution)/shard_map/ppermute | solution.py:449
  28.0 3.1 %copy-start.12 = (s32[128]{0:T(128)S(1)}, s32[128]{0:T(128)}, u32[]{:S(2)}) copy-start(s32[128]{0:T(128)} %pair_node.1) | copy-start | bytes 1540
  28.0 3.0 %copy-start.13 = (s32[128]{0:T(128)S(1)}, s32[128]{0:T(128)}, u32[]{:S(2)}) copy-start(s32[128]{0:T(128)} %pair_face.1) | copy-start | bytes 1540
  36.9 23.9 %all-to-all-start.1 = ((f32[32,12,128]{2,1,0:T(8,128)}), f32[32,12,128]{2,1,0:T(8,128)S(1)}, u32[]{:S(2)}, u32[]{:S(2)}) async-start(f32[32,12,128]{2,1,0:T(8,128)} %shard_map.179.after), calls=%async_computation.1 | async-start | bytes 524288 | tf_op jit(solution)/shard_map/all_to_all | solution.py:479
  44.9 16.0 %copy-start.8 = (f32[8192]{0:T(1024)S(1)}, f32[8192]{0:T(1024)}, u32[]{:S(2)}) copy-start(f32[8192]{0:T(1024)} %param.19) | copy-start | bytes 98308
  44.9 16.0 %copy-start.15 = (s32[64,128]{1,0:T(8,128)S(1)}, s32[64,128]{1,0:T(8,128)}, u32[]{:S(2)}) copy-start(s32[64,128]{1,0:T(8,128)} %get-tuple-element.14.slot) | copy-start | bytes 98308
  50.8 5.3 %collective-permute-start.2 = (f32[8,128]{1,0:T(8,128)S(1)}, f32[8,128]{1,0:T(8,128)S(1)}, u32[]{:S(2)}, u32[]{:S(2)}) collective-permute-start(f32[8,128]{1,0:T(8,128)S(1)} %get-tuple-element.21), channel_id=1, source_target_pairs={{0,1},{1,2},{2,3},{3,4},{4,5},{5,6},{6,7},{7,8},{8,9},{9,10},{10,1... | collective-permute-start | bytes 12296 | tf_op jit(solution)/shard_map/ppermute | solution.py:481
  54.2 6.7 %collective-permute-start.3 = (f32[8,128]{1,0:T(8,128)S(1)}, f32[8,128]{1,0:T(8,128)S(1)}, u32[]{:S(2)}, u32[]{:S(2)}) collective-permute-start(f32[8,128]{1,0:T(8,128)S(1)} %get-tuple-element.22), channel_id=1, source_target_pairs={{1,0},{2,1},{3,2},{4,3},{5,4},{6,5},{7,6},{8,7},{9,8},{10,9},{11,1... | collective-permute-start | bytes 12296 | tf_op jit(solution)/shard_map/ppermute | solution.py:480

commit v3 on v2

v3 whole, which is shorter than its diff:
```python
import functools

import jax
import jax.numpy as jnp
from jax import lax
from jax.experimental import pallas as pl
from jax.experimental.pallas import tpu as pltpu
from jax.sharding import PartitionSpec as P

LANES = 128
LOW = 64

LOBATTO_POINTS = (-1.0, -0.6546536707079771, 0.0, 0.6546536707079771, 1.0)
LOBATTO_WEIGHTS = (0.1, 49.0 / 90.0, 32.0 / 45.0, 49.0 / 90.0, 0.1)
PLANE_MODULUS = 1.0 / 0.91
POISSON = 0.3
SHEAR_MODULUS = 5.0 / 6.0 / 2.6
DAMPING = 0.3
REACH_SQ = 0.5
LOG2E = 1.4426950408889634

F32 = jnp.float32
BF16 = jnp.bfloat16
NT = (((1,), (1,)), ((), ()))
NN = (((1,), (0,)), ((), ()))


def iota(shape, dim):
    return lax.broadcasted_iota(jnp.int32, shape, dim)


def split2(x):
    high = x.astype(BF16).astype(F32)
    return high, x - high


def tiled_rows(row, count):
    packed = jnp.broadcast_to(row, (16, row.shape[1])).astype(BF16)
    return packed if count == 16 else jnp.concatenate([packed] * (count // 16), axis=0)


def arrange_kernel(owner, position, velocity, out, slot_out, acc, *, devices, capacity):
    rows = owner.shape[0]
    tiles = capacity // LANES
    upper = jnp.where(iota((LANES, 2 * LANES), 1) > iota((LANES, 2 * LANES), 0), 1.0, 0.0).astype(BF16)
    device_ids = iota((devices, LANES), 0)
    low_ids = iota((LOW, LANES), 0).astype(F32).astype(BF16)
    group_ids = iota((2 * LANES, LANES), 0).astype(F32).astype(BF16)
    acc[...] = jnp.zeros_like(acc)
    one, zero = jnp.ones((), BF16), jnp.zeros((), BF16)

    def step(k, base):
        owners = owner[pl.ds(pl.multiple_of(k * 8, 8), 8), :]
        masks = [jnp.broadcast_to(owners[s : s + 1], (devices, LANES)) == device_ids for s in range(8)]
        hot = jnp.concatenate([jnp.where(m, 1.0, 0.0).astype(BF16) for m in masks], axis=0)
        counted = lax.dot_general(hot, upper, NN, preferred_element_type=F32)
        ranks = []
        for s in range(8):
            part = counted[s * devices : (s + 1) * devices]
            ranks.append(jnp.sum(jnp.where(masks[s], part[:, :LANES] + base, 0.0), axis=0, keepdims=True))
            base = base + part[:, LANES:]
        rank = jnp.concatenate(ranks, axis=0).astype(jnp.int32)
        slot = owners * capacity + rank
        slot_out[pl.ds(pl.multiple_of(k * 8, 8), 8), :] = slot
        low = (slot & (LOW - 1)).astype(F32)
        group = (((slot >> 6) & 1) * LANES + (slot >> 7)).astype(F32)
        for first in range(0, 8, 2):
            left, right = [], []
            for s in range(first, first + 2):
                lanes = pl.ds(pl.multiple_of(k * 8 * LANES + s * LANES, LANES), LANES)
                hot_low = jnp.where(tiled_rows(low[s : s + 1], LOW) == low_ids, one, zero)
                right.append(jnp.where(tiled_rows(group[s : s + 1], 2 * LANES) == group_ids, one, zero))
                place = position[:, lanes]
                place = place + jnp.where(iota(place.shape, 0) == 0, 1.0, 0.0)
                column = []
                for data in (place, velocity[0:3, lanes]):
                    parts = split2(data)
                    for c in range(3):
                        for half in range(2):
                            column.append(hot_low * tiled_rows(parts[half][c : c + 1], LOW))
                left.append(jnp.concatenate(column, axis=0))
            acc[...] += lax.dot_general(
                jnp.concatenate(left, axis=1), jnp.concatenate(right, axis=1), NT, preferred_element_type=F32
            )
        return base

    lax.fori_loop(0, rows // 8, step, jnp.zeros((devices, LANES), F32))
    for c in range(6):
        both = acc[2 * c * LOW : (2 * c + 1) * LOW, :] + acc[(2 * c + 1) * LOW : (2 * c + 2) * LOW, :]
        square = jnp.concatenate([both[:, :LANES], both[:, LANES:]], axis=0).T
        out[:, c * tiles : (c + 1) * tiles, :] = square.reshape(devices, tiles, LANES)


FACE_ROWS = 16
PACKET = 72


def packet_kernel(
    center, angle, stiffness, ghost, velocity, stress, grads, connectivity, area, thickness, yields, slot,
    own, up, down, edge_velocity, edge_stress, edge_grads, edge_nodes, edge_scalars, arrived,
):
    del slot
    nodes = velocity.shape[1]
    rows = nodes // LANES
    copies = []
    for side in range(2):
        wide = pl.ds(0, 2 * LANES) if side else pl.ds(nodes - 2 * LANES, 2 * LANES)
        last = pl.ds(0, LANES) if side else pl.ds(nodes - LANES, LANES)
        row = pl.ds(0, 1) if side else pl.ds(rows - 1, 1)
        pairs = [
            (velocity.at[:, wide], edge_velocity.at[side]),
            (stress.at[:, :, last], edge_stress.at[side]),
            (grads.at[:, :, last], edge_grads.at[side]),
            (connectivity.at[:, last], edge_nodes.at[side]),
            (area.at[row], edge_scalars.at[side, 0]),
            (thickness.at[row], edge_scalars.at[side, 1]),
            (yields.at[row], edge_scalars.at[side, 2]),
        ]
        for n, (source, target) in enumerate(pairs):
            copies.append(pltpu.make_async_copy(source, target, arrived.at[side * len(pairs) + n]))
    for copy in copies:
        copy.start()
    count = stiffness.shape[0]
    azimuth = angle[0, :].reshape(count, LANES)
    elevation = angle[1, :].reshape(count, LANES)
    flat = jnp.cos(elevation)
    data = [center[c, :].reshape(count, LANES) for c in range(3)]
    data += [jnp.cos(azimuth) * flat, jnp.sin(azimuth) * flat, jnp.sin(elevation), stiffness[...]]
    wanted = ghost[...]
    wanted = jnp.concatenate([wanted, wanted], axis=0)
    row_of, lane_of = wanted >> 7, wanted & (LANES - 1)
    up[...] = jnp.zeros_like(up)
    down[...] = jnp.zeros_like(down)
    own[pl.ds(7, count, stride=8), :] = jnp.zeros((count, LANES), F32)
    for c in range(7):
        own[pl.ds(c, count, stride=8), :] = data[c]
        found = jnp.zeros((8, LANES), F32)
        for r in range(count):
            source = jnp.broadcast_to(data[c][r : r + 1], (8, LANES))
            found = jnp.where(row_of == r, jnp.take_along_axis(source, lane_of, axis=1), found)
        for t in range(2):
            down[8 * t + c : 8 * t + c + 1, :] = found[t : t + 1]
            up[8 * t + c : 8 * t + c + 1, :] = found[2 + t : 3 + t]
    for copy in copies:
        copy.wait()
    for side, out in ((0, up), (1, down)):
        at = FACE_ROWS
        out[at : at + 5, :] = edge_velocity[side, :, :LANES]
        out[at + 5 : at + 10, :] = edge_velocity[side, :, LANES:]
        at += 10
        for layer in range(5):
            out[at : at + 5, :] = edge_stress[side, layer]
            at += 5
        for g in range(2):
            out[at : at + 4, :] = edge_grads[side, g]
            at += 4
        out[at : at + 4, :] = edge_nodes[side].astype(F32)
        at += 4
        for n in range(3):
            out[at + n : at + n + 1, :] = edge_scalars[side, n]


def element_pack(sources, places, gx, gy, thick, limit, area, old_stress):
    corner = []
    for lane, rel in places:
        second, third = rel == 1, rel == 2
        values = []
        for c in range(5):
            g = [jnp.take_along_axis(sources[c][j], lane, axis=1) for j in range(3)]
            values.append(jnp.where(third, g[2], jnp.where(second, g[1], g[0])))
        corner.append(values)

    def total(f):
        t = [f(a) for a in range(4)]
        return (t[0] + t[1]) + (t[2] + t[3])

    memb_xx = total(lambda a: gx[a] * corner[a][0])
    bend_xx = total(lambda a: gx[a] * corner[a][4])
    memb_yy = total(lambda a: gy[a] * corner[a][1])
    bend_yy = -total(lambda a: gy[a] * corner[a][3])
    memb_xy = total(lambda a: gy[a] * corner[a][0] + gx[a] * corner[a][1])
    bend_xy = total(lambda a: gy[a] * corner[a][4] - gx[a] * corner[a][3])
    shear_xz = total(lambda a: gx[a] * corner[a][2]) + 0.25 * total(lambda a: corner[a][4])
    shear_yz = total(lambda a: gy[a] * corner[a][2]) - 0.25 * total(lambda a: corner[a][3])
    half_area = 0.5 * thick * area
    force = [None] * 5
    moment = [None] * 3
    stresses = []
    for layer in range(5):
        height = (0.5 * LOBATTO_POINTS[layer]) * thick
        xx = memb_xx + height * bend_xx
        yy = memb_yy + height * bend_yy
        xy = memb_xy + height * bend_xy
        old = old_stress(layer)
        t = [
            old[0] + PLANE_MODULUS * (xx + POISSON * yy),
            old[1] + PLANE_MODULUS * (yy + POISSON * xx),
            old[2] + (PLANE_MODULUS * 0.5 * (1.0 - POISSON)) * xy,
            old[3] + SHEAR_MODULUS * shear_xz,
            old[4] + SHEAR_MODULUS * shear_yz,
        ]
        plus, minus = t[0] + t[1], t[0] - t[1]
        mises = jnp.sqrt(
            0.25 * (plus * plus) + 0.75 * (minus * minus) + 3.0 * (t[2] * t[2] + t[3] * t[3] + t[4] * t[4])
        )
        factor = limit / jnp.maximum(mises, limit)
        weight = LOBATTO_WEIGHTS[layer] * half_area
        lever = weight * height
        values = [t[c] * factor for c in range(5)]
        stresses.append(values)
        for c in range(5):
            term = weight * values[c]
            force[c] = term if layer == 0 else force[c] + term
            if c < 3 and layer != 2:
                term = lever * values[c]
                moment[c] = term if layer == 0 else moment[c] + term
    forces = [
        (
            gx[a] * force[0] + gy[a] * force[2],
            gy[a] * force[1] + gx[a] * force[2],
            gx[a] * force[3] + gy[a] * force[4],
            -(gy[a] * moment[1] + gx[a] * moment[2]) - 0.25 * force[4],
            gx[a] * moment[0] + gy[a] * moment[2] + 0.25 * force[3],
        )
        for a in range(4)
    ]
    return forces, stresses


def spread_row(spread, pitch, row, lanes, rels, wanted):
    one, zero = jnp.ones((), BF16), jnp.zeros((), BF16)
    lane_ids = iota((LANES, LANES), 0).astype(F32).astype(BF16)
    left, right = [], []
    for a in range(4):
        data = spread[pl.ds(a * 5 * pitch + row, 8, stride=pitch), :]
        high, low = split2(data)
        both = jnp.concatenate([high, low], axis=0).astype(BF16)
        rel = tiled_rows(rels[a : a + 1], 16)
        left.append(jnp.concatenate([jnp.where(rel == jnp.asarray(j, BF16), both, zero) for j in wanted], axis=0))
        lane = tiled_rows(lanes[a : a + 1], LANES)
        right.append(jnp.where(lane == lane_ids, one, zero))
    out = lax.dot_general(
        jnp.concatenate(left, axis=1), jnp.concatenate(right, axis=1), NT, preferred_element_type=F32
    )
    return [out[16 * j : 16 * j + 8] + out[16 * j + 8 : 16 * j + 16] for j in range(len(wanted))]


def element_kernel(
    velocity, before, after, connectivity, grads, area, thickness, yields, stress, returned,
    new_stress, own, ext, spread, acc,
):
    del returned
    nodes = velocity.shape[1]
    rows = nodes // LANES
    pitch = rows + 8
    chunk = 8 * LANES
    for c in range(5):
        at = FACE_ROWS + c
        ext[c * pitch : c * pitch + 1, :] = before[at : at + 1, :]
        ext[c * pitch + 1 : c * pitch + 2, :] = before[at + 5 : at + 6, :]
        for k in range(rows // 8):
            ext[c * pitch + 2 + 8 * k : c * pitch + 10 + 8 * k, :] = velocity[c, pl.ds(k * chunk, chunk)].reshape(8, LANES)
        ext[c * pitch + rows + 2 : c * pitch + rows + 3, :] = after[at : at + 1, :]
        ext[c * pitch + rows + 3 : c * pitch + rows + 4, :] = after[at + 5 : at + 6, :]
    spread[20 * pitch :, :] = jnp.zeros((3 * pitch, LANES), F32)

    def elements(k, carry):
        here = pl.ds(pl.multiple_of(k * chunk, chunk), chunk)
        first = pl.multiple_of(k * 8, 8)
        packed = pl.ds(first, 8)
        sources = [[ext[pl.ds(c * pitch + k * 8 + j + 1, 8), :] for j in range(3)] for c in range(5)]
        row_ids = iota((8, LANES), 0) + k * 8
        places = []
        for a in range(4):
            index = connectivity[a, here].reshape(8, LANES)
            places.append((index & (LANES - 1), (index >> 7) - row_ids))
        gx = [grads[0, a, here].reshape(8, LANES) for a in range(4)]
        gy = [grads[1, a, here].reshape(8, LANES) for a in range(4)]
        forces, stresses = element_pack(
            sources, places, gx, gy, thickness[packed, :], yields[packed, :], area[packed, :],
            lambda layer: [stress[layer, c, here].reshape(8, LANES) for c in range(5)],
        )
        for layer in range(5):
            for c in range(5):
                new_stress[layer, c, here] = stresses[layer][c].reshape(chunk)
        for a in range(4):
            for c in range(5):
                spread[pl.ds((a * 5 + c) * pitch + first, 8), :] = forces[a][c]
        return carry

    lax.fori_loop(0, rows // 8, elements, 0)
    blank = jnp.zeros((6, LANES), F32)

    def edge(n):
        at = FACE_ROWS + 10 + n
        return jnp.concatenate([before[at : at + 1, :], after[at : at + 1, :], blank], axis=0)

    sub = iota((8, LANES), 0)
    sources = [
        [
            jnp.concatenate(
                [ext[c * pitch + j : c * pitch + j + 1, :], ext[c * pitch + rows + 1 + j : c * pitch + rows + 2 + j, :], blank],
                axis=0,
            )
            for j in range(3)
        ]
        for c in range(5)
    ]
    places = []
    for a in range(4):
        index = edge(33 + a).astype(jnp.int32) + jnp.where(sub == 0, -nodes, nodes)
        places.append((index & (LANES - 1), jnp.where(sub == 0, (index >> 7) + 1, (index >> 7) - rows)))
    limit = edge(39)
    forces, _ = element_pack(
        sources, places, [edge(25 + a) for a in range(4)], [edge(29 + a) for a in range(4)],
        edge(38), jnp.where(limit > 0.0, limit, 1.0), edge(37),
        lambda layer: [edge(layer * 5 + c) for c in range(5)],
    )
    for a in range(4):
        for c in range(5):
            at = (a * 5 + c) * pitch + rows
            spread[at : at + 8, :] = forces[a][c]

    acc[...] = jnp.zeros_like(acc)

    def scatter(step, carry):
        b = step * 4
        parts = []
        for i in range(4):
            index = connectivity[:, pl.ds(pl.multiple_of((b + i) * LANES, LANES), LANES)]
            lanes = (index & (LANES - 1)).astype(F32)
            rels = ((index >> 7) - (b + i)).astype(F32)
            parts.append(spread_row(spread, pitch, b + i, lanes, rels, (0, 1, 2)))
        total = {}
        for i in range(4):
            for j in range(3):
                total[i + j] = parts[i][j] if i + j not in total else total[i + j] + parts[i][j]
        for n in range(6):
            at = pl.ds(pl.multiple_of((b + n) * 8, 8), 8)
            if n < 2:
                acc[at, :] += total[n]
            else:
                acc[at, :] = total[n]
        return carry

    lax.fori_loop(0, rows // 4, scatter, 0)
    for side, row, j in ((0, 1, 2), (1, rows, 0)):
        lanes = jnp.concatenate([place[0][side : side + 1] for place in places], axis=0).astype(F32)
        rels = jnp.concatenate([place[1][side : side + 1] for place in places], axis=0).astype(F32)
        acc[8 * row : 8 * row + 8, :] += spread_row(spread, pitch, rows + side, lanes, rels, (j,))[0]
    own[...] = acc[8 : 8 + 8 * rows, :]


def contact_kernel(
    pair_node, pair_face, pair_count, nodes, own, before, after, out, raw, face, mean, table, acc, *, devices, tiles
):
    own_rows = own.shape[0]
    face_tiles = (own_rows + 32) // 8
    raw[0:16, :] = before[0:FACE_ROWS, :]
    raw[16 : 16 + own_rows, :] = own[...]
    raw[16 + own_rows :, :] = after[0:FACE_ROWS, :]
    sub = iota((8, LANES), 0)

    def prepare(f):
        data = raw[pl.ds(pl.multiple_of(f * 8, 8), 8), :]
        centre = data - 0.5
        normal = [jnp.broadcast_to(data[3 + c : 4 + c], (8, LANES)) for c in range(3)]
        place = [jnp.broadcast_to(centre[c : c + 1], (8, LANES)) for c in range(3)]
        stiff = jnp.broadcast_to(data[6:7], (8, LANES))
        m_low = jnp.where(sub == 0, normal[0], jnp.where(sub == 1, normal[1], jnp.where(sub == 2, normal[2], 0.0)))
        coef_e = jnp.where(sub < 3, (2.0 / REACH_SQ * LOG2E) * centre, jnp.where(sub == 6, 1.0, 0.0))
        coef_d = -m_low
        inside = (sub >= 3) & (sub < 6)
        coef_a = jnp.where(inside, (-DAMPING) * stiff * data, jnp.where(sub == 7, stiff, 0.0))
        square = place[0] * place[0] + place[1] * place[1] + place[2] * place[2]
        along = normal[0] * place[0] + normal[1] * place[1] + normal[2] * place[2]
        for q, (coef, const) in enumerate(((coef_e, (-LOG2E / REACH_SQ) * square), (coef_d, along), (coef_a, None))):
            high, low = split2(coef)
            if const is None:
                last = jnp.where(inside, data, 0.0)
            else:
                c_high, c_low = split2(const)
                last = jnp.where(sub == 0, c_high, jnp.where(sub == 1, c_low, 0.0))
            turned = jnp.concatenate([high, high, low, last], axis=0).T
            packed = turned.astype(BF16)
            for j in range(8):
                at = f * 384 + j * 48
                face[pl.ds(pl.multiple_of(at + q * 16, 16), 16), :] = packed[j * 16 : j * 16 + 16]
                if const is None:
                    for c in range(3):
                        column = turned[j * 16 : j * 16 + 16, 27 + c : 28 + c]
                        mean[pl.ds(pl.multiple_of(at + c * 16, 16), 16), :] = jnp.broadcast_to(column, (16, LANES))

    def prepare_group(i, carry):
        for n in range(4):
            prepare(i * 4 + n)
        return carry

    lax.fori_loop(0, face_tiles // 4, prepare_group, 0)
    total = devices * tiles
    acc[...] = jnp.zeros_like(acc)
    for c in range(6):
        flat = nodes[:, c * tiles : (c + 1) * tiles, :].reshape(total, LANES)
        if c == 0:
            table[pl.ds(7, total, stride=8), :] = jnp.where(flat > 0.5, 1.0, 0.0)
        flat = flat - (1.5, 0.5, 0.5)[c] if c < 3 else flat
        if c < 3:
            square = flat * flat if c == 0 else square + flat * flat
        table[pl.ds(c, total, stride=8), :] = flat
    table[pl.ds(6, total, stride=8), :] = (-LOG2E / REACH_SQ) * square
    ones = jnp.where(sub < 2, 1.0, 0.0)

    def pair_force(node, which):
        high, low = split2(table[pl.ds(pl.multiple_of(node * 8, 8), 8), :])
        matrix = jnp.concatenate([high, low, high, ones], axis=0).astype(BF16)
        at = pl.ds(pl.multiple_of(which * 384, 384), 384)
        terms = lax.dot_general(face[at, :], matrix, NN, preferred_element_type=F32)
        sums = [None] * 3
        for j in range(8):
            power, depth, scale = [terms[j * 48 + q * 16 : j * 48 + q * 16 + 16] for q in range(3)]
            magnitude = jnp.exp2(power) * jnp.maximum(depth, 0.0) * scale
            for c in range(3):
                term = magnitude * mean[pl.ds(pl.multiple_of(which * 384 + j * 48 + c * 16, 16), 16), :]
                term = term[:8] + term[8:]
                sums[c] = term if j == 0 else sums[c] + term
        return sums

    count = pair_count[0]
    group = 8

    def step(i, carry):
        ids = [i * group + n for n in range(group)]
        at = [pair_node[q] for q in ids]
        found = [pair_force(at[n], pair_face[ids[n]]) for n in range(group)]
        for n in range(group):
            keep = jnp.where(ids[n] < count, 1.0, 0.0)
            for c in range(3):
                rows = pl.ds(pl.multiple_of(at[n] * 24 + c * 8, 8), 8)
                acc[rows, :] += found[n][c] * keep
        return carry

    lax.fori_loop(0, (count + group - 1) // group, step, 0)
    for c in range(3):
        value = acc[pl.ds(c * 8, total, stride=24), :]
        for r in range(1, 8):
            value = value + acc[pl.ds(c * 8 + r, total, stride=24), :]
        out[:, c * tiles : (c + 1) * tiles, :] = value.reshape(devices, tiles, LANES)


def final_kernel(back, slot, own, velocity, inv_mass, out, table, *, tiles):
    devices = back.shape[0]
    rows = slot.shape[0]
    for c in range(3):
        square = back[:, c * tiles : (c + 1) * tiles, :].reshape(devices * tiles, LANES).T
        for half, data in enumerate((square[:LOW], square[LOW:])):
            high, low = split2(data)
            table[half, 2 * c * LOW : (2 * c + 1) * LOW, :] = high.astype(BF16)
            table[half, (2 * c + 1) * LOW : (2 * c + 2) * LOW, :] = low.astype(BF16)
    group_ids = iota((2 * LANES, LANES), 0).astype(F32).astype(BF16)
    low_ids = iota((LOW, LANES), 0)
    one, zero = jnp.ones((), BF16), jnp.zeros((), BF16)
    sub = iota((8, LANES), 0)

    def step(k, carry):
        slots = slot[pl.ds(pl.multiple_of(k * 8, 8), 8), :]
        low = slots & (LOW - 1)
        group = (((slots >> 6) & 1) * LANES + (slots >> 7)).astype(F32)
        for s in range(0, 8, 2):
            hot = [jnp.where(tiled_rows(group[i : i + 1], 2 * LANES) == group_ids, one, zero) for i in (s, s + 1)]
            left = jnp.concatenate([table[0], table[1]], axis=1)
            picked = lax.dot_general(left, jnp.concatenate(hot, axis=1), NN, preferred_element_type=F32)
            for i in range(2):
                r = k * 8 + s + i
                mask = jnp.broadcast_to(low[s + i : s + i + 1], (LOW, LANES)) == low_ids
                contact = jnp.zeros((8, LANES), F32)
                for c in range(3):
                    part = picked[2 * c * LOW : (2 * c + 2) * LOW, i * LANES : (i + 1) * LANES]
                    value = jnp.sum(jnp.where(mask, part[:LOW] + part[LOW:], 0.0), axis=0, keepdims=True)
                    contact = jnp.where(sub == c, value, contact)
                lanes = pl.ds(pl.multiple_of(r * LANES, LANES), LANES)
                total = contact - own[pl.ds(pl.multiple_of(r * 8, 8), 8), :]
                out[:, lanes] = velocity[:, lanes] + inv_mass[pl.ds(r, 1), :] * total[0:5]
        return carry

    lax.fori_loop(0, rows // 8, step, 0)


def call(kernel, outs, ins, scratch, cost, smem=0, limit=12, away=()):
    vmem = pl.BlockSpec(memory_space=pltpu.VMEM)
    scalar = pl.BlockSpec(memory_space=pltpu.SMEM)
    return pl.pallas_call(
        kernel,
        out_shape=outs,
        in_specs=[scalar if n < smem else pl.BlockSpec(memory_space=pl.ANY) if n in away else vmem for n in range(len(ins))],
        out_specs=jax.tree.map(lambda _: vmem, outs),
        scratch_shapes=scratch,
        compiler_params=pltpu.CompilerParams(vmem_limit_bytes=limit << 20),
        cost_estimate=pl.CostEstimate(flops=cost, bytes_accessed=cost // 100, transcendentals=0),
    )(*ins)


def body(
    velocity, position, inv_mass, connectivity, shape_grad, area, thickness, yield_stress, stress,
    contact_owner, face_center, face_angle, face_stiffness, ghost_list, pair_node, pair_face, pair_count,
):
    axes = ("dom", "sub")
    devices = lax.axis_size("dom") * lax.axis_size("sub")
    nodes = velocity.shape[1]
    faces = face_center.shape[1]
    rows = nodes // LANES
    capacity = 2 * nodes // devices
    tiles = capacity // LANES
    shape = lambda *s: jax.ShapeDtypeStruct(s, F32)
    view = lambda x: x.reshape(-1, LANES)

    outgoing, slot = call(
        functools.partial(arrange_kernel, devices=devices, capacity=capacity),
        (shape(devices, 6 * tiles, LANES), jax.ShapeDtypeStruct((rows, LANES), jnp.int32)),
        (view(contact_owner), position, velocity),
        [
            pltpu.VMEM((12 * LOW, 2 * LANES), F32),
        ],
        10**9,
        limit=56,
    )
    incoming = lax.all_to_all(outgoing, axes, split_axis=0, concat_axis=0, tiled=True)
    own_faces, send_up, send_down = call(
        packet_kernel,
        (shape(faces // LANES * 8, LANES), shape(PACKET, LANES), shape(PACKET, LANES)),
        (
            face_center, face_angle, view(face_stiffness), view(ghost_list), velocity, stress, shape_grad,
            connectivity, view(area), view(thickness), view(yield_stress), slot,
        ),
        [
            pltpu.VMEM((2, 5, 2 * LANES), F32),
            pltpu.VMEM((2, 5, 5, LANES), F32),
            pltpu.VMEM((2, 2, 4, LANES), F32),
            pltpu.VMEM((2, 4, LANES), jnp.int32),
            pltpu.VMEM((2, 3, 1, LANES), F32),
            pltpu.SemaphoreType.DMA((14,)),
        ],
        10**8,
        away=range(4, 12),
    )
    up = [(i, i + 1) for i in range(devices - 1)]
    down = [(j, i) for i, j in up]
    before = lax.ppermute(send_up, axes, up)
    after = lax.ppermute(send_down, axes, down)
    face_rows = own_faces.shape[0] + 32
    returned = call(
        functools.partial(contact_kernel, devices=devices, tiles=tiles),
        shape(devices, 3 * tiles, LANES),
        (pair_node, pair_face, pair_count, incoming, own_faces, before, after),
        [
            pltpu.VMEM((face_rows, LANES), F32),
            pltpu.VMEM((face_rows * 48, 32), BF16),
            pltpu.VMEM((face_rows * 48, LANES), F32),
            pltpu.VMEM((devices * tiles * 8, LANES), F32),
            pltpu.VMEM((devices * tiles * 24, LANES), F32),
        ],
        10**9,
        smem=3,
    )
    back = lax.all_to_all(returned, axes, split_axis=0, concat_axis=0, tiled=True)
    new_stress, own = call(
        element_kernel,
        (shape(*stress.shape), shape(8 * rows, LANES)),
        (
            velocity, before, after, connectivity, shape_grad, view(area), view(thickness), view(yield_stress),
            stress, returned,
        ),
        [
            pltpu.VMEM((5 * (rows + 8), LANES), F32),
            pltpu.VMEM((23 * (rows + 8), LANES), F32),
            pltpu.VMEM((8 * (rows + 2), LANES), F32),
        ],
        10**9,
        away=(9,),
    )
    new_velocity = call(
        functools.partial(final_kernel, tiles=tiles),
        shape(*velocity.shape),
        (back, slot, own, velocity, view(inv_mass)),
        [pltpu.VMEM((2, 6 * LOW, LANES), BF16)],
        10**9,
    )
    return (new_velocity, new_stress)


def solution(mesh):
    split = ("dom", "sub")
    in_specs = (
        P(None, split), P(None, split), P(split), P(None, split), P(None, None, split),
        P(split), P(split), P(split), P(None, None, split), P(split, None),
        P(None, split), P(None, split), P(split), P(split), P(split), P(split), P(split),
    )
    out_specs = (P(None, split), P(None, None, split))
    return jax.shard_map(body, mesh=mesh, in_specs=in_specs, out_specs=out_specs, check_vma=False)
```

time: 65.7 us -> 58.1 us (0.88)
  the two profiles are of different devices: /device:TPU:7 before, /device:TPU:0 now
where the time goes in v3:
time: 58.1 us; the launch traced here: 58 us
  Pallas kernels  31.2 us (54%)
  starting transfers between devices  13.9 us (24%)
  waiting for transfers between devices  10.6 us (18%)
  between operations  1.53 us (3%)
  local copies, waits for them, and re-layouts  0.82 us (1%)
    pallas_call x5, Pallas kernels, call(): pl.pallas_call(kernel, out_shape=outs, in_specs=[scalar if n < smem else...  31.2 us
    all_to_all x1, starting transfers between devices, body(): lax.all_to_all(outgoing, axes, split_axis=0, concat_axis=0, tiled=True)  7.31 us
    all_to_all x1, waiting for transfers between devices, body(): lax.all_to_all(outgoing, axes, split_axis=0, concat_axis=0, tiled=True)  5.56 us
    all_to_all x1, starting transfers between devices, body(): lax.all_to_all(returned, axes, split_axis=0, concat_axis=0, tiled=True)  3.09 us
    all_to_all x1, waiting for transfers between devices, body(): lax.all_to_all(returned, axes, split_axis=0, concat_axis=0, tiled=True)  2.77 us
    ppermute x1, waiting for transfers between devices, body(): after = lax.ppermute(send_down, axes, down)  2.29 us
    ppermute x1, starting transfers between devices, body(): before = lax.ppermute(send_up, axes, up)  2.16 us
    ppermute x1, starting transfers between devices, body(): after = lax.ppermute(send_down, axes, down)  1.29 us
  transfers between devices with their start and end apart: 4, of which 3 were waited for; matrix products, arithmetic and copies ran while one was open for 0% of the time, Pallas kernels for 14%

profile of v3, /device:TPU:0, one launch (start us, length us, event | category | flops | bytes accessed | tf_op | source)
XLA Modules:
  0.0 58.0 jit_solution(6669868620819962546)
XLA Ops:
  0.6 0.0 copy-start
  0.6 0.0 copy-start.1
  0.7 0.0 copy-start.2
  0.7 0.0 copy-start.3
  0.7 0.0 copy-start.4
  0.7 0.0 copy-start.5
  0.7 0.0 copy-start.6
  0.7 0.0 copy-start.7
  0.7 0.0 copy-start.10
  0.7 0.0 copy-start.11
  0.7 0.0 copy-start.12
  0.7 8.8 %shard_map.176 = (f32[32,24,128]{2,1,0:T(8,128)}, s32[64,128]{1,0:T(8,128)}) custom-call(s32[64,128]{1,0:T(8,128)} %bitcast.16, f32[3,8192]{1,0:T(4,128)} %position.1, f32[5,8192]{1,0:T(8,128)} %velocity.7), custom_call_target="tpu_custom_call" | custom-call | flops 1000000000 | bytes 10000000 | tf_op jit(solution)/shard_map/pallas_call | solution.py:491
  9.5 7.3 %all-to-all-start = ((f32[32,24,128]{2,1,0:T(8,128)}), f32[32,24,128]{2,1,0:T(8,128)S(1)}, u32[]{:S(2)}, u32[]{:S(2)}) async-start(f32[32,24,128]{2,1,0:T(8,128)} %get-tuple-element.9), calls=%async_computation | async-start | bytes 786432 | tf_op jit(solution)/shard_map/all_to_all | solution.py:526
  16.9 0.0 copy-done
  16.9 0.0 copy-done.1
  16.9 0.0 copy-done.2
  16.9 0.0 copy-done.3
  16.9 0.0 copy-done.4
  17.0 0.7 %copy-done.8 = s32[64,128]{1,0:T(8,128)S(1)} copy-done((s32[64,128]{1,0:T(8,128)S(1)}, s32[64,128]{1,0:T(8,128)}, u32[]{:S(2)}) %copy-start.8) | copy-done | bytes 32792
  17.7 0.4 shard_map.177
  18.1 2.2 %collective-permute-start = (f32[72,128]{1,0:T(8,128)S(1)}, f32[72,128]{1,0:T(8,128)S(1)}, u32[]{:S(2)}, u32[]{:S(2)}) collective-permute-start(f32[72,128]{1,0:T(8,128)S(1)} %get-tuple-element.12), channel_id=1, source_target_pairs={{0,1},{1,2},{2,3},{3,4},{4,5},{5,6},{6,7},{7,8},{8,9},{9,10},{10,1... | collective-permute-start | bytes 110600 | tf_op jit(solution)/shard_map/ppermute | solution.py:547
  20.3 1.3 %collective-permute-start.1 = (f32[72,128]{1,0:T(8,128)S(1)}, f32[72,128]{1,0:T(8,128)S(1)}, u32[]{:S(2)}, u32[]{:S(2)}) collective-permute-start(f32[72,128]{1,0:T(8,128)S(1)} %get-tuple-element.13), channel_id=1, source_target_pairs={{1,0},{2,1},{3,2},{4,3},{5,4},{6,5},{7,6},{8,7},{9,8},{10,9},{11,1... | collective-permute-start | bytes 110600 | tf_op jit(solution)/shard_map/ppermute | solution.py:548
  22.3 0.0 collective-permute-done.before
  22.3 2.3 %collective-permute-done.1.after = f32[72,128]{1,0:T(8,128)S(1)} collective-permute-done((f32[72,128]{1,0:T(8,128)S(1)}, f32[72,128]{1,0:T(8,128)S(1)}, u32[]{:S(2)}, u32[]{:S(2)}) %collective-permute-start.1) | collective-permute-done | bytes 36896 | tf_op jit(solution)/shard_map/ppermute | solution.py:548
  24.5 5.6 %all-to-all-done.nodes = f32[32,24,128]{2,1,0:T(8,128)S(1)} async-done(((f32[32,24,128]{2,1,0:T(8,128)}), f32[32,24,128]{2,1,0:T(8,128)S(1)}, u32[]{:S(2)}, u32[]{:S(2)}) %all-to-all-start) | async-done | bytes 393248 | tf_op jit(solution)/shard_map/all_to_all | solution.py:526
  30.1 0.0 copy-done.14
  30.1 10.2 %shard_map.178.returned = f32[32,12,128]{2,1,0:T(8,128)} custom-call(s32[128]{0:T(128)S(1)} %copy-done.14, s32[128]{0:T(128)S(1)} %copy-done.15, s32[1]{0:T(128)S(6)} %copy.19.pair_count, f32[32,24,128]{2,1,0:T(8,128)S(1)} %all-to-all-done.nodes, f32[128,128]{1,0:T(8,128)S(1)} %get-tuple-element.11.own, f32[72,128]{1,0:T(8,128)S(1)} %collective-permute-done.before, ...), custom_call_target="tpu_custom_call" | custom-call | flops 1000000000 | bytes 10000000 | tf_op jit(solution)/shard_map/pallas_call | solution.py:491
  40.3 3.1 %all-to-all-start.1 = ((f32[32,12,128]{2,1,0:T(8,128)}), f32[32,12,128]{2,1,0:T(8,128)S(1)}, u32[]{:S(2)}, u32[]{:S(2)}) async-start(f32[32,12,128]{2,1,0:T(8,128)} %shard_map.178.returned), calls=%async_computation.1 | async-start | bytes 524288 | tf_op jit(solution)/shard_map/all_to_all | solution.py:564
  43.4 0.0 copy-start.13
  43.5 7.8 %shard_map.179 = (f32[5,5,8192]{2,1,0:T(8,128)}, f32[512,128]{1,0:T(8,128)S(1)}) custom-call(f32[5,8192]{1,0:T(8,128)S(1)} %copy-done.2, f32[72,128]{1,0:T(8,128)S(1)} %collective-permute-done.before, f32[72,128]{1,0:T(8,128)S(1)} %collective-permute-done.1.after, s32[4,8192]{1,0:T(4,128)S(1)} %copy-done.3, f32[2,4,8192]{2,1,0:T(4,128)S(1)} %copy-done.1, ...), custom_call_target="tpu_custom_call" | custom-call | flops 1000000000 | bytes 10000000 | tf_op jit(solution)/shard_map/pallas_call | solution.py:491
  51.2 2.8 %all-to-all-done.1.back = f32[32,12,128]{2,1,0:T(8,128)S(1)} async-done(((f32[32,12,128]{2,1,0:T(8,128)}), f32[32,12,128]{2,1,0:T(8,128)S(1)}, u32[]{:S(2)}, u32[]{:S(2)}) %all-to-all-start.1) | async-done | bytes 196640 | tf_op jit(solution)/shard_map/all_to_all | solution.py:564
  54.0 4.0 %shard_map.180 = f32[5,8192]{1,0:T(8,128)} custom-call(f32[32,12,128]{2,1,0:T(8,128)S(1)} %all-to-all-done.1.back, s32[64,128]{1,0:T(8,128)S(1)} %copy-done.9, f32[512,128]{1,0:T(8,128)S(1)} %get-tuple-element.14.own, f32[5,8192]{1,0:T(8,128)S(1)} %copy-done.2, f32[64,128]{1,0:T(8,128)S(1)} %bitcast.15), custom_call_target="tpu_custom_call" | custom-call | flops 1000000000 | bytes 10000000 | tf_op jit(solution)/shard_map/pallas_call | solution.py:491
  (13 shorter events, 0.0 us)
Async XLA Ops:
  0.6 16.2 %copy-start = (f32[5,5,8192]{2,1,0:T(8,128)S(1)}, f32[5,5,8192]{2,1,0:T(8,128)}, u32[]{:S(2)}) copy-start(f32[5,5,8192]{2,1,0:T(8,128)} %stress.3) | copy-start | bytes 2457604
  0.6 16.2 %copy-start.1 = (f32[2,4,8192]{2,1,0:T(4,128)S(1)}, f32[2,4,8192]{2,1,0:T(4,128)}, u32[]{:S(2)}) copy-start(f32[2,4,8192]{2,1,0:T(4,128)} %grads.3) | copy-start | bytes 786436
  0.7 16.2 %copy-start.2 = (f32[5,8192]{1,0:T(8,128)S(1)}, f32[5,8192]{1,0:T(8,128)}, u32[]{:S(2)}) copy-start(f32[5,8192]{1,0:T(8,128)} %velocity.7) | copy-start | bytes 491524
  0.7 16.2 %copy-start.3 = (s32[4,8192]{1,0:T(4,128)S(1)}, s32[4,8192]{1,0:T(4,128)}, u32[]{:S(2)}) copy-start(s32[4,8192]{1,0:T(4,128)} %connectivity.3) | copy-start | bytes 393220
  0.7 16.2 %copy-start.4 = (f32[3,2048]{1,0:T(4,128)S(1)}, f32[3,2048]{1,0:T(4,128)}, u32[]{:S(2)}) copy-start(f32[3,2048]{1,0:T(4,128)} %center.1) | copy-start | bytes 73732
  0.7 16.2 %copy-start.5 = (f32[8192]{0:T(1024)S(1)}, f32[8192]{0:T(1024)}, u32[]{:S(2)}) copy-start(f32[8192]{0:T(1024)} %param.22) | copy-start | bytes 98308
  0.7 16.2 %copy-start.6 = (f32[8192]{0:T(1024)S(1)}, f32[8192]{0:T(1024)}, u32[]{:S(2)}) copy-start(f32[8192]{0:T(1024)} %param.23) | copy-start | bytes 98308
  0.7 16.2 %copy-start.7 = (f32[8192]{0:T(1024)S(1)}, f32[8192]{0:T(1024)}, u32[]{:S(2)}) copy-start(f32[8192]{0:T(1024)} %param.24) | copy-start | bytes 98308
  0.7 16.2 %copy-start.10 = (f32[2,2048]{1,0:T(2,128)S(1)}, f32[2,2048]{1,0:T(2,128)}, u32[]{:S(2)}) copy-start(f32[2,2048]{1,0:T(2,128)} %angle.1) | copy-start | bytes 49156
  0.7 16.2 %copy-start.11 = (f32[2048]{0:T(1024)S(1)}, f32[2048]{0:T(1024)}, u32[]{:S(2)}) copy-start(f32[2048]{0:T(1024)} %param.29) | copy-start | bytes 24580
  0.7 16.2 %copy-start.12 = (s32[512]{0:T(512)S(1)}, s32[512]{0:T(512)}, u32[]{:S(2)}) copy-start(s32[512]{0:T(512)} %param.30) | copy-start | bytes 6148
  9.5 20.6 %copy-start.14 = (s32[128]{0:T(128)S(1)}, s32[128]{0:T(128)}, u32[]{:S(2)}) copy-start(s32[128]{0:T(128)} %pair_node.1) | copy-start | bytes 1540
  9.5 20.6 %copy-start.15 = (s32[128]{0:T(128)S(1)}, s32[128]{0:T(128)}, u32[]{:S(2)}) copy-start(s32[128]{0:T(128)} %pair_face.1) | copy-start | bytes 1540
  9.5 20.6 %all-to-all-start = ((f32[32,24,128]{2,1,0:T(8,128)}), f32[32,24,128]{2,1,0:T(8,128)S(1)}, u32[]{:S(2)}, u32[]{:S(2)}) async-start(f32[32,24,128]{2,1,0:T(8,128)} %get-tuple-element.9), calls=%async_computation | async-start | bytes 786432 | tf_op jit(solution)/shard_map/all_to_all | solution.py:526
  17.0 0.8 %copy-start.8 = (s32[64,128]{1,0:T(8,128)S(1)}, s32[64,128]{1,0:T(8,128)}, u32[]{:S(2)}) copy-start(s32[64,128]{1,0:T(8,128)} %get-tuple-element.10.slot) | copy-start | bytes 98308
  18.1 4.1 %collective-permute-start = (f32[72,128]{1,0:T(8,128)S(1)}, f32[72,128]{1,0:T(8,128)S(1)}, u32[]{:S(2)}, u32[]{:S(2)}) collective-permute-start(f32[72,128]{1,0:T(8,128)S(1)} %get-tuple-element.12), channel_id=1, source_target_pairs={{0,1},{1,2},{2,3},{3,4},{4,5},{5,6},{6,7},{7,8},{8,9},{9,10},{10,1... | collective-permute-start | bytes 110600 | tf_op jit(solution)/shard_map/ppermute | solution.py:547
  20.3 4.2 %collective-permute-start.1 = (f32[72,128]{1,0:T(8,128)S(1)}, f32[72,128]{1,0:T(8,128)S(1)}, u32[]{:S(2)}, u32[]{:S(2)}) collective-permute-start(f32[72,128]{1,0:T(8,128)S(1)} %get-tuple-element.13), channel_id=1, source_target_pairs={{1,0},{2,1},{3,2},{4,3},{5,4},{6,5},{7,6},{8,7},{9,8},{10,9},{11,1... | collective-permute-start | bytes 110600 | tf_op jit(solution)/shard_map/ppermute | solution.py:548
  40.3 13.7 %all-to-all-start.1 = ((f32[32,12,128]{2,1,0:T(8,128)}), f32[32,12,128]{2,1,0:T(8,128)S(1)}, u32[]{:S(2)}, u32[]{:S(2)}) async-start(f32[32,12,128]{2,1,0:T(8,128)} %shard_map.178.returned), calls=%async_computation.1 | async-start | bytes 524288 | tf_op jit(solution)/shard_map/all_to_all | solution.py:564
  43.4 10.6 %copy-start.9 = (s32[64,128]{1,0:T(8,128)S(1)}, s32[64,128]{1,0:T(8,128)}, u32[]{:S(2)}) copy-start(s32[64,128]{1,0:T(8,128)} %get-tuple-element.10.slot) | copy-start | bytes 98308
  43.4 10.6 %copy-start.13 = (f32[8192]{0:T(1024)S(1)}, f32[8192]{0:T(1024)}, u32[]{:S(2)}) copy-start(f32[8192]{0:T(1024)} %param.19) | copy-start | bytes 98308

commit v4 on v3

--- a/solution.py
+++ b/solution.py
@@ -1,4 +1,5 @@
 import functools
+import math
 
 import jax
 import jax.numpy as jnp
@@ -9,6 +10,7 @@
 
 LANES = 128
 LOW = 64
+THIN = 32
 
 LOBATTO_POINTS = (-1.0, -0.6546536707079771, 0.0, 0.6546536707079771, 1.0)
 LOBATTO_WEIGHTS = (0.1, 49.0 / 90.0, 32.0 / 45.0, 49.0 / 90.0, 0.1)
@@ -39,56 +41,106 @@
     return packed if count == 16 else jnp.concatenate([packed] * (count // 16), axis=0)
 
 
-def arrange_kernel(owner, position, velocity, out, slot_out, acc, *, devices, capacity):
+def arrange_kernel(
+    owner, position_away, velocity_away, out, slot_out, acc, ordered, bounds, bounds_scalar, position, velocity,
+    arrived, *, devices, capacity
+):
     rows = owner.shape[0]
+    load_position = pltpu.make_async_copy(position_away, position, arrived.at[1])
+    load_velocity = pltpu.make_async_copy(velocity_away, velocity, arrived.at[2])
+    load_position.start()
+    load_velocity.start()
     tiles = capacity // LANES
     upper = jnp.where(iota((LANES, 2 * LANES), 1) > iota((LANES, 2 * LANES), 0), 1.0, 0.0).astype(BF16)
     device_ids = iota((devices, LANES), 0)
-    low_ids = iota((LOW, LANES), 0).astype(F32).astype(BF16)
-    group_ids = iota((2 * LANES, LANES), 0).astype(F32).astype(BF16)
-    acc[...] = jnp.zeros_like(acc)
-    one, zero = jnp.ones((), BF16), jnp.zeros((), BF16)
-
-    def step(k, base):
-        owners = owner[pl.ds(pl.multiple_of(k * 8, 8), 8), :]
-        masks = [jnp.broadcast_to(owners[s : s + 1], (devices, LANES)) == device_ids for s in range(8)]
+
+    def count(k, base):
+        owners = owner[pl.ds(pl.multiple_of(k * 32, 32), 32), :]
+        masks = [jnp.broadcast_to(owners[s : s + 1], (devices, LANES)) == device_ids for s in range(32)]
         hot = jnp.concatenate([jnp.where(m, 1.0, 0.0).astype(BF16) for m in masks], axis=0)
         counted = lax.dot_general(hot, upper, NN, preferred_element_type=F32)
         ranks = []
-        for s in range(8):
+        for s in range(32):
             part = counted[s * devices : (s + 1) * devices]
             ranks.append(jnp.sum(jnp.where(masks[s], part[:, :LANES] + base, 0.0), axis=0, keepdims=True))
             base = base + part[:, LANES:]
         rank = jnp.concatenate(ranks, axis=0).astype(jnp.int32)
-        slot = owners * capacity + rank
-        slot_out[pl.ds(pl.multiple_of(k * 8, 8), 8), :] = slot
-        low = (slot & (LOW - 1)).astype(F32)
-        group = (((slot >> 6) & 1) * LANES + (slot >> 7)).astype(F32)
-        for first in range(0, 8, 2):
-            left, right = [], []
-            for s in range(first, first + 2):
-                lanes = pl.ds(pl.multiple_of(k * 8 * LANES + s * LANES, LANES), LANES)
-                hot_low = jnp.where(tiled_rows(low[s : s + 1], LOW) == low_ids, one, zero)
-                right.append(jnp.where(tiled_rows(group[s : s + 1], 2 * LANES) == group_ids, one, zero))
-                place = position[:, lanes]
-                place = place + jnp.where(iota(place.shape, 0) == 0, 1.0, 0.0)
-                column = []
-                for data in (place, velocity[0:3, lanes]):
-                    parts = split2(data)
-                    for c in range(3):
-                        for half in range(2):
-                            column.append(hot_low * tiled_rows(parts[half][c : c + 1], LOW))
-                left.append(jnp.concatenate(column, axis=0))
-            acc[...] += lax.dot_general(
-                jnp.concatenate(left, axis=1), jnp.concatenate(right, axis=1), NT, preferred_element_type=F32
-            )
+        slot_out[pl.ds(pl.multiple_of(k * 32, 32), 32), :] = owners * capacity + rank
         return base
 
-    lax.fori_loop(0, rows // 8, step, jnp.zeros((devices, LANES), F32))
+    totals = lax.fori_loop(0, rows // 32, count, jnp.zeros((devices, LANES), F32))
+    lower = jnp.where(iota((devices, devices), 0) > iota((devices, devices), 1), 1.0, 0.0).astype(BF16)
+    high, low = split2(totals)
+    starts = lax.dot_general(lower, jnp.concatenate([high, low], axis=1).astype(BF16), NN, preferred_element_type=F32)
+    starts = starts[:, :LANES] + starts[:, LANES:]
+    by_lane = []
+    for data in (starts, totals):
+        if devices < LANES:
+            data = jnp.concatenate([data, jnp.zeros((LANES - devices, LANES), F32)], axis=0)
+        by_lane.append(data.T[0:8].astype(jnp.int32))
+    start_lanes = by_lane[0]
+    bounds[...] = jnp.where(iota((8, LANES), 0) == 0, by_lane[0], by_lane[1])
+    copy = pltpu.make_async_copy(bounds, bounds_scalar, arrived.at[0])
+    copy.start()
+
+    low_ids = iota((THIN, LANES), 0).astype(F32).astype(BF16)
+    group_ids = iota((2 * LANES, LANES), 0).astype(F32).astype(BF16)
+    acc[...] = jnp.zeros_like(acc)
+    one, zero = jnp.ones((), BF16), jnp.zeros((), BF16)
+    load_position.wait()
+    load_velocity.wait()
+
+    def sort(k, carry):
+        owners = owner[pl.ds(pl.multiple_of(k * 64, 64), 64), :]
+        rank = slot_out[pl.ds(pl.multiple_of(k * 64, 64), 64), :] - owners * capacity
+        place = jnp.concatenate([jnp.take_along_axis(start_lanes, owners[8 * h : 8 * h + 8], axis=1) for h in range(8)], axis=0) + rank
+        low = (place & (THIN - 1)).astype(F32)
+        group = (((place >> 6) & 1) * LANES + ((place >> 5) & 1) * (LANES // 2) + (place >> 7)).astype(F32)
+        left, right = [], []
+        for s in range(64):
+            lanes = pl.ds(pl.multiple_of(k * 64 * LANES + s * LANES, LANES), LANES)
+            hot_low = jnp.where(tiled_rows(low[s : s + 1], THIN) == low_ids, one, zero)
+            right.append(jnp.where(tiled_rows(group[s : s + 1], 2 * LANES) == group_ids, one, zero))
+            where = position[:, lanes]
+            where = where + jnp.where(iota(where.shape, 0) == 0, 1.0, 0.0)
+            column = []
+            for data in (where, velocity[0:3, lanes]):
+                parts = split2(data)
+                for c in range(3):
+                    for half in range(2):
+                        column.append(hot_low * tiled_rows(parts[half][c : c + 1], THIN))
+            left.append(jnp.concatenate(column, axis=0))
+        acc[...] += lax.dot_general(
+            jnp.concatenate(left, axis=1), jnp.concatenate(right, axis=1), NT, preferred_element_type=F32
+        )
+        return carry
+
+    lax.fori_loop(0, rows // 64, sort, 0)
     for c in range(6):
-        both = acc[2 * c * LOW : (2 * c + 1) * LOW, :] + acc[(2 * c + 1) * LOW : (2 * c + 2) * LOW, :]
-        square = jnp.concatenate([both[:, :LANES], both[:, LANES:]], axis=0).T
-        out[:, c * tiles : (c + 1) * tiles, :] = square.reshape(devices, tiles, LANES)
+        both = acc[2 * c * THIN : (2 * c + 1) * THIN, :] + acc[(2 * c + 1) * THIN : (2 * c + 2) * THIN, :]
+        pieces = []
+        for data in (both[:, :LANES], both[:, LANES:]):
+            pieces += [data, pltpu.roll(data, LANES // 2, 1)]
+        ordered[pl.ds(c, rows, stride=8), :] = jnp.concatenate(pieces, axis=0).T[0:rows]
+    ordered[8 * rows :, :] = jnp.zeros((8, LANES), F32)
+    copy.wait()
+    lane = iota((8, LANES), 1)
+
+    def place_runs(i, carry):
+        for n in range(4):
+            device = i * 4 + n
+            start, amount = bounds_scalar[0, device], bounds_scalar[1, device]
+            for t in range(tiles):
+                at = start + t * LANES
+                row = jnp.minimum(at >> 7, rows - 1)
+                shift = at & (LANES - 1)
+                this = ordered[pl.ds(pl.multiple_of(row * 8, 8), 8), :]
+                following = ordered[pl.ds(pl.multiple_of(row * 8 + 8, 8), 8), :]
+                turned = pltpu.roll(jnp.where(lane >= shift, this, following), (LANES - shift) & (LANES - 1), 1)
+                out[device, pl.ds(t, 6, stride=tiles), :] = jnp.where(lane < amount - t * LANES, turned, 0.0)[0:6]
+        return carry
+
+    lax.fori_loop(0, devices // 4, place_runs, 0)
 
 
 FACE_ROWS = 16
@@ -324,18 +376,18 @@
     acc[...] = jnp.zeros_like(acc)
 
     def scatter(step, carry):
-        b = step * 4
+        b = step * 16
         parts = []
-        for i in range(4):
+        for i in range(16):
             index = connectivity[:, pl.ds(pl.multiple_of((b + i) * LANES, LANES), LANES)]
             lanes = (index & (LANES - 1)).astype(F32)
             rels = ((index >> 7) - (b + i)).astype(F32)
             parts.append(spread_row(spread, pitch, b + i, lanes, rels, (0, 1, 2)))
         total = {}
-        for i in range(4):
+        for i in range(16):
             for j in range(3):
                 total[i + j] = parts[i][j] if i + j not in total else total[i + j] + parts[i][j]
-        for n in range(6):
+        for n in range(18):
             at = pl.ds(pl.multiple_of((b + n) * 8, 8), 8)
             if n < 2:
                 acc[at, :] += total[n]
@@ -343,7 +395,7 @@
                 acc[at, :] = total[n]
         return carry
 
-    lax.fori_loop(0, rows // 4, scatter, 0)
+    lax.fori_loop(0, rows // 16, scatter, 0)
     for side, row, j in ((0, 1, 2), (1, rows, 0)):
         lanes = jnp.concatenate([place[0][side : side + 1] for place in places], axis=0).astype(F32)
         rels = jnp.concatenate([place[1][side : side + 1] for place in places], axis=0).astype(F32)
@@ -351,9 +403,7 @@
     own[...] = acc[8 : 8 + 8 * rows, :]
 
 
-def contact_kernel(
-    pair_node, pair_face, pair_count, nodes, own, before, after, out, raw, face, mean, table, acc, *, devices, tiles
-):
+def prepare_kernel(own, before, after, face, raw):
     own_rows = own.shape[0]
     face_tiles = (own_rows + 32) // 8
     raw[0:16, :] = before[0:FACE_ROWS, :]
@@ -374,22 +424,18 @@
         coef_a = jnp.where(inside, (-DAMPING) * stiff * data, jnp.where(sub == 7, stiff, 0.0))
         square = place[0] * place[0] + place[1] * place[1] + place[2] * place[2]
         along = normal[0] * place[0] + normal[1] * place[1] + normal[2] * place[2]
-        for q, (coef, const) in enumerate(((coef_e, (-LOG2E / REACH_SQ) * square), (coef_d, along), (coef_a, None))):
+        zero = jnp.zeros((8, LANES), F32)
+        pieces = []
+        for coef, const in ((coef_e, (-LOG2E / REACH_SQ) * square), (coef_d, along), (coef_a, None)):
             high, low = split2(coef)
-            if const is None:
-                last = jnp.where(inside, data, 0.0)
-            else:
+            last = zero
+            if const is not None:
                 c_high, c_low = split2(const)
                 last = jnp.where(sub == 0, c_high, jnp.where(sub == 1, c_low, 0.0))
-            turned = jnp.concatenate([high, high, low, last], axis=0).T
-            packed = turned.astype(BF16)
-            for j in range(8):
-                at = f * 384 + j * 48
-                face[pl.ds(pl.multiple_of(at + q * 16, 16), 16), :] = packed[j * 16 : j * 16 + 16]
-                if const is None:
-                    for c in range(3):
-                        column = turned[j * 16 : j * 16 + 16, 27 + c : 28 + c]
-                        mean[pl.ds(pl.multiple_of(at + c * 16, 16), 16), :] = jnp.broadcast_to(column, (16, LANES))
+            pieces += [high, high, low, last]
+        pieces.append(jnp.where(sub < 3, split2(m_low)[0], jnp.where(inside, split2(data)[1], 0.0)))
+        turned = jnp.concatenate(pieces + [zero] * 3, axis=0).T
+        face[pl.ds(pl.multiple_of(f * LANES, LANES), LANES), :] = turned.astype(BF16)
 
     def prepare_group(i, carry):
         for n in range(4):
@@ -397,6 +443,19 @@
         return carry
 
     lax.fori_loop(0, face_tiles // 4, prepare_group, 0)
+
+
+def contact_kernel(pair_node, pair_face, pair_count, nodes, face, out, mean, table, acc, *, devices, tiles):
+    row_ids, column_ids = iota((LANES, 3 * LANES), 0), iota((LANES, 3 * LANES), 1) // LANES
+    picks = jnp.where((row_ids == 96 + column_ids) | (row_ids == 99 + column_ids), 1.0, 0.0).astype(BF16)
+    step_rows = face.shape[0] // 2
+
+    def widen(i, carry):
+        at = pl.ds(pl.multiple_of(i * step_rows, step_rows), step_rows)
+        mean[at, :] = lax.dot_general(face[at, :], picks, NN, preferred_element_type=F32)
+        return carry
+
+    lax.fori_loop(0, face.shape[0] // step_rows, widen, 0)
     total = devices * tiles
     acc[...] = jnp.zeros_like(acc)
     for c in range(6):
@@ -408,25 +467,28 @@
             square = flat * flat if c == 0 else square + flat * flat
         table[pl.ds(c, total, stride=8), :] = flat
     table[pl.ds(6, total, stride=8), :] = (-LOG2E / REACH_SQ) * square
-    ones = jnp.where(sub < 2, 1.0, 0.0)
+    ones = jnp.where(iota((8, LANES), 0) < 2, 1.0, 0.0)
+    gap = jnp.zeros((32, LANES), BF16)
 
     def pair_force(node, which):
         high, low = split2(table[pl.ds(pl.multiple_of(node * 8, 8), 8), :])
         matrix = jnp.concatenate([high, low, high, ones], axis=0).astype(BF16)
-        at = pl.ds(pl.multiple_of(which * 384, 384), 384)
-        terms = lax.dot_general(face[at, :], matrix, NN, preferred_element_type=F32)
+        blocks = [jnp.concatenate([gap] * q + [matrix] + [gap] * (3 - q), axis=0) for q in range(3)]
+        at = pl.ds(pl.multiple_of(which * LANES, LANES), LANES)
+        terms = lax.dot_general(face[at, :], jnp.concatenate(blocks, axis=1), NN, preferred_element_type=F32)
         sums = [None] * 3
         for j in range(8):
-            power, depth, scale = [terms[j * 48 + q * 16 : j * 48 + q * 16 + 16] for q in range(3)]
+            power, depth, scale = [terms[j * 16 : j * 16 + 16, q * LANES : (q + 1) * LANES] for q in range(3)]
             magnitude = jnp.exp2(power) * jnp.maximum(depth, 0.0) * scale
+            at = pl.ds(pl.multiple_of(which * LANES + j * 16, 16), 16)
             for c in range(3):
-                term = magnitude * mean[pl.ds(pl.multiple_of(which * 384 + j * 48 + c * 16, 16), 16), :]
+                term = magnitude * mean[at, c * LANES : (c + 1) * LANES]
                 term = term[:8] + term[8:]
                 sums[c] = term if j == 0 else sums[c] + term
         return sums
 
     count = pair_count[0]
-    group = 8
+    group = math.gcd(32, pair_node.shape[0])
 
     def step(i, carry):
         ids = [i * group + n for n in range(group)]
@@ -462,37 +524,38 @@
     sub = iota((8, LANES), 0)
 
     def step(k, carry):
-        slots = slot[pl.ds(pl.multiple_of(k * 8, 8), 8), :]
+        slots = slot[pl.ds(pl.multiple_of(k * 64, 64), 64), :]
         low = slots & (LOW - 1)
         group = (((slots >> 6) & 1) * LANES + (slots >> 7)).astype(F32)
-        for s in range(0, 8, 2):
-            hot = [jnp.where(tiled_rows(group[i : i + 1], 2 * LANES) == group_ids, one, zero) for i in (s, s + 1)]
-            left = jnp.concatenate([table[0], table[1]], axis=1)
-            picked = lax.dot_general(left, jnp.concatenate(hot, axis=1), NN, preferred_element_type=F32)
-            for i in range(2):
-                r = k * 8 + s + i
-                mask = jnp.broadcast_to(low[s + i : s + i + 1], (LOW, LANES)) == low_ids
-                contact = jnp.zeros((8, LANES), F32)
-                for c in range(3):
-                    part = picked[2 * c * LOW : (2 * c + 2) * LOW, i * LANES : (i + 1) * LANES]
-                    value = jnp.sum(jnp.where(mask, part[:LOW] + part[LOW:], 0.0), axis=0, keepdims=True)
-                    contact = jnp.where(sub == c, value, contact)
-                lanes = pl.ds(pl.multiple_of(r * LANES, LANES), LANES)
-                total = contact - own[pl.ds(pl.multiple_of(r * 8, 8), 8), :]
-                out[:, lanes] = velocity[:, lanes] + inv_mass[pl.ds(r, 1), :] * total[0:5]
-        return carry
-
-    lax.fori_loop(0, rows // 8, step, 0)
-
-
-def call(kernel, outs, ins, scratch, cost, smem=0, limit=12, away=()):
+        hot = [jnp.where(tiled_rows(group[i : i + 1], 2 * LANES) == group_ids, one, zero) for i in range(64)]
+        left = jnp.concatenate([table[0], table[1]], axis=1)
+        picked = lax.dot_general(left, jnp.concatenate(hot, axis=1), NN, preferred_element_type=F32)
+        for i in range(64):
+            r = k * 64 + i
+            mask = jnp.broadcast_to(low[i : i + 1], (LOW, LANES)) == low_ids
+            contact = jnp.zeros((8, LANES), F32)
+            for c in range(3):
+                part = picked[2 * c * LOW : (2 * c + 2) * LOW, i * LANES : (i + 1) * LANES]
+                value = jnp.sum(jnp.where(mask, part[:LOW] + part[LOW:], 0.0), axis=0, keepdims=True)
+                contact = jnp.where(sub == c, value, contact)
+            lanes = pl.ds(pl.multiple_of(r * LANES, LANES), LANES)
+            total = contact - own[pl.ds(pl.multiple_of(r * 8, 8), 8), :]
+            out[:, lanes] = velocity[:, lanes] + inv_mass[pl.ds(r, 1), :] * total[0:5]
+        return carry
+
+    lax.fori_loop(0, rows // 64, step, 0)
+
+
+def call(kernel, outs, ins, scratch, cost, smem=0, limit=12, away=(), out_away=()):
     vmem = pl.BlockSpec(memory_space=pltpu.VMEM)
     scalar = pl.BlockSpec(memory_space=pltpu.SMEM)
     return pl.pallas_call(
         kernel,
         out_shape=outs,
-        in_specs=[scalar if n < smem else pl.BlockSpec(memory_space=pl.ANY) if n in away else vmem for n in range(len(ins))],
-        out_specs=jax.tree.map(lambda _: vmem, outs),
+        in_specs=[scalar if n < smem else pl.BlockSpec(memory_space=pltpu.HBM) if n in away else vmem for n in range(len(ins))],
+        out_specs=tuple(pl.BlockSpec(memory_space=pl.ANY) if n in out_away else vmem for n in range(len(outs)))
+        if isinstance(outs, tuple)
+        else vmem,
         scratch_shapes=scratch,
         compiler_params=pltpu.CompilerParams(vmem_limit_bytes=limit << 20),
         cost_estimate=pl.CostEstimate(flops=cost, bytes_accessed=cost // 100, transcendentals=0),
@@ -518,10 +581,17 @@
         (shape(devices, 6 * tiles, LANES), jax.ShapeDtypeStruct((rows, LANES), jnp.int32)),
         (view(contact_owner), position, velocity),
         [
-            pltpu.VMEM((12 * LOW, 2 * LANES), F32),
+            pltpu.VMEM((12 * THIN, 2 * LANES), F32),
+            pltpu.VMEM((8 * (rows + 1), LANES), F32),
+            pltpu.VMEM((8, LANES), jnp.int32),
+            pltpu.SMEM((8, LANES), jnp.int32),
+            pltpu.VMEM(position.shape, F32),
+            pltpu.VMEM(velocity.shape, F32),
+            pltpu.SemaphoreType.DMA((3,)),
         ],
         10**9,
         limit=56,
+        away=(1, 2),
     )
     incoming = lax.all_to_all(outgoing, axes, split_axis=0, concat_axis=0, tiled=True)
     own_faces, send_up, send_down = call(
@@ -547,14 +617,19 @@
     before = lax.ppermute(send_up, axes, up)
     after = lax.ppermute(send_down, axes, down)
     face_rows = own_faces.shape[0] + 32
+    face_matrix = call(
+        prepare_kernel,
+        jax.ShapeDtypeStruct((face_rows * 16, LANES), BF16),
+        (own_faces, before, after),
+        [pltpu.VMEM((face_rows, LANES), F32)],
+        10**8,
+    )
     returned = call(
         functools.partial(contact_kernel, devices=devices, tiles=tiles),
         shape(devices, 3 * tiles, LANES),
-        (pair_node, pair_face, pair_count, incoming, own_faces, before, after),
+        (pair_node, pair_face, pair_count, incoming, face_matrix),
         [
-            pltpu.VMEM((face_rows, LANES), F32),
-            pltpu.VMEM((face_rows * 48, 32), BF16),
-            pltpu.VMEM((face_rows * 48, LANES), F32),
+            pltpu.VMEM((face_rows * 16, 3 * LANES), F32),
             pltpu.VMEM((devices * tiles * 8, LANES), F32),
             pltpu.VMEM((devices * tiles * 24, LANES), F32),
         ],

time: 58.1 us -> 49.6 us (0.85)
  Pallas kernels: 31.2 us -> 20.1 us
  starting transfers between devices: 13.9 us -> 15.5 us
  waiting for transfers between devices: 10.6 us -> 11.5 us
    pallas_call x5 -> x6, Pallas kernels: 31.2 us -> 20.1 us  [call(): pl.pallas_call(kernel, out_shape=outs, in_specs=[scalar if n < smem else...]
    all_to_all x1, starting transfers between devices: 3.09 us -> 4.72 us  [body(): lax.all_to_all(returned, axes, split_axis=0, concat_axis=0, tiled=True)]
    all_to_all x1, waiting for transfers between devices: 2.77 us -> 4.23 us  [body(): lax.all_to_all(returned, axes, split_axis=0, concat_axis=0, tiled=True)]
    all_to_all x1, waiting for transfers between devices: 5.56 us -> 4.94 us  [body(): lax.all_to_all(outgoing, axes, split_axis=0, concat_axis=0, tiled=True)]
  transfers between devices with their start and end apart: 4 -> 4, of which waited for: 3 -> 3; matrix products, arithmetic and copies ran while one was open for 0% -> 0% of each run, Pallas kernels for 14% -> 15%
where the time goes in v4:
time: 49.6 us; the launch traced here: 49.5 us
  Pallas kernels  20.1 us (41%)
  starting transfers between devices  15.5 us (31%)
  waiting for transfers between devices  11.5 us (23%)
  between operations  1.55 us (3%)
  local copies, waits for them, and re-layouts  0.82 us (2%)
    pallas_call x6, Pallas kernels, call(): pl.pallas_call(kernel, out_shape=outs, in_specs=[scalar if n < smem else...  20.1 us
    all_to_all x1, starting transfers between devices, body(): lax.all_to_all(outgoing, axes, split_axis=0, concat_axis=0, tiled=True)  7.33 us
    all_to_all x1, waiting for transfers between devices, body(): lax.all_to_all(outgoing, axes, split_axis=0, concat_axis=0, tiled=True)  4.94 us
    all_to_all x1, starting transfers between devices, body(): lax.all_to_all(returned, axes, split_axis=0, concat_axis=0, tiled=True)  4.72 us
    all_to_all x1, waiting for transfers between devices, body(): lax.all_to_all(returned, axes, split_axis=0, concat_axis=0, tiled=True)  4.23 us
    ppermute x1, waiting for transfers between devices, body(): after = lax.ppermute(send_down, axes, down)  2.29 us
    ppermute x1, starting transfers between devices, body(): before = lax.ppermute(send_up, axes, up)  2.16 us
    ppermute x1, starting transfers between devices, body(): after = lax.ppermute(send_down, axes, down)  1.29 us
  transfers between devices with their start and end apart: 4, of which 3 were waited for; matrix products, arithmetic and copies ran while one was open for 0% of the time, Pallas kernels for 15%

profile of v4, /device:TPU:0, one launch (start us, length us, event | category | flops | bytes accessed | tf_op | source)
XLA Modules:
  0.0 49.5 jit_solution(2636950131881144777)
XLA Ops:
  0.6 0.0 copy-start
  0.6 0.0 copy-start.1
  0.7 0.0 copy-start.2
  0.7 0.0 copy-start.3
  0.7 0.0 copy-start.4
  0.7 0.0 copy-start.5
  0.7 0.0 copy-start.6
  0.7 0.0 copy-start.7
  0.7 0.0 copy-start.10
  0.7 0.0 copy-start.11
  0.7 0.0 copy-start.12
  0.7 5.6 %shard_map.176 = (f32[32,24,128]{2,1,0:T(8,128)}, s32[64,128]{1,0:T(8,128)}) custom-call(s32[64,128]{1,0:T(8,128)} %bitcast.16, f32[3,8192]{1,0:T(4,128)} %position_away.1, f32[5,8192]{1,0:T(8,128)} %velocity.5), custom_call_target="tpu_custom_call" | custom-call | flops 1000000000 | bytes 10000000 | tf_op jit(solution)/shard_map/pallas_call | solution.py:552
  6.4 7.3 %all-to-all-start = ((f32[32,24,128]{2,1,0:T(8,128)}), f32[32,24,128]{2,1,0:T(8,128)S(1)}, u32[]{:S(2)}, u32[]{:S(2)}) async-start(f32[32,24,128]{2,1,0:T(8,128)} %get-tuple-element.9), calls=%async_computation | async-start | bytes 786432 | tf_op jit(solution)/shard_map/all_to_all | solution.py:596
  13.7 0.0 copy-done
  13.7 0.0 copy-done.1
  13.7 0.0 copy-done.2
  13.8 0.7 %copy-done.8 = s32[64,128]{1,0:T(8,128)S(1)} copy-done((s32[64,128]{1,0:T(8,128)S(1)}, s32[64,128]{1,0:T(8,128)}, u32[]{:S(2)}) %copy-start.8) | copy-done | bytes 32792
  14.6 0.4 shard_map.177
  15.0 2.2 %collective-permute-start = (f32[72,128]{1,0:T(8,128)S(1)}, f32[72,128]{1,0:T(8,128)S(1)}, u32[]{:S(2)}, u32[]{:S(2)}) collective-permute-start(f32[72,128]{1,0:T(8,128)S(1)} %get-tuple-element.12), channel_id=1, source_target_pairs={{0,1},{1,2},{2,3},{3,4},{4,5},{5,6},{6,7},{7,8},{8,9},{9,10},{10,1... | collective-permute-start | bytes 110600 | tf_op jit(solution)/shard_map/ppermute | solution.py:617
  17.1 1.3 %collective-permute-start.1 = (f32[72,128]{1,0:T(8,128)S(1)}, f32[72,128]{1,0:T(8,128)S(1)}, u32[]{:S(2)}, u32[]{:S(2)}) collective-permute-start(f32[72,128]{1,0:T(8,128)S(1)} %get-tuple-element.13), channel_id=1, source_target_pairs={{1,0},{2,1},{3,2},{4,3},{5,4},{6,5},{7,6},{8,7},{9,8},{10,9},{11,1... | collective-permute-start | bytes 110600 | tf_op jit(solution)/shard_map/ppermute | solution.py:618
  19.1 0.0 collective-permute-done.before
  19.1 2.3 %collective-permute-done.1.after = f32[72,128]{1,0:T(8,128)S(1)} collective-permute-done((f32[72,128]{1,0:T(8,128)S(1)}, f32[72,128]{1,0:T(8,128)S(1)}, u32[]{:S(2)}, u32[]{:S(2)}) %collective-permute-start.1) | collective-permute-done | bytes 36896 | tf_op jit(solution)/shard_map/ppermute | solution.py:618
  21.4 0.6 %shard_map.178.face = bf16[2560,128]{1,0:T(8,128)(2,1)S(1)} custom-call(f32[128,128]{1,0:T(8,128)S(1)} %get-tuple-element.11.own, f32[72,128]{1,0:T(8,128)S(1)} %collective-permute-done.before, f32[72,128]{1,0:T(8,128)S(1)} %collective-permute-done.1.after), custom_call_target="tpu_custom_call" | custom-call | flops 100000000 | bytes 1000000 | tf_op jit(solution)/shard_map/pallas_call | solution.py:552
  22.0 4.9 %all-to-all-done.nodes = f32[32,24,128]{2,1,0:T(8,128)S(1)} async-done(((f32[32,24,128]{2,1,0:T(8,128)}), f32[32,24,128]{2,1,0:T(8,128)S(1)}, u32[]{:S(2)}, u32[]{:S(2)}) %all-to-all-start) | async-done | bytes 393248 | tf_op jit(solution)/shard_map/all_to_all | solution.py:596
  26.9 0.0 copy-done.14
  27.0 4.6 %shard_map.179.returned = f32[32,12,128]{2,1,0:T(8,128)} custom-call(s32[128]{0:T(128)S(1)} %copy-done.14, s32[128]{0:T(128)S(1)} %copy-done.15, s32[1]{0:T(128)S(6)} %copy.19.pair_count, f32[32,24,128]{2,1,0:T(8,128)S(1)} %all-to-all-done.nodes, bf16[2560,128]{1,0:T(8,128)(2,1)S(1)} %shard_map.178.face), custom_call_target="tpu_custom_call" | custom-call | flops 1000000000 | bytes 10000000 | tf_op jit(solution)/shard_map/pallas_call | solution.py:552
  31.5 4.7 %all-to-all-start.1 = ((f32[32,12,128]{2,1,0:T(8,128)}), f32[32,12,128]{2,1,0:T(8,128)S(1)}, u32[]{:S(2)}, u32[]{:S(2)}) async-start(f32[32,12,128]{2,1,0:T(8,128)} %shard_map.179.returned), calls=%async_computation.1 | async-start | bytes 524288 | tf_op jit(solution)/shard_map/all_to_all | solution.py:639
  36.3 0.0 copy-start.13
  36.3 6.3 %shard_map.180 = (f32[5,5,8192]{2,1,0:T(8,128)}, f32[512,128]{1,0:T(8,128)S(1)}) custom-call(f32[5,8192]{1,0:T(8,128)S(1)} %copy-done.2, f32[72,128]{1,0:T(8,128)S(1)} %collective-permute-done.before, f32[72,128]{1,0:T(8,128)S(1)} %collective-permute-done.1.after, s32[4,8192]{1,0:T(4,128)S(1)} %copy-done.3, f32[2,4,8192]{2,1,0:T(4,128)S(1)} %copy-done.1, ...), custom_call_target="tpu_custom_call" | custom-call | flops 1000000000 | bytes 10000000 | tf_op jit(solution)/shard_map/pallas_call | solution.py:552
  42.6 4.2 %all-to-all-done.1.back = f32[32,12,128]{2,1,0:T(8,128)S(1)} async-done(((f32[32,12,128]{2,1,0:T(8,128)}), f32[32,12,128]{2,1,0:T(8,128)S(1)}, u32[]{:S(2)}, u32[]{:S(2)}) %all-to-all-start.1) | async-done | bytes 196640 | tf_op jit(solution)/shard_map/all_to_all | solution.py:639
  46.8 0.0 copy-done.13
  46.8 2.6 %shard_map.181 = f32[5,8192]{1,0:T(8,128)} custom-call(f32[32,12,128]{2,1,0:T(8,128)S(1)} %all-to-all-done.1.back, s32[64,128]{1,0:T(8,128)S(1)} %copy-done.9, f32[512,128]{1,0:T(8,128)S(1)} %get-tuple-element.14.own, f32[5,8192]{1,0:T(8,128)S(1)} %copy-done.2, f32[64,128]{1,0:T(8,128)S(1)} %bitcast.15), custom_call_target="tpu_custom_call" | custom-call | flops 1000000000 | bytes 10000000 | tf_op jit(solution)/shard_map/pallas_call | solution.py:552
  (14 shorter events, 0.0 us)
Async XLA Ops:
  0.6 13.1 %copy-start = (f32[5,5,8192]{2,1,0:T(8,128)S(1)}, f32[5,5,8192]{2,1,0:T(8,128)}, u32[]{:S(2)}) copy-start(f32[5,5,8192]{2,1,0:T(8,128)} %stress.3) | copy-start | bytes 2457604
  0.6 13.1 %copy-start.1 = (f32[2,4,8192]{2,1,0:T(4,128)S(1)}, f32[2,4,8192]{2,1,0:T(4,128)}, u32[]{:S(2)}) copy-start(f32[2,4,8192]{2,1,0:T(4,128)} %grads.3) | copy-start | bytes 786436
  0.7 13.1 %copy-start.2 = (f32[5,8192]{1,0:T(8,128)S(1)}, f32[5,8192]{1,0:T(8,128)}, u32[]{:S(2)}) copy-start(f32[5,8192]{1,0:T(8,128)} %velocity.5) | copy-start | bytes 491524
  0.7 13.1 %copy-start.3 = (s32[4,8192]{1,0:T(4,128)S(1)}, s32[4,8192]{1,0:T(4,128)}, u32[]{:S(2)}) copy-start(s32[4,8192]{1,0:T(4,128)} %connectivity.3) | copy-start | bytes 393220
  0.7 13.1 %copy-start.4 = (f32[3,2048]{1,0:T(4,128)S(1)}, f32[3,2048]{1,0:T(4,128)}, u32[]{:S(2)}) copy-start(f32[3,2048]{1,0:T(4,128)} %center.1) | copy-start | bytes 73732
  0.7 13.1 %copy-start.5 = (f32[8192]{0:T(1024)S(1)}, f32[8192]{0:T(1024)}, u32[]{:S(2)}) copy-start(f32[8192]{0:T(1024)} %param.22) | copy-start | bytes 98308
  0.7 13.1 %copy-start.6 = (f32[8192]{0:T(1024)S(1)}, f32[8192]{0:T(1024)}, u32[]{:S(2)}) copy-start(f32[8192]{0:T(1024)} %param.23) | copy-start | bytes 98308
  0.7 13.1 %copy-start.7 = (f32[8192]{0:T(1024)S(1)}, f32[8192]{0:T(1024)}, u32[]{:S(2)}) copy-start(f32[8192]{0:T(1024)} %param.24) | copy-start | bytes 98308
  0.7 13.1 %copy-start.10 = (f32[2,2048]{1,0:T(2,128)S(1)}, f32[2,2048]{1,0:T(2,128)}, u32[]{:S(2)}) copy-start(f32[2,2048]{1,0:T(2,128)} %angle.1) | copy-start | bytes 49156
  0.7 13.1 %copy-start.11 = (f32[2048]{0:T(1024)S(1)}, f32[2048]{0:T(1024)}, u32[]{:S(2)}) copy-start(f32[2048]{0:T(1024)} %param.29) | copy-start | bytes 24580
  0.7 13.1 %copy-start.12 = (s32[512]{0:T(512)S(1)}, s32[512]{0:T(512)}, u32[]{:S(2)}) copy-start(s32[512]{0:T(512)} %param.30) | copy-start | bytes 6148
  6.4 20.6 %all-to-all-start = ((f32[32,24,128]{2,1,0:T(8,128)}), f32[32,24,128]{2,1,0:T(8,128)S(1)}, u32[]{:S(2)}, u32[]{:S(2)}) async-start(f32[32,24,128]{2,1,0:T(8,128)} %get-tuple-element.9), calls=%async_computation | async-start | bytes 786432 | tf_op jit(solution)/shard_map/all_to_all | solution.py:596
  13.8 0.8 %copy-start.8 = (s32[64,128]{1,0:T(8,128)S(1)}, s32[64,128]{1,0:T(8,128)}, u32[]{:S(2)}) copy-start(s32[64,128]{1,0:T(8,128)} %get-tuple-element.10.slot) | copy-start | bytes 98308
  14.6 12.4 %copy-start.14 = (s32[128]{0:T(128)S(1)}, s32[128]{0:T(128)}, u32[]{:S(2)}) copy-start(s32[128]{0:T(128)} %pair_node.1) | copy-start | bytes 1540
  14.6 12.4 %copy-start.15 = (s32[128]{0:T(128)S(1)}, s32[128]{0:T(128)}, u32[]{:S(2)}) copy-start(s32[128]{0:T(128)} %pair_face.1) | copy-start | bytes 1540
  15.0 4.1 %collective-permute-start = (f32[72,128]{1,0:T(8,128)S(1)}, f32[72,128]{1,0:T(8,128)S(1)}, u32[]{:S(2)}, u32[]{:S(2)}) collective-permute-start(f32[72,128]{1,0:T(8,128)S(1)} %get-tuple-element.12), channel_id=1, source_target_pairs={{0,1},{1,2},{2,3},{3,4},{4,5},{5,6},{6,7},{7,8},{8,9},{9,10},{10,1... | collective-permute-start | bytes 110600 | tf_op jit(solution)/shard_map/ppermute | solution.py:617
  17.1 4.2 %collective-permute-start.1 = (f32[72,128]{1,0:T(8,128)S(1)}, f32[72,128]{1,0:T(8,128)S(1)}, u32[]{:S(2)}, u32[]{:S(2)}) collective-permute-start(f32[72,128]{1,0:T(8,128)S(1)} %get-tuple-element.13), channel_id=1, source_target_pairs={{1,0},{2,1},{3,2},{4,3},{5,4},{6,5},{7,6},{8,7},{9,8},{10,9},{11,1... | collective-permute-start | bytes 110600 | tf_op jit(solution)/shard_map/ppermute | solution.py:618
  31.5 15.3 %all-to-all-start.1 = ((f32[32,12,128]{2,1,0:T(8,128)}), f32[32,12,128]{2,1,0:T(8,128)S(1)}, u32[]{:S(2)}, u32[]{:S(2)}) async-start(f32[32,12,128]{2,1,0:T(8,128)} %shard_map.179.returned), calls=%async_computation.1 | async-start | bytes 524288 | tf_op jit(solution)/shard_map/all_to_all | solution.py:639
  36.3 10.6 %copy-start.9 = (s32[64,128]{1,0:T(8,128)S(1)}, s32[64,128]{1,0:T(8,128)}, u32[]{:S(2)}) copy-start(s32[64,128]{1,0:T(8,128)} %get-tuple-element.10.slot) | copy-start | bytes 98308
  36.3 10.6 %copy-start.13 = (f32[8192]{0:T(1024)S(1)}, f32[8192]{0:T(1024)}, u32[]{:S(2)}) copy-start(f32[8192]{0:T(1024)} %param.19) | copy-start | bytes 98308

commit v5 on v4

--- a/solution.py
+++ b/solution.py
@@ -127,8 +127,8 @@
     lane = iota((8, LANES), 1)
 
     def place_runs(i, carry):
-        for n in range(4):
-            device = i * 4 + n
+        for n in range(8):
+            device = i * 8 + n
             start, amount = bounds_scalar[0, device], bounds_scalar[1, device]
             for t in range(tiles):
                 at = start + t * LANES
@@ -140,7 +140,7 @@
                 out[device, pl.ds(t, 6, stride=tiles), :] = jnp.where(lane < amount - t * LANES, turned, 0.0)[0:6]
         return carry
 
-    lax.fori_loop(0, devices // 4, place_runs, 0)
+    lax.fori_loop(0, devices // 8, place_runs, 0)
 
 
 FACE_ROWS = 16
@@ -488,7 +488,7 @@
         return sums
 
     count = pair_count[0]
-    group = math.gcd(32, pair_node.shape[0])
+    group = math.gcd(64, pair_node.shape[0])
 
     def step(i, carry):
         ids = [i * group + n for n in range(group)]

time: 49.6 us -> 49.3 us (level)
  starting transfers between devices: 15.5 us -> 13.5 us
  Pallas kernels: 20.1 us -> 21.6 us
    all_to_all x1, starting transfers between devices: 4.72 us -> 2.71 us  [body(): lax.all_to_all(returned, axes, split_axis=0, concat_axis=0, tiled=True)]
    pallas_call x6, Pallas kernels: 20.1 us -> 21.6 us  [call(): pl.pallas_call(kernel, out_shape=outs, in_specs=[scalar if n < smem else...]
where the time goes in v5:
time: 49.3 us; the launch traced here: 49 us
  Pallas kernels  21.6 us (44%)
  starting transfers between devices  13.5 us (27%)
  waiting for transfers between devices  11.5 us (23%)
  between operations  1.55 us (3%)
  local copies, waits for them, and re-layouts  0.82 us (2%)
    pallas_call x6, Pallas kernels, call(): pl.pallas_call(kernel, out_shape=outs, in_specs=[scalar if n < smem else...  21.6 us
    all_to_all x1, starting transfers between devices, body(): lax.all_to_all(outgoing, axes, split_axis=0, concat_axis=0, tiled=True)  7.33 us
    all_to_all x1, waiting for transfers between devices, body(): lax.all_to_all(outgoing, axes, split_axis=0, concat_axis=0, tiled=True)  4.94 us
    all_to_all x1, waiting for transfers between devices, body(): lax.all_to_all(returned, axes, split_axis=0, concat_axis=0, tiled=True)  4.23 us
    all_to_all x1, starting transfers between devices, body(): lax.all_to_all(returned, axes, split_axis=0, concat_axis=0, tiled=True)  2.71 us
    ppermute x1, waiting for transfers between devices, body(): after = lax.ppermute(send_down, axes, down)  2.29 us
    ppermute x1, starting transfers between devices, body(): before = lax.ppermute(send_up, axes, up)  2.16 us
    ppermute x1, starting transfers between devices, body(): after = lax.ppermute(send_down, axes, down)  1.29 us
  transfers between devices with their start and end apart: 4, of which 3 were waited for; matrix products, arithmetic and copies ran while one was open for 0% of the time, Pallas kernels for 15%

profile of v5, /device:TPU:0, one launch (start us, length us, event | category | flops | bytes accessed | tf_op | source)
XLA Modules:
  0.0 49.0 jit_solution(17001507928044126319)
XLA Ops:
  0.6 0.0 copy-start
  0.6 0.0 copy-start.1
  0.7 0.0 copy-start.2
  0.7 0.0 copy-start.3
  0.7 5.4 %shard_map.176 = (f32[32,24,128]{2,1,0:T(8,128)}, s32[64,128]{1,0:T(8,128)}) custom-call(s32[64,128]{1,0:T(8,128)} %bitcast.16, f32[3,8192]{1,0:T(4,128)} %position_away.1, f32[5,8192]{1,0:T(8,128)} %velocity.5), custom_call_target="tpu_custom_call" | custom-call | flops 1000000000 | bytes 10000000 | tf_op jit(solution)/shard_map/pallas_call | solution.py:552
  6.1 7.3 %all-to-all-start = ((f32[32,24,128]{2,1,0:T(8,128)}), f32[32,24,128]{2,1,0:T(8,128)S(1)}, u32[]{:S(2)}, u32[]{:S(2)}) async-start(f32[32,24,128]{2,1,0:T(8,128)} %get-tuple-element.9), calls=%async_computation | async-start | bytes 786432 | tf_op jit(solution)/shard_map/all_to_all | solution.py:596
  13.5 0.0 copy-done
  13.5 0.0 copy-done.1
  13.5 0.0 copy-done.2
  13.5 0.0 copy-done.3
  13.5 0.0 copy-done.4
  13.5 0.0 copy-done.5
  13.5 0.0 copy-done.6
  13.5 0.0 copy-done.7
  13.5 0.0 copy-done.10
  13.5 0.0 copy-done.11
  13.6 0.0 copy-done.12
  13.6 0.0 copy-start.8
  13.6 0.7 %copy-done.8 = s32[64,128]{1,0:T(8,128)S(1)} copy-done((s32[64,128]{1,0:T(8,128)S(1)}, s32[64,128]{1,0:T(8,128)}, u32[]{:S(2)}) %copy-start.8) | copy-done | bytes 32792
  14.3 0.4 shard_map.177
  14.7 2.2 %collective-permute-start = (f32[72,128]{1,0:T(8,128)S(1)}, f32[72,128]{1,0:T(8,128)S(1)}, u32[]{:S(2)}, u32[]{:S(2)}) collective-permute-start(f32[72,128]{1,0:T(8,128)S(1)} %get-tuple-element.12), channel_id=1, source_target_pairs={{0,1},{1,2},{2,3},{3,4},{4,5},{5,6},{6,7},{7,8},{8,9},{9,10},{10,1... | collective-permute-start | bytes 110600 | tf_op jit(solution)/shard_map/ppermute | solution.py:617
  16.9 1.3 %collective-permute-start.1 = (f32[72,128]{1,0:T(8,128)S(1)}, f32[72,128]{1,0:T(8,128)S(1)}, u32[]{:S(2)}, u32[]{:S(2)}) collective-permute-start(f32[72,128]{1,0:T(8,128)S(1)} %get-tuple-element.13), channel_id=1, source_target_pairs={{1,0},{2,1},{3,2},{4,3},{5,4},{6,5},{7,6},{8,7},{9,8},{10,9},{11,1... | collective-permute-start | bytes 110600 | tf_op jit(solution)/shard_map/ppermute | solution.py:618
  18.8 0.0 collective-permute-done.before
  18.9 2.3 %collective-permute-done.1.after = f32[72,128]{1,0:T(8,128)S(1)} collective-permute-done((f32[72,128]{1,0:T(8,128)S(1)}, f32[72,128]{1,0:T(8,128)S(1)}, u32[]{:S(2)}, u32[]{:S(2)}) %collective-permute-start.1) | collective-permute-done | bytes 36896 | tf_op jit(solution)/shard_map/ppermute | solution.py:618
  21.1 0.6 %shard_map.178.face = bf16[2560,128]{1,0:T(8,128)(2,1)S(1)} custom-call(f32[128,128]{1,0:T(8,128)S(1)} %get-tuple-element.11.own, f32[72,128]{1,0:T(8,128)S(1)} %collective-permute-done.before, f32[72,128]{1,0:T(8,128)S(1)} %collective-permute-done.1.after), custom_call_target="tpu_custom_call" | custom-call | flops 100000000 | bytes 1000000 | tf_op jit(solution)/shard_map/pallas_call | solution.py:552
  21.8 4.9 %all-to-all-done.nodes = f32[32,24,128]{2,1,0:T(8,128)S(1)} async-done(((f32[32,24,128]{2,1,0:T(8,128)}), f32[32,24,128]{2,1,0:T(8,128)S(1)}, u32[]{:S(2)}, u32[]{:S(2)}) %all-to-all-start) | async-done | bytes 393248 | tf_op jit(solution)/shard_map/all_to_all | solution.py:596
  26.7 6.3 %shard_map.179.returned = f32[32,12,128]{2,1,0:T(8,128)} custom-call(s32[128]{0:T(128)S(1)} %copy-done.14, s32[128]{0:T(128)S(1)} %copy-done.15, s32[1]{0:T(128)S(6)} %copy.19.pair_count, f32[32,24,128]{2,1,0:T(8,128)S(1)} %all-to-all-done.nodes, bf16[2560,128]{1,0:T(8,128)(2,1)S(1)} %shard_map.178.face), custom_call_target="tpu_custom_call" | custom-call | flops 1000000000 | bytes 10000000 | tf_op jit(solution)/shard_map/pallas_call | solution.py:552
  33.0 2.7 %all-to-all-start.1 = ((f32[32,12,128]{2,1,0:T(8,128)}), f32[32,12,128]{2,1,0:T(8,128)S(1)}, u32[]{:S(2)}, u32[]{:S(2)}) async-start(f32[32,12,128]{2,1,0:T(8,128)} %shard_map.179.returned), calls=%async_computation.1 | async-start | bytes 524288 | tf_op jit(solution)/shard_map/all_to_all | solution.py:639
  35.8 0.0 copy-start.13
  35.8 6.3 %shard_map.180 = (f32[5,5,8192]{2,1,0:T(8,128)}, f32[512,128]{1,0:T(8,128)S(1)}) custom-call(f32[5,8192]{1,0:T(8,128)S(1)} %copy-done.2, f32[72,128]{1,0:T(8,128)S(1)} %collective-permute-done.before, f32[72,128]{1,0:T(8,128)S(1)} %collective-permute-done.1.after, s32[4,8192]{1,0:T(4,128)S(1)} %copy-done.3, f32[2,4,8192]{2,1,0:T(4,128)S(1)} %copy-done.1, ...), custom_call_target="tpu_custom_call" | custom-call | flops 1000000000 | bytes 10000000 | tf_op jit(solution)/shard_map/pallas_call | solution.py:552
  42.1 4.2 %all-to-all-done.1.back = f32[32,12,128]{2,1,0:T(8,128)S(1)} async-done(((f32[32,12,128]{2,1,0:T(8,128)}), f32[32,12,128]{2,1,0:T(8,128)S(1)}, u32[]{:S(2)}, u32[]{:S(2)}) %all-to-all-start.1) | async-done | bytes 196640 | tf_op jit(solution)/shard_map/all_to_all | solution.py:639
  46.3 2.6 %shard_map.181 = f32[5,8192]{1,0:T(8,128)} custom-call(f32[32,12,128]{2,1,0:T(8,128)S(1)} %all-to-all-done.1.back, s32[64,128]{1,0:T(8,128)S(1)} %copy-done.9, f32[512,128]{1,0:T(8,128)S(1)} %get-tuple-element.14.own, f32[5,8192]{1,0:T(8,128)S(1)} %copy-done.2, f32[64,128]{1,0:T(8,128)S(1)} %bitcast.15), custom_call_target="tpu_custom_call" | custom-call | flops 1000000000 | bytes 10000000 | tf_op jit(solution)/shard_map/pallas_call | solution.py:552
  (14 shorter events, 0.0 us)
Async XLA Ops:
  0.6 12.8 %copy-start = (f32[5,5,8192]{2,1,0:T(8,128)S(1)}, f32[5,5,8192]{2,1,0:T(8,128)}, u32[]{:S(2)}) copy-start(f32[5,5,8192]{2,1,0:T(8,128)} %stress.3) | copy-start | bytes 2457604
  0.6 12.8 %copy-start.1 = (f32[2,4,8192]{2,1,0:T(4,128)S(1)}, f32[2,4,8192]{2,1,0:T(4,128)}, u32[]{:S(2)}) copy-start(f32[2,4,8192]{2,1,0:T(4,128)} %grads.3) | copy-start | bytes 786436
  0.7 12.8 %copy-start.2 = (f32[5,8192]{1,0:T(8,128)S(1)}, f32[5,8192]{1,0:T(8,128)}, u32[]{:S(2)}) copy-start(f32[5,8192]{1,0:T(8,128)} %velocity.5) | copy-start | bytes 491524
  0.7 12.8 %copy-start.3 = (s32[4,8192]{1,0:T(4,128)S(1)}, s32[4,8192]{1,0:T(4,128)}, u32[]{:S(2)}) copy-start(s32[4,8192]{1,0:T(4,128)} %connectivity.3) | copy-start | bytes 393220
  0.7 12.8 %copy-start.4 = (f32[3,2048]{1,0:T(4,128)S(1)}, f32[3,2048]{1,0:T(4,128)}, u32[]{:S(2)}) copy-start(f32[3,2048]{1,0:T(4,128)} %center.1) | copy-start | bytes 73732
  0.7 12.8 %copy-start.5 = (f32[8192]{0:T(1024)S(1)}, f32[8192]{0:T(1024)}, u32[]{:S(2)}) copy-start(f32[8192]{0:T(1024)} %param.22) | copy-start | bytes 98308
  0.7 12.8 %copy-start.6 = (f32[8192]{0:T(1024)S(1)}, f32[8192]{0:T(1024)}, u32[]{:S(2)}) copy-start(f32[8192]{0:T(1024)} %param.23) | copy-start | bytes 98308
  0.7 12.8 %copy-start.7 = (f32[8192]{0:T(1024)S(1)}, f32[8192]{0:T(1024)}, u32[]{:S(2)}) copy-start(f32[8192]{0:T(1024)} %param.24) | copy-start | bytes 98308
  0.7 12.8 %copy-start.10 = (f32[2,2048]{1,0:T(2,128)S(1)}, f32[2,2048]{1,0:T(2,128)}, u32[]{:S(2)}) copy-start(f32[2,2048]{1,0:T(2,128)} %angle.1) | copy-start | bytes 49156
  0.7 12.8 %copy-start.11 = (f32[2048]{0:T(1024)S(1)}, f32[2048]{0:T(1024)}, u32[]{:S(2)}) copy-start(f32[2048]{0:T(1024)} %param.29) | copy-start | bytes 24580
  0.7 12.8 %copy-start.12 = (s32[512]{0:T(512)S(1)}, s32[512]{0:T(512)}, u32[]{:S(2)}) copy-start(s32[512]{0:T(512)} %param.30) | copy-start | bytes 6148
  6.1 20.6 %all-to-all-start = ((f32[32,24,128]{2,1,0:T(8,128)}), f32[32,24,128]{2,1,0:T(8,128)S(1)}, u32[]{:S(2)}, u32[]{:S(2)}) async-start(f32[32,24,128]{2,1,0:T(8,128)} %get-tuple-element.9), calls=%async_computation | async-start | bytes 786432 | tf_op jit(solution)/shard_map/all_to_all | solution.py:596
  13.6 0.8 %copy-start.8 = (s32[64,128]{1,0:T(8,128)S(1)}, s32[64,128]{1,0:T(8,128)}, u32[]{:S(2)}) copy-start(s32[64,128]{1,0:T(8,128)} %get-tuple-element.10.slot) | copy-start | bytes 98308
  14.3 12.4 %copy-start.14 = (s32[128]{0:T(128)S(1)}, s32[128]{0:T(128)}, u32[]{:S(2)}) copy-start(s32[128]{0:T(128)} %pair_node.1) | copy-start | bytes 1540
  14.3 12.4 %copy-start.15 = (s32[128]{0:T(128)S(1)}, s32[128]{0:T(128)}, u32[]{:S(2)}) copy-start(s32[128]{0:T(128)} %pair_face.1) | copy-start | bytes 1540
  14.7 4.1 %collective-permute-start = (f32[72,128]{1,0:T(8,128)S(1)}, f32[72,128]{1,0:T(8,128)S(1)}, u32[]{:S(2)}, u32[]{:S(2)}) collective-permute-start(f32[72,128]{1,0:T(8,128)S(1)} %get-tuple-element.12), channel_id=1, source_target_pairs={{0,1},{1,2},{2,3},{3,4},{4,5},{5,6},{6,7},{7,8},{8,9},{9,10},{10,1... | collective-permute-start | bytes 110600 | tf_op jit(solution)/shard_map/ppermute | solution.py:617
  16.9 4.2 %collective-permute-start.1 = (f32[72,128]{1,0:T(8,128)S(1)}, f32[72,128]{1,0:T(8,128)S(1)}, u32[]{:S(2)}, u32[]{:S(2)}) collective-permute-start(f32[72,128]{1,0:T(8,128)S(1)} %get-tuple-element.13), channel_id=1, source_target_pairs={{1,0},{2,1},{3,2},{4,3},{5,4},{6,5},{7,6},{8,7},{9,8},{10,9},{11,1... | collective-permute-start | bytes 110600 | tf_op jit(solution)/shard_map/ppermute | solution.py:618
  33.0 13.3 %all-to-all-start.1 = ((f32[32,12,128]{2,1,0:T(8,128)}), f32[32,12,128]{2,1,0:T(8,128)S(1)}, u32[]{:S(2)}, u32[]{:S(2)}) async-start(f32[32,12,128]{2,1,0:T(8,128)} %shard_map.179.returned), calls=%async_computation.1 | async-start | bytes 524288 | tf_op jit(solution)/shard_map/all_to_all | solution.py:639
  35.7 10.6 %copy-start.9 = (s32[64,128]{1,0:T(8,128)S(1)}, s32[64,128]{1,0:T(8,128)}, u32[]{:S(2)}) copy-start(s32[64,128]{1,0:T(8,128)} %get-tuple-element.10.slot) | copy-start | bytes 98308
  35.8 10.6 %copy-start.13 = (f32[8192]{0:T(1024)S(1)}, f32[8192]{0:T(1024)}, u32[]{:S(2)}) copy-start(f32[8192]{0:T(1024)} %param.19) | copy-start | bytes 98308
